TPU v7x, 256 devices: a whole 4x4x8 slice. The times are simulated.
256 devices in a mesh: row: 32 (over z, y_hi, core), col: 8 (over x, y_lo).
Axes of the slice: x: 4, y: 4 (y_hi: 2, y_lo: 2; y = y_hi * 2 + y_lo), z: 8, core: 2. Of those that a mesh axis runs over, the one named last changes fastest.
Arguments:
- feature_map: bfloat16 [256, 256, 384], P('row', 'col'), may hold values from -6 to 6
- kernel: float32 [7, 7, 384], replicated, may hold values from -0.875 to 0.875
- ln_gain: float32 [384], replicated, may hold values from 0.5 to 1.5
- ln_bias: float32 [384], replicated, may hold values from -3 to 3
- w_in: bfloat16 [384, 1536], P(None, ('row', 'col')), may hold values from -0.3125 to 0.3125
- b_in: float32 [1536], replicated, may hold values from -3 to 3
- w_out: bfloat16 [1536, 384], P(('row', 'col')), may hold values from -0.15625 to 0.15625
- b_out: float32 [384], replicated, may hold values from -3 to 3
- layer_scale: float32 [384], replicated, may hold values from 0.5 to 1.5
- cotangent: bfloat16 [256, 256, 384], P('row', 'col'), may hold values from -6 to 6
Outputs:
- block_out: bfloat16 [256, 256, 384], P('row', 'col')
- grad_input: bfloat16 [256, 256, 384], P('row', 'col')
- grad_w_in: float32 [384, 1536], P(None, ('row', 'col'))
- grad_w_out: float32 [1536, 384], P(('row', 'col'))
- small_grads: float32 [53, 384], replicated
- grad_b_in: float32 [1536], replicated
All inputs are finite; a program needn't handle non-finite values.
Results may differ from a plain program's by a relative error of at most 0.007.
Values may be sent and summed in bfloat16 or wider, within the bound.
No kernel may reach another device: no remote copies, remote signals or barrier semaphores. Data moves between devices by JAX's collectives and lax.ppermute only.
A program may use at most 64 MiB of HBM per device.

v0:
```python
import math

import jax
import jax.numpy as jnp
from jax import lax
from jax.sharding import PartitionSpec as P


def padded_2(x, sides, width):
    for axis, dim in sides:
        peers, length = (lax.axis_size(axis), x.shape[dim])
        up = [(i, (i + 1) % peers) for i in range(peers - 1)]
        down = [(j, i) for i, j in up]
        last = lax.slice_in_dim(x, length - width, length, axis=dim)
        first = lax.slice_in_dim(x, 0, width, axis=dim)
        before = lax.ppermute(last, axis, up)
        after = lax.ppermute(first, axis, down)
        x = jnp.concatenate([before, x, after], axis=dim)
    return x


def gelu_parts(hidden):
    normal_cdf = 0.5 * (1.0 + jax.scipy.special.erf(hidden * (1.0 / math.sqrt(2.0))))
    density = jnp.exp(-0.5 * hidden * hidden) * (1.0 / math.sqrt(2.0 * math.pi))
    return (hidden * normal_cdf, normal_cdf + hidden * density)


def extend(field):
    return padded_2(field, (("row", 0), ("col", 1)), 3)


def on_device(
    feature_map, kernel, ln_gain, ln_bias, w_in, b_in, w_out, b_out, layer_scale, cotangent
):
    row_count, col_count, channels = feature_map.shape
    pixels = row_count * col_count
    padded = extend(feature_map).astype(jnp.float32)
    conv = jnp.zeros((row_count, col_count, channels), jnp.float32)
    for tap_row in range(7):
        for tap_col in range(7):
            conv = (
                conv
                + padded[tap_row : tap_row + row_count, tap_col : tap_col + col_count]
                * kernel[tap_row, tap_col]
            )
    average = jnp.mean(conv, -1, keepdims=True)
    centered = conv - average
    variance = jnp.mean(centered * centered, -1, keepdims=True)
    inv_std = lax.rsqrt(variance + 1e-06)
    unit_scaled = centered * inv_std
    normed = (unit_scaled * ln_gain + ln_bias).astype(jnp.bfloat16).reshape(pixels, channels)
    contract_last = (((1,), (1,)), ((), ()))
    contract_first = (((0,), (0,)), ((), ()))
    w_in_full = lax.all_gather(w_in, ("row", "col"), axis=1, tiled=True)
    w_out_full = lax.all_gather(w_out, ("row", "col"), axis=0, tiled=True)
    hidden = jnp.dot(normed, w_in_full, preferred_element_type=jnp.float32) + b_in
    act_value, slope = gelu_parts(hidden)
    activated = act_value.astype(jnp.bfloat16)
    mixed = jnp.dot(activated, w_out_full, preferred_element_type=jnp.float32) + b_out
    source = feature_map.astype(jnp.float32).reshape(pixels, channels)
    block_out = (
        (source + layer_scale * mixed).astype(jnp.bfloat16).reshape(row_count, col_count, channels)
    )
    grad_flow = cotangent.astype(jnp.float32).reshape(pixels, channels)
    grad_mixed = grad_flow * layer_scale
    mixed_low = grad_mixed.astype(jnp.bfloat16)
    grad_act = lax.dot_general(
        mixed_low, w_out_full, contract_last, preferred_element_type=jnp.float32
    )
    grad_hidden = (grad_act * slope).astype(jnp.bfloat16)
    grad_w_out = lax.psum_scatter(
        lax.dot_general(activated, mixed_low, contract_first, preferred_element_type=jnp.float32),
        ("row", "col"),
        scatter_dimension=0,
        tiled=True,
    )
    win_term = lax.dot_general(
        normed, grad_hidden, contract_first, preferred_element_type=jnp.float32
    )
    grad_w_in = lax.psum_scatter(win_term, ("row", "col"), scatter_dimension=1, tiled=True)
    grad_normed = lax.dot_general(
        grad_hidden, w_in_full, contract_last, preferred_element_type=jnp.float32
    )
    grad_normed = grad_normed.reshape(row_count, col_count, channels)
    grad_gain = jnp.sum(grad_normed * unit_scaled, (0, 1))
    grad_lnb = jnp.sum(grad_normed, (0, 1))
    scaled_grad = grad_normed * ln_gain
    grad_conv = inv_std * (
        scaled_grad
        - jnp.mean(scaled_grad, -1, keepdims=True)
        - unit_scaled * jnp.mean(scaled_grad * unit_scaled, -1, keepdims=True)
    )
    tap_terms = []
    for tap_row in range(7):
        for tap_col in range(7):
            tap_terms.append(
                jnp.sum(
                    padded[tap_row : tap_row + row_count, tap_col : tap_col + col_count]
                    * grad_conv,
                    (0, 1),
                )
            )
    grad_pad = extend(grad_conv.astype(jnp.bfloat16)).astype(jnp.float32)
    back_conv = jnp.zeros((row_count, col_count, channels), jnp.float32)
    for tap_row in range(7):
        for tap_col in range(7):
            back_conv = (
                back_conv
                + grad_pad[
                    6 - tap_row : 6 - tap_row + row_count, 6 - tap_col : 6 - tap_col + col_count
                ]
                * kernel[tap_row, tap_col]
            )
    grad_input = (cotangent.astype(jnp.float32) + back_conv).astype(jnp.bfloat16)
    small_local = jnp.concatenate(
        [
            jnp.stack(tap_terms, 0),
            grad_gain[None],
            grad_lnb[None],
            jnp.sum(grad_mixed, 0)[None],
            jnp.sum(grad_flow * mixed, 0)[None],
        ],
        0,
    )
    bias_local = jnp.sum(grad_hidden.astype(jnp.float32), 0)
    small_grads, grad_b_in = lax.psum((small_local, bias_local), ("row", "col"))
    return (block_out, grad_input, grad_w_in, grad_w_out, small_grads, grad_b_in)


def solution(mesh):
    placed = (
        P("row", "col", None),
        P(),
        P(),
        P(),
        P(None, ("row", "col")),
        P(),
        P(("row", "col"), None),
        P(),
        P(),
        P("row", "col", None),
    )
    return jax.shard_map(
        on_device,
        mesh=mesh,
        in_specs=placed,
        out_specs=(
            P("row", "col", None),
            P("row", "col", None),
            P(None, ("row", "col")),
            P(("row", "col"), None),
            P(),
            P(),
        ),
        check_vma=False,
    )
```

profile of v0, /device:TPU:6, one launch (start us, length us, event | category | flops | bytes accessed | tf_op | source)
XLA Modules:
  0.0 1692.7 jit_solution(1590831697639832717)
XLA Ops:
  7.2 0.0 all-gather.5.cloned.1.call-start
  7.2 0.7 all-gather.5.cloned.1.call-update
  7.9 0.0 all-gather.7.cloned.1.call-start
  7.9 0.9 fusion.63
  8.9 1.7 collective-permute-start
  10.6 1.3 collective-permute-start.1
  11.9 0.0 all-gather.7.cloned.1.call-update
  12.0 0.0 all-reduce.5.cloned.1.call-start
  12.0 1.1 slice_reduce_fusion.47
  13.1 1.0 fusion.56
  14.1 1.2 slice_reduce_fusion.48
  15.4 0.0 copy-start.5
  15.4 0.0 collective-permute-done
  15.5 1.0 constant_dynamic-update-slice_fusion.1
  16.4 0.4 collective-permute-done.1
  16.8 3.4 collective-permute-start.3
  20.3 2.4 collective-permute-start.2
  22.7 1.0 slice_reduce_fusion.46
  23.7 0.0 copy-start.35
  23.8 0.0 copy-start.37
  23.8 0.6 broadcast_in_dim.10
  24.3 2.8 collective-permute-done.2
  27.1 0.1 maximum_convert_fusion
  27.2 0.0 copy-start.39
  27.2 0.0 copy-start.42
  27.2 3.2 fusion.60
  30.6 0.2 multiply_reduce_fusion.52
  30.8 0.1 add_convert_fusion
  30.9 663.2 %all-gather.5.cloned.1.call-done = bf16[256,6,384]{2,1,0:T(8,128)(2,1)} async-done(((bf16[1,6,384]{2,1,0:T(8,128)(2,1)}), bf16[256,6,384]{2,1,0:T(8,128)(2,1)}) %all-gather.5.cloned.1.call-update) | async-done | bytes 1179664 | tf_op jit(solution)/shard_map/all_gather | solution.py:54
  694.2 2.3 reshape.74
  696.5 2.5 multiply_convert_fusion
  699.0 684.4 %all-gather.7.cloned.1.call-done = bf16[256,6,384]{2,1,0:T(8,128)(2,1)} async-done(((bf16[1,6,384]{2,1,0:T(8,128)(2,1)}), bf16[256,6,384]{2,1,0:T(8,128)(2,1)}) %all-gather.7.cloned.1.call-update) | async-done | bytes 1179664 | tf_op jit(solution)/shard_map/all_gather | solution.py:55
  1383.4 3.3 reshape.76
  1386.6 3.5 fusion.58
  1390.1 0.9 convert_reduce_fusion
  1391.1 0.7 fusion.59
  1391.8 2.0 fusion.64
  1393.8 2.1 fusion.65
  1395.9 0.2 multiply_reduce_fusion
  1396.1 0.1 div.17
  1396.2 0.9 multiply_reduce_fusion.1
  1397.1 0.7 multiply_reduce_fusion.19
  1397.9 0.0 copy-start.41
  1397.9 0.6 multiply_reduce_fusion.37
  1399.0 4.4 concatenate.19
  1403.4 0.0 all-reduce.5.cloned.1.call-update
  1403.4 0.0 copy-start.4
  1403.4 0.0 copy-start.6
  1403.6 0.0 copy-start.36
  1403.6 0.0 copy-start.38
  1403.6 1.3 collective-permute-start.5
  1404.9 3.0 collective-permute-start.4
  1408.0 0.0 collective-permute-done.5
  1408.0 0.9 collective-permute-done.4
  1408.9 1.9 collective-permute-start.7
  1410.8 3.9 collective-permute-start.6
  1414.8 89.9 %psum.15 = f32[1536]{0:T(1024)} all-reduce(f32[1536]{0:T(1024)S(1)} %get-tuple-element.129), channel_id=1, replica_groups=mesh['row'=32,'col'=8] {'row','col'}, use_global_device_ids=true, to_apply=%region_61.0 | all-reduce | flops 1536 | bytes 12288 | tf_op jit(solution)/shard_map/psum | solution.py:126
  1504.6 0.0 collective-permute-done.7
  1504.6 0.1 maximum_convert_fusion.1
  1505.0 3.5 fusion.7
  1508.5 173.5 %all-reduce.5.cloned.1.call-done = (f32[384,1536]{0,1:T(8,128)}, f32[1536,384]{1,0:T(8,128)}, f32[53,384]{1,0:T(8,128)}) async-done(((f32[384,1536]{0,1:T(8,128)}, f32[1536,384]{1,0:T(8,128)}, f32[53,384]{1,0:T(8,128)}), (f32[384,1536]{0,1:T(8,128)}, f32[1536,384]{1,0:T(8,128)}, f32[53,384]{1,0:T(8,128)})) %all-reduce.5.cloned.1.call-update) | async-done | bytes 4800016
  1681.9 1.3 constant_dynamic-slice_fusion.1
  1683.3 1.3 constant_dynamic-slice_fusion
  1684.6 1.5 copy.21
  (141 shorter events, 0.5 us)
Async XLA Ops:
  7.2 687.0 %all-gather.5.cloned.1.call-start = ((), (), s32[]{:S(2)}) async-start(), calls=%async_computation | async-start | bytes 1579008 | tf_op jit(solution)/shard_map/all_gather | solution.py:54
  7.9 1375.5 %all-gather.7.cloned.1.call-start = ((), (), s32[]{:S(2)}) async-start(), calls=%async_computation.1 | async-start | bytes 1579008 | tf_op jit(solution)/shard_map/all_gather | solution.py:55
  8.9 6.5 collective-permute-start
  10.6 6.1 collective-permute-start.1
  12.0 1670.0 %all-reduce.5.cloned.1.call-start = ((), (), s32[]{:S(2)}) async-start(), calls=%async_computation.2 | async-start | bytes 9609216
  15.4 15.0 copy-start.5
  15.4 15.0 copy-start.7
  15.4 15.0 copy-start.9
  15.4 15.0 copy-start.11
  15.4 15.0 copy-start.13
  15.4 15.0 copy-start.15
  16.8 7.5 collective-permute-start.3
  20.3 6.8 collective-permute-start.2
  23.7 6.8 copy-start.17
  23.7 6.8 copy-start.19
  23.7 6.8 copy-start.21
  23.7 6.8 copy-start.23
  23.7 6.8 copy-start.25
  23.7 6.8 copy-start.27
  23.7 6.8 copy-start.29
  23.7 6.8 copy-start.31
  23.7 6.8 copy-start.33
  23.7 6.8 copy-start.35
  23.8 6.8 copy-start.37
  27.2 3.5 copy-start.39
  27.2 3.5 copy-start.42
  699.0 691.1 %copy-start = (bf16[256,1536]{1,0:T(8,128)(2,1)}, bf16[256,1536]{1,0:T(8,128)(2,1)S(1)}, u32[]{:S(2)}) copy-start(bf16[256,1536]{1,0:T(8,128)(2,1)S(1)} %get-tuple-element.126) | copy-start | bytes 2359300
  1386.6 3.5 copy-start.2
  1386.6 3.5 copy-start.3
  1390.1 0.9 copy-start.40
  1391.7 2.0 copy-start.1
  1397.9 1.1 copy-start.43
  1397.9 1.2 copy-start.41
  1403.4 101.4 %copy-start.4 = (bf16[8,32,384]{2,1,0:T(8,128)(2,1)S(1)}, bf16[8,32,384]{2,1,0:T(8,128)(2,1)}, u32[]{:S(2)}) copy-start(bf16[8,32,384]{2,1,0:T(8,128)(2,1)} %param.19) | copy-start | bytes 589828
  1403.4 101.4 %copy-start.6 = (f32[384]{0:T(512)S(1)}, f32[384]{0:T(512)}, u32[]{:S(2)}) copy-start(f32[384]{0:T(512)} %copy-done.5) | copy-start | bytes 4612
  1403.4 101.4 %copy-start.8 = (f32[384]{0:T(512)S(1)}, f32[384]{0:T(512)}, u32[]{:S(2)}) copy-start(f32[384]{0:T(512)} %copy-done.7) | copy-start | bytes 4612
  1403.4 101.4 %copy-start.10 = (f32[384]{0:T(512)S(1)}, f32[384]{0:T(512)}, u32[]{:S(2)}) copy-start(f32[384]{0:T(512)} %copy-done.9) | copy-start | bytes 4612
  1403.5 101.4 %copy-start.12 = (f32[384]{0:T(512)S(1)}, f32[384]{0:T(512)}, u32[]{:S(2)}) copy-start(f32[384]{0:T(512)} %copy-done.11) | copy-start | bytes 4612
  1403.5 101.4 %copy-start.14 = (f32[384]{0:T(512)S(1)}, f32[384]{0:T(512)}, u32[]{:S(2)}) copy-start(f32[384]{0:T(512)} %copy-done.13) | copy-start | bytes 4612
  1403.5 101.4 %copy-start.16 = (f32[384]{0:T(512)S(1)}, f32[384]{0:T(512)}, u32[]{:S(2)}) copy-start(f32[384]{0:T(512)} %copy-done.15) | copy-start | bytes 4612
  1403.5 101.4 %copy-start.18 = (f32[384]{0:T(512)S(1)}, f32[384]{0:T(512)}, u32[]{:S(2)}) copy-start(f32[384]{0:T(512)} %copy-done.17) | copy-start | bytes 4612
  1403.5 101.4 %copy-start.20 = (f32[384]{0:T(512)S(1)}, f32[384]{0:T(512)}, u32[]{:S(2)}) copy-start(f32[384]{0:T(512)} %copy-done.19) | copy-start | bytes 4612
  1403.5 101.4 %copy-start.22 = (f32[384]{0:T(512)S(1)}, f32[384]{0:T(512)}, u32[]{:S(2)}) copy-start(f32[384]{0:T(512)} %copy-done.21) | copy-start | bytes 4612
  1403.5 101.4 %copy-start.24 = (f32[384]{0:T(512)S(1)}, f32[384]{0:T(512)}, u32[]{:S(2)}) copy-start(f32[384]{0:T(512)} %copy-done.23) | copy-start | bytes 4612
  1403.5 101.4 %copy-start.26 = (f32[384]{0:T(512)S(1)}, f32[384]{0:T(512)}, u32[]{:S(2)}) copy-start(f32[384]{0:T(512)} %copy-done.25) | copy-start | bytes 4612
  1403.5 101.4 %copy-start.28 = (f32[384]{0:T(512)S(1)}, f32[384]{0:T(512)}, u32[]{:S(2)}) copy-start(f32[384]{0:T(512)} %copy-done.27) | copy-start | bytes 4612
  1403.5 101.4 %copy-start.30 = (f32[384]{0:T(512)S(1)}, f32[384]{0:T(512)}, u32[]{:S(2)}) copy-start(f32[384]{0:T(512)} %copy-done.29) | copy-start | bytes 4612
  1403.6 101.4 %copy-start.32 = (f32[384]{0:T(512)S(1)}, f32[384]{0:T(512)}, u32[]{:S(2)}) copy-start(f32[384]{0:T(512)} %copy-done.31) | copy-start | bytes 4612
  1403.6 101.4 %copy-start.34 = (f32[384]{0:T(512)S(1)}, f32[384]{0:T(512)}, u32[]{:S(2)}) copy-start(f32[384]{0:T(512)} %copy-done.33) | copy-start | bytes 4612
  1403.6 101.4 %copy-start.36 = (f32[384]{0:T(512)S(1)}, f32[384]{0:T(512)}, u32[]{:S(2)}) copy-start(f32[384]{0:T(512)} %copy-done.35) | copy-start | bytes 4612
  1403.6 101.4 %copy-start.38 = (f32[384]{0:T(512)S(1)}, f32[384]{0:T(512)}, u32[]{:S(2)}) copy-start(f32[384]{0:T(512)} %copy-done.37) | copy-start | bytes 4612
  1403.6 4.3 collective-permute-start.5
  1404.9 3.9 collective-permute-start.4
  1408.9 95.7 %collective-permute-start.7 = (bf16[14,3,384]{2,1,0:T(4,128)(2,1)S(1)}, bf16[14,3,384]{2,1,0:T(4,128)(2,1)S(1)}, u32[]{:S(2)}, u32[]{:S(2)}) collective-permute-start(bf16[14,3,384]{2,1,0:T(4,128)(2,1)S(1)} %get-tuple-element.118), channel_id=1, source_target_pairs={{1,0},{2,1},{3,2},{4,3},{5,4},{6,5},{7,6},{9,8},{10,9},{11,10},{12... | collective-permute-start | bytes 96776 | tf_op jit(solution)/shard_map/ppermute | solution.py:17
  1410.8 93.8 %collective-permute-start.6 = (bf16[14,3,384]{2,1,0:T(4,128)(2,1)S(1)}, bf16[14,3,384]{2,1,0:T(4,128)(2,1)S(1)}, u32[]{:S(2)}, u32[]{:S(2)}) collective-permute-start(bf16[14,3,384]{2,1,0:T(4,128)(2,1)S(1)} %get-tuple-element.117), channel_id=1, source_target_pairs={{0,1},{1,2},{2,3},{3,4},{4,5},{5,6},{6,7},{8,9},{9,10},{10,11},{11... | collective-permute-start | bytes 96776 | tf_op jit(solution)/shard_map/ppermute | solution.py:16
Sparse Core Ops, SparseCore 0:
  9.9 684.2 all-gather.4
  696.0 687.2 all-gather.6
  1403.5 278.3 all-reduce.4
where the time goes:
time: 1690 us
  waiting for transfers between devices  1530 us (91%)
  blocking collectives  89.9 us (5%)
  local copies, waits for them, and re-layouts  20.5 us (1%)
  starting transfers between devices  19.2 us (1%)
    all_gather x1, waiting for transfers between devices, on_device(): w_out_full = lax.all_gather(w_out, ('row', 'col'), axis=0, tiled=True)  684 us
    all_gather x1, waiting for transfers between devices, on_device(): w_in_full = lax.all_gather(w_in, ('row', 'col'), axis=1, tiled=True)  663 us
    unnamed x4, waiting for transfers between devices  174 us
    psum x1, blocking collectives, on_device(): small_grads, grad_b_in = lax.psum((small_local, bias_local), ('row', 'col'))  89.9 us
  transfers between devices with their start and end apart: 11, of which 6 were waited for; matrix products, arithmetic and copies ran while one was open for 1% of the time, Pallas kernels for 0%

commit v1 on v0

v1 whole, which is shorter than its diff:
```python
import math

import jax
import jax.numpy as jnp
from jax import lax
from jax.sharding import Mesh
from jax.sharding import PartitionSpec as P

ROW = ("z", "yh", "c")
COL = ("x", "yl")
Y = ("yh", "yl")
BF = jnp.bfloat16
F4 = jnp.float32


def swap(x, axis, flip):
    count = lax.axis_size(axis)
    return lax.ppermute(x, axis, [(i, i ^ flip) for i in range(count)])


def padded_2(x, sides, width):
    for axis, dim in sides:
        peers, length = (lax.axis_size(axis), x.shape[dim])
        up = [(i, (i + 1) % peers) for i in range(peers - 1)]
        down = [(j, i) for i, j in up]
        last = lax.slice_in_dim(x, length - width, length, axis=dim)
        first = lax.slice_in_dim(x, 0, width, axis=dim)
        before = lax.ppermute(last, axis, up)
        after = lax.ppermute(first, axis, down)
        x = jnp.concatenate([before, x, after], axis=dim)
    return x


def gelu_parts(hidden):
    normal_cdf = 0.5 * (1.0 + jax.scipy.special.erf(hidden * (1.0 / math.sqrt(2.0))))
    density = jnp.exp(-0.5 * hidden * hidden) * (1.0 / math.sqrt(2.0 * math.pi))
    return (hidden * normal_cdf, normal_cdf + hidden * density)


def extend(field):
    return padded_2(field, ((ROW, 0), (COL, 1)), 3)


def pair_gather(x, axis, bit):
    mine = (lax.axis_index(axis) & bit) != 0
    other = swap(x, axis, bit)
    return jnp.concatenate([jnp.where(mine, other, x), jnp.where(mine, x, other)], axis=1)


def quad_gather(x, axis):
    me = lax.axis_index(axis)
    rows = x.shape[1]
    others = [swap(x, axis, flip) for flip in (1, 2, 3)]
    full = jnp.zeros((x.shape[0], 4 * rows, x.shape[2]), x.dtype)
    for flip, piece in zip((0, 1, 2, 3), [x] + others):
        full = lax.dynamic_update_slice_in_dim(full, piece, (me ^ flip) * rows, axis=1)
    return full


def piece_of(x, index, rows):
    return lax.dynamic_slice_in_dim(x, index * rows, rows, axis=1)


def fan_reduce(x, axis, flips, size, dtype):
    rows = x.shape[1] // size
    where = lax.axis_index(axis)
    unit = flips[0]
    me = (where // unit) % size
    total = piece_of(x, me, rows)
    got = [swap(piece_of(x, me ^ (flip // unit), rows).astype(dtype), axis, flip) for flip in flips]
    for g in got:
        total = total + g.astype(F4)
    return total


def on_device(
    feature_map, kernel, ln_gain, ln_bias, w_in, b_in, w_out, b_out, layer_scale, cotangent
):
    row_count, col_count, channels = feature_map.shape
    pixels = row_count * col_count
    hidden_count = b_in.shape[0]
    contract_last = (((1,), (1,)), ((), ()))
    contract_first = (((0,), (0,)), ((), ()))

    weights = jnp.stack([w_in.T, w_out], 0)
    for bit in (4, 2, 1):
        weights = pair_gather(weights, "z", bit)
    weights = quad_gather(weights, Y)
    weights = quad_gather(weights, "x")
    weights = pair_gather(weights, "c", 1)
    w_in_t, w_out_full = weights[0], weights[1]
    units = hidden_count // 256
    b_mine = (
        b_in.reshape(2, 2, 2, 2, 2, 4, 2, units).transpose(4, 5, 3, 6, 2, 1, 0, 7).reshape(hidden_count)
    )

    padded = extend(feature_map).astype(F4)
    conv = jnp.zeros((row_count, col_count, channels), F4)
    for tap_row in range(7):
        for tap_col in range(7):
            conv = (
                conv
                + padded[tap_row : tap_row + row_count, tap_col : tap_col + col_count]
                * kernel[tap_row, tap_col]
            )
    average = jnp.mean(conv, -1, keepdims=True)
    centered = conv - average
    variance = jnp.mean(centered * centered, -1, keepdims=True)
    inv_std = lax.rsqrt(variance + 1e-06)
    unit_scaled = centered * inv_std
    normed = (unit_scaled * ln_gain + ln_bias).astype(BF).reshape(pixels, channels)
    hidden = lax.dot_general(normed, w_in_t, contract_last, preferred_element_type=F4) + b_mine
    act_value, slope = gelu_parts(hidden)
    activated = act_value.astype(BF)
    mixed = jnp.dot(activated, w_out_full, preferred_element_type=F4) + b_out
    source = feature_map.astype(F4).reshape(pixels, channels)
    block_out = (source + layer_scale * mixed).astype(BF).reshape(row_count, col_count, channels)
    grad_flow = cotangent.astype(F4).reshape(pixels, channels)
    grad_mixed = grad_flow * layer_scale
    mixed_low = grad_mixed.astype(BF)
    grad_act = lax.dot_general(mixed_low, w_out_full, contract_last, preferred_element_type=F4)
    grad_hidden = (grad_act * slope).astype(BF)
    wout_term = lax.dot_general(activated, mixed_low, contract_first, preferred_element_type=F4)
    win_term = lax.dot_general(grad_hidden, normed, contract_first, preferred_element_type=F4)

    terms = jnp.stack([win_term, wout_term], 0)
    terms = fan_reduce(terms, "c", (1,), 2, BF)
    terms = fan_reduce(terms, "x", (1, 2, 3), 4, BF)
    terms = fan_reduce(terms, Y, (1, 2, 3), 4, BF)
    for bit in (1, 2, 4):
        terms = fan_reduce(terms, "z", (bit,), 2, F4)
    grad_w_in, grad_w_out = terms[0].T, terms[1]

    grad_normed = jnp.dot(grad_hidden, w_in_t, preferred_element_type=F4)
    grad_normed = grad_normed.reshape(row_count, col_count, channels)
    grad_gain = jnp.sum(grad_normed * unit_scaled, (0, 1))
    grad_lnb = jnp.sum(grad_normed, (0, 1))
    scaled_grad = grad_normed * ln_gain
    grad_conv = inv_std * (
        scaled_grad
        - jnp.mean(scaled_grad, -1, keepdims=True)
        - unit_scaled * jnp.mean(scaled_grad * unit_scaled, -1, keepdims=True)
    )
    tap_terms = []
    for tap_row in range(7):
        for tap_col in range(7):
            tap_terms.append(
                jnp.sum(
                    padded[tap_row : tap_row + row_count, tap_col : tap_col + col_count]
                    * grad_conv,
                    (0, 1),
                )
            )
    grad_pad = extend(grad_conv.astype(BF)).astype(F4)
    back_conv = jnp.zeros((row_count, col_count, channels), F4)
    for tap_row in range(7):
        for tap_col in range(7):
            back_conv = (
                back_conv
                + grad_pad[
                    6 - tap_row : 6 - tap_row + row_count, 6 - tap_col : 6 - tap_col + col_count
                ]
                * kernel[tap_row, tap_col]
            )
    grad_input = (cotangent.astype(F4) + back_conv).astype(BF)
    bias_local = jnp.sum(grad_hidden.astype(F4), 0)
    bias_local = (
        bias_local.reshape(2, 4, 2, 2, 2, 2, 2, units)
        .transpose(6, 5, 4, 2, 0, 1, 3, 7)
        .reshape(hidden_count // channels, channels)
    )
    small = jnp.concatenate(
        [
            jnp.stack(tap_terms, 0),
            grad_gain[None],
            grad_lnb[None],
            jnp.sum(grad_mixed, 0)[None],
            jnp.sum(grad_flow * mixed, 0)[None],
            bias_local,
        ],
        0,
    )
    for axis, bits in (("c", (1,)), ("x", (1, 2)), (Y, (1, 2)), ("z", (1, 2, 4))):
        for bit in bits:
            small = small + swap(small, axis, bit)
    return (block_out, grad_input, grad_w_in, grad_w_out, small[:53], small[53:].reshape(hidden_count))


def solution(mesh):
    fine = Mesh(mesh.devices.reshape(8, 2, 2, 4, 2), ("z", "yh", "c", "x", "yl"))
    every = ROW + COL
    placed = (
        P(ROW, COL, None),
        P(),
        P(),
        P(),
        P(None, every),
        P(),
        P(every, None),
        P(),
        P(),
        P(ROW, COL, None),
    )
    return jax.shard_map(
        on_device,
        mesh=fine,
        in_specs=placed,
        out_specs=(
            P(ROW, COL, None),
            P(ROW, COL, None),
            P(None, every),
            P(every, None),
            P(),
            P(),
        ),
        check_vma=False,
    )
```

time: 1690 us -> 158 us (0.09)
  waiting for transfers between devices: 1530 us -> 37.6 us
  blocking collectives: 89.9 us -> 0 us
  starting transfers between devices: 19.2 us -> 75.7 us
    all_gather x2 -> x0, waiting for transfers between devices: 1350 us -> none  [the longest x1 684 us: on_device(): w_out_full = lax.all_gather(w_out, ('row', 'col'), axis=0, tiled=True)]
    unnamed x4 -> x0, waiting for transfers between devices: 174 us -> none
    psum x1 -> x0, blocking collectives: 89.9 us -> none  [on_device(): small_grads, grad_b_in = lax.psum((small_local, bias_local), ('row', 'col'))]
    ppermute x0 -> x28, starting transfers between devices: none -> 55.3 us  [swap(): return lax.ppermute(x, axis, [(i, i ^ flip) for i in range(count)])]
    ppermute x0 -> x28, waiting for transfers between devices: none -> 37.6 us  [swap(): return lax.ppermute(x, axis, [(i, i ^ flip) for i in range(count)])]
  transfers between devices with their start and end apart: 11 -> 36, of which waited for: 6 -> 9; matrix products, arithmetic and copies ran while one was open for 1% -> 17% of each run, Pallas kernels for 0% -> 0%
where the time goes in v1:
time: 158 us; the launch traced here: 156 us
  starting transfers between devices  75.7 us (48%)
  waiting for transfers between devices  37.6 us (24%)
  other arithmetic  19.2 us (12%)
  local copies, waits for them, and re-layouts  12.4 us (8%)
  matrix products  8.12 us (5%)
  between operations  2.98 us (2%)
    ppermute x28, starting transfers between devices, swap(): return lax.ppermute(x, axis, [(i, i ^ flip) for i in range(count)])  55.3 us
    ppermute x28, waiting for transfers between devices, swap(): return lax.ppermute(x, axis, [(i, i ^ flip) for i in range(count)])  37.6 us
    ppermute x4, starting transfers between devices, padded_2(): after = lax.ppermute(first, axis, down)  11.3 us
    ppermute x4, starting transfers between devices, padded_2(): before = lax.ppermute(last, axis, up)  9.11 us
    convert_element_type x1, other arithmetic, on_device(): grad_input = (cotangent.astype(F4) + back_conv).astype(BF)  4.15 us
    slice x3, local copies, waits for them, and re-layouts, on_device(): kernel[tap_row, tap_col]  3.99 us
    reduce_sum x1, other arithmetic, on_device(): average = jnp.mean(conv, -1, keepdims=True)  3.78 us
    reduce_sum x3, other arithmetic, on_device(): jnp.sum(padded[tap_row:tap_row + row_count, tap_col:tap_col + col_count]...  3.29 us
  transfers between devices with their start and end apart: 36, of which 9 were waited for; matrix products, arithmetic and copies ran while one was open for 17% of the time, Pallas kernels for 0%

profile of v1, /device:TPU:6, one launch (start us, length us, event | category | flops | bytes accessed | tf_op | source)
XLA Modules:
  0.0 155.9 jit_solution(3263351866944970534)
XLA Ops:
  0.6 0.8 pad_maximum_fusion.7
  1.4 7.3 %collective-permute-start.4 = (bf16[2,6,384]{2,1,0:T(8,128)(2,1)S(1)}, bf16[2,6,384]{2,1,0:T(8,128)(2,1)S(1)}, u32[]{:S(2)}, u32[]{:S(2)}) collective-permute-start(bf16[2,6,384]{2,1,0:T(8,128)(2,1)S(1)} %pad_maximum_fusion.7), channel_id=1, source_target_pairs={{0,128},{32,160},{64,192},{96,224},{128,0},{160,32},{192,64},{224,... | collective-permute-start | bytes 27656 | tf_op jit(solution)/shard_map/ppermute | solution.py:18
  8.7 0.9 fusion.78
  9.6 1.3 collective-permute-start.1
  10.9 3.0 %collective-permute-start = (bf16[3,32,384]{2,1,0:T(8,128)(2,1)S(1)}, bf16[3,32,384]{2,1,0:T(8,128)(2,1)S(1)}, u32[]{:S(2)}, u32[]{:S(2)}) collective-permute-start(bf16[3,32,384]{2,1,0:T(8,128)(2,1)S(1)} %get-tuple-element.132), channel_id=1, source_target_pairs={{0,8},{8,16},{16,24},{24,32},{32,40},{40,48},{48,56},{56,64},{64,7... | collective-permute-start | bytes 221192 | tf_op jit(solution)/shard_map/ppermute | solution.py:28
  14.0 1.0 fusion.65
  15.0 0.7 broadcast_select_fusion.7
  15.7 3.9 %collective-permute-start.5 = (bf16[2,12,384]{2,1,0:T(8,128)(2,1)S(1)}, bf16[2,12,384]{2,1,0:T(8,128)(2,1)S(1)}, u32[]{:S(2)}, u32[]{:S(2)}) collective-permute-start(bf16[2,12,384]{2,1,0:T(8,128)(2,1)S(1)} %pad_maximum_fusion.6), channel_id=1, source_target_pairs={{0,64},{32,96},{64,0},{96,32},{128,192},{160,224},{192,128},{224,1... | collective-permute-start | bytes 55304 | tf_op jit(solution)/shard_map/ppermute | solution.py:18
  19.6 1.2 slice_reduce_fusion.47
  21.4 2.6 %collective-permute-start.6 = (bf16[2,24,384]{2,1,0:T(8,128)(2,1)S(1)}, bf16[2,24,384]{2,1,0:T(8,128)(2,1)S(1)}, u32[]{:S(2)}, u32[]{:S(2)}) collective-permute-start(bf16[2,24,384]{2,1,0:T(8,128)(2,1)S(1)} %pad_maximum_fusion.5), channel_id=1, source_target_pairs={{0,32},{32,0},{64,96},{96,64},{128,160},{160,128},{192,224},{224,1... | collective-permute-start | bytes 110600 | tf_op jit(solution)/shard_map/ppermute | solution.py:18
  24.0 1.2 slice_reduce_fusion.48
  25.4 0.5 collective-permute-done.6
  26.0 2.0 %collective-permute-start.8 = (bf16[2,48,384]{2,1,0:T(8,128)(2,1)S(1)}, bf16[2,48,384]{2,1,0:T(8,128)(2,1)S(1)}, u32[]{:S(2)}, u32[]{:S(2)}) collective-permute-start(bf16[2,48,384]{2,1,0:T(8,128)(2,1)S(1)} %get-tuple-element.133), channel_id=1, source_target_pairs={{0,16},{1,17},{16,0},{17,1},{2,18},{3,19},{18,2},{19,3},{4,20},{5,... | collective-permute-start | bytes 221192 | tf_op jit(solution)/shard_map/ppermute | solution.py:18
  28.0 0.7 collective-permute-start.7
  28.7 1.5 collective-permute-start.9
  30.3 2.8 %collective-permute-start.2 = (bf16[14,3,384]{2,1,0:T(4,128)(2,1)S(1)}, bf16[14,3,384]{2,1,0:T(4,128)(2,1)S(1)}, u32[]{:S(2)}, u32[]{:S(2)}) collective-permute-start(bf16[14,3,384]{2,1,0:T(4,128)(2,1)S(1)} %get-tuple-element.124), channel_id=1, source_target_pairs={{0,1},{1,2},{2,3},{3,4},{4,5},{5,6},{6,7},{8,9},{9,10},{10,11},{11... | collective-permute-start | bytes 96776 | tf_op jit(solution)/shard_map/ppermute | solution.py:28
  33.1 4.0 %collective-permute-start.3 = (bf16[14,3,384]{2,1,0:T(4,128)(2,1)S(1)}, bf16[14,3,384]{2,1,0:T(4,128)(2,1)S(1)}, u32[]{:S(2)}, u32[]{:S(2)}) collective-permute-start(bf16[14,3,384]{2,1,0:T(4,128)(2,1)S(1)} %get-tuple-element.125), channel_id=1, source_target_pairs={{1,0},{2,1},{3,2},{4,3},{5,4},{6,5},{7,6},{9,8},{10,9},{11,10},{12... | collective-permute-start | bytes 96776 | tf_op jit(solution)/shard_map/ppermute | solution.py:29
  37.2 0.9 collective-permute-start.10
  38.1 1.6 %slice_reduce_fusion.46 = (f32[384]{0:T(512)S(1)}, f32[384]{0:T(512)}, f32[384]{0:T(512)}, f32[384]{0:T(512)}, f32[384]{0:T(512)}, /*index=5*/f32[384]{0:T(512)}...) fusion(f32[7,7,384]{2,1,0:T(8,128)} %param.11), kind=kLoop, calls=%fused_computation.289 | loop fusion | bytes 33792 | tf_op jit(solution)/shard_map/slice | solution.py:104
  40.2 0.5 broadcast_in_dim.32
  40.8 0.6 collective-permute-start.11
  41.5 3.4 %collective-permute-start.12 = (bf16[2,192,384]{2,1,0:T(8,128)(2,1)S(1)}, bf16[2,192,384]{2,1,0:T(8,128)(2,1)S(1)}, u32[]{:S(2)}, u32[]{:S(2)}) collective-permute-start(bf16[2,192,384]{2,1,0:T(8,128)(2,1)S(1)} %constant_dynamic-update-slice_fusion.7), channel_id=1, source_target_pairs={{0,6},{2,4},{4,2},{6,0},{1,7},{3,5},{5,3},{7,1},{8,14},{10,12},{12... | collective-permute-start | bytes 884744 | tf_op jit(solution)/shard_map/ppermute | solution.py:18
  45.0 2.2 %collective-permute-done.10 = bf16[2,192,384]{2,1,0:T(8,128)(2,1)S(1)} collective-permute-done((bf16[2,192,384]{2,1,0:T(8,128)(2,1)S(1)}, bf16[2,192,384]{2,1,0:T(8,128)(2,1)S(1)}, u32[]{:S(2)}, u32[]{:S(2)}) %collective-permute-start.10) | collective-permute-done | bytes 294944 | tf_op jit(solution)/shard_map/ppermute | solution.py:18
  47.3 4.0 %collective-permute-done.11 = bf16[2,192,384]{2,1,0:T(8,128)(2,1)S(1)} collective-permute-done((bf16[2,192,384]{2,1,0:T(8,128)(2,1)S(1)}, bf16[2,192,384]{2,1,0:T(8,128)(2,1)S(1)}, u32[]{:S(2)}, u32[]{:S(2)}) %collective-permute-start.11) | collective-permute-done | bytes 294944 | tf_op jit(solution)/shard_map/ppermute | solution.py:18
  51.3 4.5 %collective-permute-done.12 = bf16[2,192,384]{2,1,0:T(8,128)(2,1)S(1)} collective-permute-done((bf16[2,192,384]{2,1,0:T(8,128)(2,1)S(1)}, bf16[2,192,384]{2,1,0:T(8,128)(2,1)S(1)}, u32[]{:S(2)}, u32[]{:S(2)}) %collective-permute-start.12) | collective-permute-done | bytes 294944 | tf_op jit(solution)/shard_map/ppermute | solution.py:18
  56.6 3.8 %fusion.75 = (f32[8,32]{1,0:T(8,128)S(1)}, f32[8,32,384]{2,1,0:T(8,128)S(1)}) fusion(f32[384]{0:T(512)} %get-tuple-element.106, f32[14,38,384]{2,1,0:T(8,128)S(1)} %maximum_convert_fusion, f32[384]{0:T(512)} %get-tuple-element.107, f32[384]{0:T(512)S(1)} %get-tuple-element.60, f32[384]{0:T(512)S(1)} %get-tuple-element.61, f32[384]{0:T(512)S(1)} %get-tuple-element.62, ...), kind=kLoop, calls=%fused_computation.294 | loop fusion | flops 9633536 | bytes 19737088 | tf_op jit(solution)/shard_map/reduce_sum | solution.py:106
  61.0 0.7 multiply_convert_fusion
  61.6 2.4 %convert_reduce_fusion = (f32[1536]{0:T(1024)S(1)}, bf16[256,1536]{1,0:T(8,128)(2,1)S(1)}) fusion(f32[256,1536]{1,0:T(8,128)S(1)} %get-tuple-element.144, bf16[256,384]{1,0:T(8,128)(2,1)S(1)} %bitcast.61, bf16[2,768,384]{2,1,0:T(8,128)(2,1)S(1)} %get-tuple-element.114, bf16[2,768,384]{2,1,0:T(8,128)(2,1)S(1)} %get-tuple-element.115), kind=kOutput, calls=%fused_computation.20 | convolution fusion | flops 309066240 | bytes 4921344 | tf_op jit(solution)/shard_map/dot_general | solution.py:121
  64.0 0.6 convolution_bitcast_fusion.1
  64.7 1.9 %multiply_reduce_fusion = (f32[384]{0:T(512)}, f32[8,32]{1,0:T(8,128)S(1)}, f32[8,32]{1,0:T(8,128)S(1)}, f32[384]{0:T(512)}, f32[8,32,384]{2,1,0:T(8,128)}) fusion(f32[8,32,384]{2,1,0:T(8,128)S(1)} %get-tuple-element.110, f32[8,32]{1,0:T(8,128)S(1)} %add_rsqrt_fusion, f32[8,32]{1,0:T(8,128)S(1)} %broadcast_multiply_fusion.2, f32[384]{0:T(512)S(1)} %copy-done.86, ...), kind=kOutput, calls=%fused_computation.146 | convolution fusion | flops 305232640 | bytes 3940864 | tf_op jit(solution)/shard_map/dot_general | solution.py:134
  66.6 1.9 %fusion.68 = (f32[384]{0:T(512)}, bf16[256,384]{1,0:T(8,128)(2,1)}, bf16[256,384]{1,0:T(8,128)(2,1)S(1)}) fusion(bf16[8,32,384]{2,1,0:T(8,128)(2,1)S(1)} %copy-done.3, f32[384]{0:T(512)S(1)} %copy-done.90, bf16[8,32,384]{2,1,0:T(8,128)(2,1)S(1)} %copy-done.5, f32[384]{0:T(512)S(1)} %copy-done.94, bf16[256,1536]{1,0:T(8,128)(2,1)S(1)} %get-tuple-element.143, ...), kind=kOutput, calls=%fused_computation.145 | convolution fusion | flops 305331840 | bytes 3936768 | tf_op jit(solution)/shard_map/dot_general | solution.py:115
  68.5 0.6 convolution_bitcast_fusion
  69.2 1.3 fusion.2
  71.0 0.5 collective-permute-start.18
  71.7 0.8 reshape.82
  72.6 2.0 %multiply_reduce_fusion.1 = (f32[384]{0:T(512)S(1)}, f32[384]{0:T(512)S(1)}, f32[384]{0:T(512)S(1)}, f32[384]{0:T(512)S(1)}, f32[384]{0:T(512)S(1)}, /*index=5*/...) fusion(f32[14,38,384]{2,1,0:T(8,128)S(1)} %maximum_convert_fusi, ...), kind=kLoop, calls=%fused_computation.147 | loop fusion | flops 4220160 | bytes 8290816 | tf_op jit(solution)/shard_map/reduce_sum | solution.py:148
  74.8 0.7 multiply_reduce_fusion.19
  75.5 0.6 multiply_reduce_fusion.37
  76.9 1.9 %fusion.4 = f32[2,768,384]{2,1,0:T(8,128)S(1)} fusion(s32[]{:T(128)S(6)} %select_n.179, f32[1,1536,384]{2,1,0:T(8,128)S(1)} %convolution_bitcast_fusion.1, f32[1,1536,384]{2,1,0:T(8,128)} %copy-done, bf16[2,768,384]{2,1,0:T(8,128)(2,1)} %collective-permute-done.18), kind=kLoop, calls=%fused_computation.13 | loop fusion | flops 1769472 | bytes 8257540 | tf_op jit(solution)/shard_map/add | solution.py:72
  78.8 1.4 copy-done.2
  80.5 2.4 %collective-permute-start.21 = (bf16[2,192,384]{2,1,0:T(8,128)(2,1)S(1)}, bf16[2,192,384]{2,1,0:T(8,128)(2,1)S(1)}, u32[]{:S(2)}, u32[]{:S(2)}) collective-permute-start(bf16[2,192,384]{2,1,0:T(8,128)(2,1)S(1)} %get-tuple-element.112), channel_id=1, source_target_pairs={{0,6},{2,4},{4,2},{6,0},{1,7},{3,5},{5,3},{7,1},{8,14},{10,12},{12... | collective-permute-start | bytes 884744 | tf_op jit(solution)/shard_map/ppermute | solution.py:18
  82.9 1.6 %collective-permute-start.20 = (bf16[2,192,384]{2,1,0:T(8,128)(2,1)S(1)}, bf16[2,192,384]{2,1,0:T(8,128)(2,1)S(1)}, u32[]{:S(2)}, u32[]{:S(2)}) collective-permute-start(bf16[2,192,384]{2,1,0:T(8,128)(2,1)S(1)} %get-tuple-element.113), channel_id=1, source_target_pairs={{0,4},{2,6},{4,0},{6,2},{1,5},{3,7},{5,1},{7,3},{8,12},{10,14},{12... | collective-permute-start | bytes 884744 | tf_op jit(solution)/shard_map/ppermute | solution.py:18
  84.9 13.3 %collective-permute-done.29 = f32[57,384]{1,0:T(8,128)S(1)} collective-permute-done((f32[57,384]{1,0:T(8,128)S(1)}, f32[57,384]{1,0:T(8,128)S(1)}, u32[]{:S(2)}, u32[]{:S(2)}) %collective-permute-start.29) | collective-permute-done | bytes 87584 | tf_op jit(solution)/shard_map/ppermute | solution.py:18
  98.3 2.0 %collective-permute-start.30 = (f32[57,384]{1,0:T(8,128)S(1)}, f32[57,384]{1,0:T(8,128)S(1)}, u32[]{:S(2)}, u32[]{:S(2)}) collective-permute-start(f32[57,384]{1,0:T(8,128)S(1)} %add.647), channel_id=1, source_target_pairs={{0,4},{2,6},{4,0},{6,2},{1,5},{3,7},{5,1},{7,3},{8,12},{10,14},{12... | collective-permute-start | bytes 262664 | tf_op jit(solution)/shard_map/ppermute | solution.py:18
  100.3 4.2 %collective-permute-done.30 = f32[57,384]{1,0:T(8,128)S(1)} collective-permute-done((f32[57,384]{1,0:T(8,128)S(1)}, f32[57,384]{1,0:T(8,128)S(1)}, u32[]{:S(2)}, u32[]{:S(2)}) %collective-permute-start.30) | collective-permute-done | bytes 87584 | tf_op jit(solution)/shard_map/ppermute | solution.py:18
  104.5 0.6 collective-permute-start.31
  105.1 4.1 %collective-permute-done.31 = f32[57,384]{1,0:T(8,128)S(1)} collective-permute-done((f32[57,384]{1,0:T(8,128)S(1)}, f32[57,384]{1,0:T(8,128)S(1)}, u32[]{:S(2)}, u32[]{:S(2)}) %collective-permute-start.31) | collective-permute-done | bytes 87584 | tf_op jit(solution)/shard_map/ppermute | solution.py:18
  109.2 4.2 %collective-permute-start.32 = (f32[57,384]{1,0:T(8,128)S(1)}, f32[57,384]{1,0:T(8,128)S(1)}, u32[]{:S(2)}, u32[]{:S(2)}) collective-permute-start(f32[57,384]{1,0:T(8,128)S(1)} %add.649), channel_id=1, source_target_pairs={{0,16},{1,17},{16,0},{17,1},{2,18},{3,19},{18,2},{19,3},{4,20},{5,... | collective-permute-start | bytes 262664 | tf_op jit(solution)/shard_map/ppermute | solution.py:18
  113.4 1.2 convert_add_fusion
  114.8 0.6 collective-permute-start.24
  115.4 3.5 %collective-permute-start.23 = (bf16[2,48,384]{2,1,0:T(8,128)(2,1)S(1)}, bf16[2,48,384]{2,1,0:T(8,128)(2,1)S(1)}, u32[]{:S(2)}, u32[]{:S(2)}) collective-permute-start(bf16[2,48,384]{2,1,0:T(8,128)(2,1)S(1)} %get-tuple-element.118), channel_id=1, source_target_pairs={{0,16},{1,17},{16,0},{17,1},{2,18},{3,19},{18,2},{19,3},{4,20},{5,... | collective-permute-start | bytes 221192 | tf_op jit(solution)/shard_map/ppermute | solution.py:18
  118.9 1.3 collective-permute-start.14
  120.2 1.3 collective-permute-start.15
  121.5 6.8 %collective-permute-start.33 = (f32[57,384]{1,0:T(8,128)S(1)}, f32[57,384]{1,0:T(8,128)S(1)}, u32[]{:S(2)}, u32[]{:S(2)}) collective-permute-start(f32[57,384]{1,0:T(8,128)S(1)} %add.650), channel_id=1, source_target_pairs={{0,32},{32,0},{64,96},{96,64},{128,160},{160,128},{192,224},{224,1... | collective-permute-start | bytes 262664 | tf_op jit(solution)/shard_map/ppermute | solution.py:18
  128.9 2.0 %collective-permute-start.16 = (bf16[14,3,384]{2,1,0:T(4,128)(2,1)S(1)}, bf16[14,3,384]{2,1,0:T(4,128)(2,1)S(1)}, u32[]{:S(2)}, u32[]{:S(2)}) collective-permute-start(bf16[14,3,384]{2,1,0:T(4,128)(2,1)S(1)} %get-tuple-element.122), channel_id=1, source_target_pairs={{0,1},{1,2},{2,3},{3,4},{4,5},{5,6},{6,7},{8,9},{9,10},{10,11},{11... | collective-permute-start | bytes 96776 | tf_op jit(solution)/shard_map/ppermute | solution.py:28
  130.9 4.7 %collective-permute-start.17 = (bf16[14,3,384]{2,1,0:T(4,128)(2,1)S(1)}, bf16[14,3,384]{2,1,0:T(4,128)(2,1)S(1)}, u32[]{:S(2)}, u32[]{:S(2)}) collective-permute-start(bf16[14,3,384]{2,1,0:T(4,128)(2,1)S(1)} %get-tuple-element.123), channel_id=1, source_target_pairs={{1,0},{2,1},{3,2},{4,3},{5,4},{6,5},{7,6},{9,8},{10,9},{11,10},{12... | collective-permute-start | bytes 96776 | tf_op jit(solution)/shard_map/ppermute | solution.py:29
  135.7 2.9 %collective-permute-start.34 = (f32[57,384]{1,0:T(8,128)S(1)}, f32[57,384]{1,0:T(8,128)S(1)}, u32[]{:S(2)}, u32[]{:S(2)}) collective-permute-start(f32[57,384]{1,0:T(8,128)S(1)} %add.651), channel_id=1, source_target_pairs={{0,64},{32,96},{64,0},{96,32},{128,192},{160,224},{192,128},{224,1... | collective-permute-start | bytes 262664 | tf_op jit(solution)/shard_map/ppermute | solution.py:18
  139.0 4.4 %collective-permute-done.34 = f32[57,384]{1,0:T(8,128)S(1)} collective-permute-done((f32[57,384]{1,0:T(8,128)S(1)}, f32[57,384]{1,0:T(8,128)S(1)}, u32[]{:S(2)}, u32[]{:S(2)}) %collective-permute-start.34) | collective-permute-done | bytes 87584 | tf_op jit(solution)/shard_map/ppermute | solution.py:18
  143.4 1.5 collective-permute-start.35
  144.9 4.6 %collective-permute-start.27 = (f32[2,6,384]{2,1,0:T(8,128)S(1)}, f32[2,6,384]{2,1,0:T(8,128)S(1)}, u32[]{:S(2)}, u32[]{:S(2)}) collective-permute-start(f32[2,6,384]{2,1,0:T(8,128)S(1)} %constant_dynamic-slice_fusion), channel_id=1, source_target_pairs={{0,128},{32,160},{64,192},{96,224},{128,0},{160,32},{192,64},{224,... | collective-permute-start | bytes 55304 | tf_op jit(solution)/shard_map/ppermute | solution.py:18
  149.9 4.1 %fusion.16 = bf16[8,32,384]{2,1,0:T(8,128)(2,1)} fusion(f32[14,38,384]{2,1,0:T(8,128)S(1)} %maximum_convert_fusion.1, bf16[8,32,384]{2,1,0:T(8,128)(2,1)S(1)} %copy-done.4, f32[384]{0:T(512)} %get-tuple-element.106, f32[384]{0:T(512)} %get-tuple-element.107, f32[384]{0:T(512)S(1)} %copy-done.48, f32[384]{0:T(512)S(1)} %copy-done.50, f32[384]{0:T(512)S(1)} %copy-done.52, ...), kind=kLoop, calls=%fused_computation.41 | loop fusion | flops 9830400 | bytes 19736064 | tf_op jit(solution)/shard_map/convert_element_type | solution.py:165
  154.1 0.6 slice.848
  154.7 0.6 reshape.83
  155.3 0.6 slice_bitcast_fusion
  (328 shorter events, 5.9 us)
Async XLA Ops:
  1.4 13.6 %collective-permute-start.4 = (bf16[2,6,384]{2,1,0:T(8,128)(2,1)S(1)}, bf16[2,6,384]{2,1,0:T(8,128)(2,1)S(1)}, u32[]{:S(2)}, u32[]{:S(2)}) collective-permute-start(bf16[2,6,384]{2,1,0:T(8,128)(2,1)S(1)} %pad_maximum_fusion.7), channel_id=1, source_target_pairs={{0,128},{32,160},{64,192},{96,224},{128,0},{160,32},{192,64},{224,... | collective-permute-start | bytes 27656 | tf_op jit(solution)/shard_map/ppermute | solution.py:18
  9.6 20.7 %collective-permute-start.1 = (bf16[3,32,384]{2,1,0:T(8,128)(2,1)S(1)}, bf16[3,32,384]{2,1,0:T(8,128)(2,1)S(1)}, u32[]{:S(2)}, u32[]{:S(2)}) collective-permute-start(bf16[3,32,384]{2,1,0:T(8,128)(2,1)S(1)} %get-tuple-element.131), channel_id=1, source_target_pairs={{8,0},{16,8},{24,16},{32,24},{40,32},{48,40},{56,48},{64,56},{72,6... | collective-permute-start | bytes 221192 | tf_op jit(solution)/shard_map/ppermute | solution.py:29
  10.9 19.3 %collective-permute-start = (bf16[3,32,384]{2,1,0:T(8,128)(2,1)S(1)}, bf16[3,32,384]{2,1,0:T(8,128)(2,1)S(1)}, u32[]{:S(2)}, u32[]{:S(2)}) collective-permute-start(bf16[3,32,384]{2,1,0:T(8,128)(2,1)S(1)} %get-tuple-element.132), channel_id=1, source_target_pairs={{0,8},{8,16},{16,24},{24,32},{32,40},{40,48},{48,56},{56,64},{64,7... | collective-permute-start | bytes 221192 | tf_op jit(solution)/shard_map/ppermute | solution.py:28
  15.7 5.7 %collective-permute-start.5 = (bf16[2,12,384]{2,1,0:T(8,128)(2,1)S(1)}, bf16[2,12,384]{2,1,0:T(8,128)(2,1)S(1)}, u32[]{:S(2)}, u32[]{:S(2)}) collective-permute-start(bf16[2,12,384]{2,1,0:T(8,128)(2,1)S(1)} %pad_maximum_fusion.6), channel_id=1, source_target_pairs={{0,64},{32,96},{64,0},{96,32},{128,192},{160,224},{192,128},{224,1... | collective-permute-start | bytes 55304 | tf_op jit(solution)/shard_map/ppermute | solution.py:18
  20.8 35.3 %copy-start.7 = (f32[384]{0:T(512)}, f32[384]{0:T(512)S(1)}, u32[]{:S(2)}) copy-start(f32[384]{0:T(512)S(1)} %get-tuple-element.78) | copy-start | bytes 4612
  20.8 35.3 %copy-start.9 = (f32[384]{0:T(512)}, f32[384]{0:T(512)S(1)}, u32[]{:S(2)}) copy-start(f32[384]{0:T(512)S(1)} %get-tuple-element.79) | copy-start | bytes 4612
  20.8 35.3 %copy-start.11 = (f32[384]{0:T(512)}, f32[384]{0:T(512)S(1)}, u32[]{:S(2)}) copy-start(f32[384]{0:T(512)S(1)} %get-tuple-element.80) | copy-start | bytes 4612
  20.8 35.3 %copy-start.13 = (f32[384]{0:T(512)}, f32[384]{0:T(512)S(1)}, u32[]{:S(2)}) copy-start(f32[384]{0:T(512)S(1)} %get-tuple-element.81) | copy-start | bytes 4612
  20.8 35.3 %copy-start.15 = (f32[384]{0:T(512)}, f32[384]{0:T(512)S(1)}, u32[]{:S(2)}) copy-start(f32[384]{0:T(512)S(1)} %get-tuple-element.82) | copy-start | bytes 4612
  20.8 35.3 %copy-start.17 = (f32[384]{0:T(512)}, f32[384]{0:T(512)S(1)}, u32[]{:S(2)}) copy-start(f32[384]{0:T(512)S(1)} %get-tuple-element.83) | copy-start | bytes 4612
  20.9 35.3 %copy-start.19 = (f32[384]{0:T(512)}, f32[384]{0:T(512)S(1)}, u32[]{:S(2)}) copy-start(f32[384]{0:T(512)S(1)} %get-tuple-element.84) | copy-start | bytes 4612
  20.9 35.3 %copy-start.21 = (f32[384]{0:T(512)}, f32[384]{0:T(512)S(1)}, u32[]{:S(2)}) copy-start(f32[384]{0:T(512)S(1)} %get-tuple-element.85) | copy-start | bytes 4612
  20.9 35.3 %copy-start.23 = (f32[384]{0:T(512)}, f32[384]{0:T(512)S(1)}, u32[]{:S(2)}) copy-start(f32[384]{0:T(512)S(1)} %get-tuple-element.86) | copy-start | bytes 4612
  20.9 35.3 %copy-start.25 = (f32[384]{0:T(512)}, f32[384]{0:T(512)S(1)}, u32[]{:S(2)}) copy-start(f32[384]{0:T(512)S(1)} %get-tuple-element.87) | copy-start | bytes 4612
  20.9 35.3 %copy-start.27 = (f32[384]{0:T(512)}, f32[384]{0:T(512)S(1)}, u32[]{:S(2)}) copy-start(f32[384]{0:T(512)S(1)} %get-tuple-element.88) | copy-start | bytes 4612
  20.9 35.3 %copy-start.29 = (f32[384]{0:T(512)}, f32[384]{0:T(512)S(1)}, u32[]{:S(2)}) copy-start(f32[384]{0:T(512)S(1)} %get-tuple-element.89) | copy-start | bytes 4612
  20.9 35.3 %copy-start.31 = (f32[384]{0:T(512)}, f32[384]{0:T(512)S(1)}, u32[]{:S(2)}) copy-start(f32[384]{0:T(512)S(1)} %get-tuple-element.90) | copy-start | bytes 4612
  20.9 35.3 %copy-start.33 = (f32[384]{0:T(512)}, f32[384]{0:T(512)S(1)}, u32[]{:S(2)}) copy-start(f32[384]{0:T(512)S(1)} %get-tuple-element.91) | copy-start | bytes 4612
  20.9 35.3 %copy-start.35 = (f32[384]{0:T(512)}, f32[384]{0:T(512)S(1)}, u32[]{:S(2)}) copy-start(f32[384]{0:T(512)S(1)} %get-tuple-element.92) | copy-start | bytes 4612
  20.9 35.3 %copy-start.37 = (f32[384]{0:T(512)}, f32[384]{0:T(512)S(1)}, u32[]{:S(2)}) copy-start(f32[384]{0:T(512)S(1)} %get-tuple-element.93) | copy-start | bytes 4612
  21.0 35.3 %copy-start.39 = (f32[384]{0:T(512)}, f32[384]{0:T(512)S(1)}, u32[]{:S(2)}) copy-start(f32[384]{0:T(512)S(1)} %get-tuple-element.94) | copy-start | bytes 4612
  21.0 35.3 %copy-start.41 = (f32[384]{0:T(512)}, f32[384]{0:T(512)S(1)}, u32[]{:S(2)}) copy-start(f32[384]{0:T(512)S(1)} %get-tuple-element.95) | copy-start | bytes 4612
  21.0 35.3 %copy-start.43 = (f32[384]{0:T(512)}, f32[384]{0:T(512)S(1)}, u32[]{:S(2)}) copy-start(f32[384]{0:T(512)S(1)} %get-tuple-element.96) | copy-start | bytes 4612
  21.4 4.5 %collective-permute-start.6 = (bf16[2,24,384]{2,1,0:T(8,128)(2,1)S(1)}, bf16[2,24,384]{2,1,0:T(8,128)(2,1)S(1)}, u32[]{:S(2)}, u32[]{:S(2)}) collective-permute-start(bf16[2,24,384]{2,1,0:T(8,128)(2,1)S(1)} %pad_maximum_fusion.5), channel_id=1, source_target_pairs={{0,32},{32,0},{64,96},{96,64},{128,160},{160,128},{192,224},{224,1... | collective-permute-start | bytes 110600 | tf_op jit(solution)/shard_map/ppermute | solution.py:18
  25.2 31.1 %copy-start.45 = (f32[384]{0:T(512)}, f32[384]{0:T(512)S(1)}, u32[]{:S(2)}) copy-start(f32[384]{0:T(512)S(1)} %get-tuple-element.59) | copy-start | bytes 4612
  25.2 31.1 %copy-start.47 = (f32[384]{0:T(512)}, f32[384]{0:T(512)S(1)}, u32[]{:S(2)}) copy-start(f32[384]{0:T(512)S(1)} %get-tuple-element.60) | copy-start | bytes 4612
  25.2 31.1 %copy-start.49 = (f32[384]{0:T(512)}, f32[384]{0:T(512)S(1)}, u32[]{:S(2)}) copy-start(f32[384]{0:T(512)S(1)} %get-tuple-element.61) | copy-start | bytes 4612
  25.2 31.1 %copy-start.51 = (f32[384]{0:T(512)}, f32[384]{0:T(512)S(1)}, u32[]{:S(2)}) copy-start(f32[384]{0:T(512)S(1)} %get-tuple-element.62) | copy-start | bytes 4612
  25.2 31.1 %copy-start.53 = (f32[384]{0:T(512)}, f32[384]{0:T(512)S(1)}, u32[]{:S(2)}) copy-start(f32[384]{0:T(512)S(1)} %get-tuple-element.63) | copy-start | bytes 4612
  25.2 31.1 %copy-start.55 = (f32[384]{0:T(512)}, f32[384]{0:T(512)S(1)}, u32[]{:S(2)}) copy-start(f32[384]{0:T(512)S(1)} %get-tuple-element.64) | copy-start | bytes 4612
  25.3 31.1 %copy-start.57 = (f32[384]{0:T(512)}, f32[384]{0:T(512)S(1)}, u32[]{:S(2)}) copy-start(f32[384]{0:T(512)S(1)} %get-tuple-element.65) | copy-start | bytes 4612
  25.3 31.1 %copy-start.59 = (f32[384]{0:T(512)}, f32[384]{0:T(512)S(1)}, u32[]{:S(2)}) copy-start(f32[384]{0:T(512)S(1)} %get-tuple-element.66) | copy-start | bytes 4612
  25.3 31.1 %copy-start.61 = (f32[384]{0:T(512)}, f32[384]{0:T(512)S(1)}, u32[]{:S(2)}) copy-start(f32[384]{0:T(512)S(1)} %get-tuple-element.67) | copy-start | bytes 4612
  26.0 11.1 %collective-permute-start.8 = (bf16[2,48,384]{2,1,0:T(8,128)(2,1)S(1)}, bf16[2,48,384]{2,1,0:T(8,128)(2,1)S(1)}, u32[]{:S(2)}, u32[]{:S(2)}) collective-permute-start(bf16[2,48,384]{2,1,0:T(8,128)(2,1)S(1)} %get-tuple-element.133), channel_id=1, source_target_pairs={{0,16},{1,17},{16,0},{17,1},{2,18},{3,19},{18,2},{19,3},{4,20},{5,... | collective-permute-start | bytes 221192 | tf_op jit(solution)/shard_map/ppermute | solution.py:18
  28.0 9.1 %collective-permute-start.7 = (bf16[2,48,384]{2,1,0:T(8,128)(2,1)S(1)}, bf16[2,48,384]{2,1,0:T(8,128)(2,1)S(1)}, u32[]{:S(2)}, u32[]{:S(2)}) collective-permute-start(bf16[2,48,384]{2,1,0:T(8,128)(2,1)S(1)} %get-tuple-element.133), channel_id=1, source_target_pairs={{0,1},{1,0},{16,17},{17,16},{2,3},{3,2},{18,19},{19,18},{4,5},{5,4... | collective-permute-start | bytes 221192 | tf_op jit(solution)/shard_map/ppermute | solution.py:18
  28.7 8.5 %collective-permute-start.9 = (bf16[2,48,384]{2,1,0:T(8,128)(2,1)S(1)}, bf16[2,48,384]{2,1,0:T(8,128)(2,1)S(1)}, u32[]{:S(2)}, u32[]{:S(2)}) collective-permute-start(bf16[2,48,384]{2,1,0:T(8,128)(2,1)S(1)} %get-tuple-element.133), channel_id=1, source_target_pairs={{0,17},{1,16},{16,1},{17,0},{2,19},{3,18},{18,3},{19,2},{4,21},{5,... | collective-permute-start | bytes 221192 | tf_op jit(solution)/shard_map/ppermute | solution.py:18
  30.3 11.0 %collective-permute-start.2 = (bf16[14,3,384]{2,1,0:T(4,128)(2,1)S(1)}, bf16[14,3,384]{2,1,0:T(4,128)(2,1)S(1)}, u32[]{:S(2)}, u32[]{:S(2)}) collective-permute-start(bf16[14,3,384]{2,1,0:T(4,128)(2,1)S(1)} %get-tuple-element.124), channel_id=1, source_target_pairs={{0,1},{1,2},{2,3},{3,4},{4,5},{5,6},{6,7},{8,9},{9,10},{10,11},{11... | collective-permute-start | bytes 96776 | tf_op jit(solution)/shard_map/ppermute | solution.py:28
  33.1 8.2 %collective-permute-start.3 = (bf16[14,3,384]{2,1,0:T(4,128)(2,1)S(1)}, bf16[14,3,384]{2,1,0:T(4,128)(2,1)S(1)}, u32[]{:S(2)}, u32[]{:S(2)}) collective-permute-start(bf16[14,3,384]{2,1,0:T(4,128)(2,1)S(1)} %get-tuple-element.125), channel_id=1, source_target_pairs={{1,0},{2,1},{3,2},{4,3},{5,4},{6,5},{7,6},{9,8},{10,9},{11,10},{12... | collective-permute-start | bytes 96776 | tf_op jit(solution)/shard_map/ppermute | solution.py:29
  37.2 10.0 %collective-permute-start.10 = (bf16[2,192,384]{2,1,0:T(8,128)(2,1)S(1)}, bf16[2,192,384]{2,1,0:T(8,128)(2,1)S(1)}, u32[]{:S(2)}, u32[]{:S(2)}) collective-permute-start(bf16[2,192,384]{2,1,0:T(8,128)(2,1)S(1)} %constant_dynamic-update-slice_fusion.7), channel_id=1, source_target_pairs={{0,2},{2,0},{4,6},{6,4},{1,3},{3,1},{5,7},{7,5},{8,10},{10,8},{12,... | collective-permute-start | bytes 884744 | tf_op jit(solution)/shard_map/ppermute | solution.py:18
  40.8 10.5 %collective-permute-start.11 = (bf16[2,192,384]{2,1,0:T(8,128)(2,1)S(1)}, bf16[2,192,384]{2,1,0:T(8,128)(2,1)S(1)}, u32[]{:S(2)}, u32[]{:S(2)}) collective-permute-start(bf16[2,192,384]{2,1,0:T(8,128)(2,1)S(1)} %constant_dynamic-update-slice_fusion.7), channel_id=1, source_target_pairs={{0,4},{2,6},{4,0},{6,2},{1,5},{3,7},{5,1},{7,3},{8,12},{10,14},{12... | collective-permute-start | bytes 884744 | tf_op jit(solution)/shard_map/ppermute | solution.py:18
  41.5 14.3 %collective-permute-start.12 = (bf16[2,192,384]{2,1,0:T(8,128)(2,1)S(1)}, bf16[2,192,384]{2,1,0:T(8,128)(2,1)S(1)}, u32[]{:S(2)}, u32[]{:S(2)}) collective-permute-start(bf16[2,192,384]{2,1,0:T(8,128)(2,1)S(1)} %constant_dynamic-update-slice_fusion.7), channel_id=1, source_target_pairs={{0,6},{2,4},{4,2},{6,0},{1,7},{3,5},{5,3},{7,1},{8,14},{10,12},{12... | collective-permute-start | bytes 884744 | tf_op jit(solution)/shard_map/ppermute | solution.py:18
  55.9 4.9 %collective-permute-start.13 = (bf16[2,768,384]{2,1,0:T(8,128)(2,1)S(1)}, bf16[2,768,384]{2,1,0:T(8,128)(2,1)S(1)}, u32[]{:S(2)}, u32[]{:S(2)}) collective-permute-start(bf16[2,768,384]{2,1,0:T(8,128)(2,1)S(1)} %constant_dynamic-update-slice_fusion.3), channel_id=1, source_target_pairs={{0,8},{8,0},{1,9},{9,1},{2,10},{10,2},{3,11},{11,3},{4,12},{12,4},... | collective-permute-start | bytes 3538952 | tf_op jit(solution)/shard_map/ppermute | solution.py:18
  71.0 6.0 %collective-permute-start.18 = (bf16[2,768,384]{2,1,0:T(8,128)(2,1)}, bf16[2,768,384]{2,1,0:T(8,128)(2,1)}, u32[]{:S(2)}, u32[]{:S(2)}) collective-permute-start(bf16[2,768,384]{2,1,0:T(8,128)(2,1)} %fusion.2), channel_id=1, source_target_pairs={{0,8},{8,0},{1,9},{9,1},{2,10},{10,2},{3,11},{11,3},{4,12},{12,4},... | collective-permute-start | bytes 3538952 | tf_op jit(solution)/shard_map/ppermute | solution.py:18
  76.8 7.7 %collective-permute-start.28 = (f32[57,384]{1,0:T(8,128)S(1)}, f32[57,384]{1,0:T(8,128)S(1)}, u32[]{:S(2)}, u32[]{:S(2)}) collective-permute-start(f32[57,384]{1,0:T(8,128)S(1)} %concatenate.35), channel_id=1, source_target_pairs={{0,8},{8,0},{1,9},{9,1},{2,10},{10,2},{3,11},{11,3},{4,12},{12,4},... | collective-permute-start | bytes 262664 | tf_op jit(solution)/shard_map/ppermute | solution.py:18
  80.3 33.1 %collective-permute-start.19 = (bf16[2,192,384]{2,1,0:T(8,128)(2,1)S(1)}, bf16[2,192,384]{2,1,0:T(8,128)(2,1)S(1)}, u32[]{:S(2)}, u32[]{:S(2)}) collective-permute-start(bf16[2,192,384]{2,1,0:T(8,128)(2,1)S(1)} %get-tuple-element.111), channel_id=1, source_target_pairs={{0,2},{2,0},{4,6},{6,4},{1,3},{3,1},{5,7},{7,5},{8,10},{10,8},{12,... | collective-permute-start | bytes 884744 | tf_op jit(solution)/shard_map/ppermute | solution.py:18
  80.5 32.9 %collective-permute-start.21 = (bf16[2,192,384]{2,1,0:T(8,128)(2,1)S(1)}, bf16[2,192,384]{2,1,0:T(8,128)(2,1)S(1)}, u32[]{:S(2)}, u32[]{:S(2)}) collective-permute-start(bf16[2,192,384]{2,1,0:T(8,128)(2,1)S(1)} %get-tuple-element.112), channel_id=1, source_target_pairs={{0,6},{2,4},{4,2},{6,0},{1,7},{3,5},{5,3},{7,1},{8,14},{10,12},{12... | collective-permute-start | bytes 884744 | tf_op jit(solution)/shard_map/ppermute | solution.py:18
  82.9 30.5 %collective-permute-start.20 = (bf16[2,192,384]{2,1,0:T(8,128)(2,1)S(1)}, bf16[2,192,384]{2,1,0:T(8,128)(2,1)S(1)}, u32[]{:S(2)}, u32[]{:S(2)}) collective-permute-start(bf16[2,192,384]{2,1,0:T(8,128)(2,1)S(1)} %get-tuple-element.113), channel_id=1, source_target_pairs={{0,4},{2,6},{4,0},{6,2},{1,5},{3,7},{5,1},{7,3},{8,12},{10,14},{12... | collective-permute-start | bytes 884744 | tf_op jit(solution)/shard_map/ppermute | solution.py:18
  84.5 13.7 %collective-permute-start.29 = (f32[57,384]{1,0:T(8,128)S(1)}, f32[57,384]{1,0:T(8,128)S(1)}, u32[]{:S(2)}, u32[]{:S(2)}) collective-permute-start(f32[57,384]{1,0:T(8,128)S(1)} %add.646), channel_id=1, source_target_pairs={{0,2},{2,0},{4,6},{6,4},{1,3},{3,1},{5,7},{7,5},{8,10},{10,8},{12,... | collective-permute-start | bytes 262664 | tf_op jit(solution)/shard_map/ppermute | solution.py:18
  98.3 6.2 %collective-permute-start.30 = (f32[57,384]{1,0:T(8,128)S(1)}, f32[57,384]{1,0:T(8,128)S(1)}, u32[]{:S(2)}, u32[]{:S(2)}) collective-permute-start(f32[57,384]{1,0:T(8,128)S(1)} %add.647), channel_id=1, source_target_pairs={{0,4},{2,6},{4,0},{6,2},{1,5},{3,7},{5,1},{7,3},{8,12},{10,14},{12... | collective-permute-start | bytes 262664 | tf_op jit(solution)/shard_map/ppermute | solution.py:18
  104.5 4.7 %collective-permute-start.31 = (f32[57,384]{1,0:T(8,128)S(1)}, f32[57,384]{1,0:T(8,128)S(1)}, u32[]{:S(2)}, u32[]{:S(2)}) collective-permute-start(f32[57,384]{1,0:T(8,128)S(1)} %add.648), channel_id=1, source_target_pairs={{0,1},{1,0},{16,17},{17,16},{2,3},{3,2},{18,19},{19,18},{4,5},{5,4... | collective-permute-start | bytes 262664 | tf_op jit(solution)/shard_map/ppermute | solution.py:18
  109.2 10.9 %collective-permute-start.32 = (f32[57,384]{1,0:T(8,128)S(1)}, f32[57,384]{1,0:T(8,128)S(1)}, u32[]{:S(2)}, u32[]{:S(2)}) collective-permute-start(f32[57,384]{1,0:T(8,128)S(1)} %add.649), channel_id=1, source_target_pairs={{0,16},{1,17},{16,0},{17,1},{2,18},{3,19},{18,2},{19,3},{4,20},{5,... | collective-permute-start | bytes 262664 | tf_op jit(solution)/shard_map/ppermute | solution.py:18
  114.7 6.8 %collective-permute-start.22 = (bf16[2,48,384]{2,1,0:T(8,128)(2,1)S(1)}, bf16[2,48,384]{2,1,0:T(8,128)(2,1)S(1)}, u32[]{:S(2)}, u32[]{:S(2)}) collective-permute-start(bf16[2,48,384]{2,1,0:T(8,128)(2,1)S(1)} %get-tuple-element.116), channel_id=1, source_target_pairs={{0,1},{1,0},{16,17},{17,16},{2,3},{3,2},{18,19},{19,18},{4,5},{5,4... | collective-permute-start | bytes 221192 | tf_op jit(solution)/shard_map/ppermute | solution.py:18
  114.8 13.5 %collective-permute-start.24 = (bf16[2,48,384]{2,1,0:T(8,128)(2,1)S(1)}, bf16[2,48,384]{2,1,0:T(8,128)(2,1)S(1)}, u32[]{:S(2)}, u32[]{:S(2)}) collective-permute-start(bf16[2,48,384]{2,1,0:T(8,128)(2,1)S(1)} %get-tuple-element.117), channel_id=1, source_target_pairs={{0,17},{1,16},{16,1},{17,0},{2,19},{3,18},{18,3},{19,2},{4,21},{5,... | collective-permute-start | bytes 221192 | tf_op jit(solution)/shard_map/ppermute | solution.py:18
  115.4 12.9 %collective-permute-start.23 = (bf16[2,48,384]{2,1,0:T(8,128)(2,1)S(1)}, bf16[2,48,384]{2,1,0:T(8,128)(2,1)S(1)}, u32[]{:S(2)}, u32[]{:S(2)}) collective-permute-start(bf16[2,48,384]{2,1,0:T(8,128)(2,1)S(1)} %get-tuple-element.118), channel_id=1, source_target_pairs={{0,16},{1,17},{16,0},{17,1},{2,18},{3,19},{18,2},{19,3},{4,20},{5,... | collective-permute-start | bytes 221192 | tf_op jit(solution)/shard_map/ppermute | solution.py:18
  118.9 10.0 %collective-permute-start.14 = (bf16[3,32,384]{2,1,0:T(8,128)(2,1)S(1)}, bf16[3,32,384]{2,1,0:T(8,128)(2,1)S(1)}, u32[]{:S(2)}, u32[]{:S(2)}) collective-permute-start(bf16[3,32,384]{2,1,0:T(8,128)(2,1)S(1)} %get-tuple-element.129), channel_id=1, source_target_pairs={{0,8},{8,16},{16,24},{24,32},{32,40},{40,48},{48,56},{56,64},{64,7... | collective-permute-start | bytes 221192 | tf_op jit(solution)/shard_map/ppermute | solution.py:28
  120.2 8.7 %collective-permute-start.15 = (bf16[3,32,384]{2,1,0:T(8,128)(2,1)S(1)}, bf16[3,32,384]{2,1,0:T(8,128)(2,1)S(1)}, u32[]{:S(2)}, u32[]{:S(2)}) collective-permute-start(bf16[3,32,384]{2,1,0:T(8,128)(2,1)S(1)} %get-tuple-element.130), channel_id=1, source_target_pairs={{8,0},{16,8},{24,16},{32,24},{40,32},{48,40},{56,48},{64,56},{72,6... | collective-permute-start | bytes 221192 | tf_op jit(solution)/shard_map/ppermute | solution.py:29
  121.5 14.2 %collective-permute-start.33 = (f32[57,384]{1,0:T(8,128)S(1)}, f32[57,384]{1,0:T(8,128)S(1)}, u32[]{:S(2)}, u32[]{:S(2)}) collective-permute-start(f32[57,384]{1,0:T(8,128)S(1)} %add.650), channel_id=1, source_target_pairs={{0,32},{32,0},{64,96},{96,64},{128,160},{160,128},{192,224},{224,1... | collective-permute-start | bytes 262664 | tf_op jit(solution)/shard_map/ppermute | solution.py:18
  128.8 9.8 %collective-permute-start.25 = (f32[2,24,384]{2,1,0:T(8,128)S(1)}, f32[2,24,384]{2,1,0:T(8,128)S(1)}, u32[]{:S(2)}, u32[]{:S(2)}) collective-permute-start(f32[2,24,384]{2,1,0:T(8,128)S(1)} %constant_dynamic-slice_fusion.2), channel_id=1, source_target_pairs={{0,32},{32,0},{64,96},{96,64},{128,160},{160,128},{192,224},{224,1... | collective-permute-start | bytes 221192 | tf_op jit(solution)/shard_map/ppermute | solution.py:18
  128.9 9.9 %collective-permute-start.16 = (bf16[14,3,384]{2,1,0:T(4,128)(2,1)S(1)}, bf16[14,3,384]{2,1,0:T(4,128)(2,1)S(1)}, u32[]{:S(2)}, u32[]{:S(2)}) collective-permute-start(bf16[14,3,384]{2,1,0:T(4,128)(2,1)S(1)} %get-tuple-element.122), channel_id=1, source_target_pairs={{0,1},{1,2},{2,3},{3,4},{4,5},{5,6},{6,7},{8,9},{9,10},{10,11},{11... | collective-permute-start | bytes 96776 | tf_op jit(solution)/shard_map/ppermute | solution.py:28
  130.9 7.9 %collective-permute-start.17 = (bf16[14,3,384]{2,1,0:T(4,128)(2,1)S(1)}, bf16[14,3,384]{2,1,0:T(4,128)(2,1)S(1)}, u32[]{:S(2)}, u32[]{:S(2)}) collective-permute-start(bf16[14,3,384]{2,1,0:T(4,128)(2,1)S(1)} %get-tuple-element.123), channel_id=1, source_target_pairs={{1,0},{2,1},{3,2},{4,3},{5,4},{6,5},{7,6},{9,8},{10,9},{11,10},{12... | collective-permute-start | bytes 96776 | tf_op jit(solution)/shard_map/ppermute | solution.py:29
  135.7 7.6 %collective-permute-start.34 = (f32[57,384]{1,0:T(8,128)S(1)}, f32[57,384]{1,0:T(8,128)S(1)}, u32[]{:S(2)}, u32[]{:S(2)}) collective-permute-start(f32[57,384]{1,0:T(8,128)S(1)} %add.651), channel_id=1, source_target_pairs={{0,64},{32,96},{64,0},{96,32},{128,192},{160,224},{192,128},{224,1... | collective-permute-start | bytes 262664 | tf_op jit(solution)/shard_map/ppermute | solution.py:18
  138.6 6.2 %collective-permute-start.26 = (f32[2,12,384]{2,1,0:T(8,128)S(1)}, f32[2,12,384]{2,1,0:T(8,128)S(1)}, u32[]{:S(2)}, u32[]{:S(2)}) collective-permute-start(f32[2,12,384]{2,1,0:T(8,128)S(1)} %constant_dynamic-slice_fusion.1), channel_id=1, source_target_pairs={{0,64},{32,96},{64,0},{96,32},{128,192},{160,224},{192,128},{224,1... | collective-permute-start | bytes 110600 | tf_op jit(solution)/shard_map/ppermute | solution.py:18
  143.4 10.7 %collective-permute-start.35 = (f32[57,384]{1,0:T(8,128)S(1)}, f32[57,384]{1,0:T(8,128)S(1)}, u32[]{:S(2)}, u32[]{:S(2)}) collective-permute-start(f32[57,384]{1,0:T(8,128)S(1)} %add.652), channel_id=1, source_target_pairs={{0,128},{32,160},{64,192},{96,224},{128,0},{160,32},{192,64},{224,... | collective-permute-start | bytes 262664 | tf_op jit(solution)/shard_map/ppermute | solution.py:18
  144.9 10.4 %collective-permute-start.27 = (f32[2,6,384]{2,1,0:T(8,128)S(1)}, f32[2,6,384]{2,1,0:T(8,128)S(1)}, u32[]{:S(2)}, u32[]{:S(2)}) collective-permute-start(f32[2,6,384]{2,1,0:T(8,128)S(1)} %constant_dynamic-slice_fusion), channel_id=1, source_target_pairs={{0,128},{32,160},{64,192},{96,224},{128,0},{160,32},{192,64},{224,... | collective-permute-start | bytes 55304 | tf_op jit(solution)/shard_map/ppermute | solution.py:18
  (67 other events, 1271.2 us)

commit v2 on v1

v2 whole, which is shorter than its diff:
```python
import functools
import math

import jax
import jax.numpy as jnp
from jax import lax
from jax.experimental import pallas as pl
from jax.experimental.pallas import tpu as pltpu
from jax.sharding import Mesh
from jax.sharding import PartitionSpec as P

ROW = ("z", "yh", "c")
COL = ("x", "yl")
Y = ("yh", "yl")
BF = jnp.bfloat16
F4 = jnp.float32


def swap(x, axis, flip):
    count = lax.axis_size(axis)
    return lax.ppermute(x, axis, [(i, i ^ flip) for i in range(count)])


def edge_sends(x, axis, dim, width=3):
    length = x.shape[dim]
    odd = (lax.axis_index(axis) & 1) != 0
    last = lax.slice_in_dim(x, length - width, length, axis=dim)
    first = lax.slice_in_dim(x, 0, width, axis=dim)
    return jnp.where(odd, first, last), jnp.where(odd, last, first)


def outer_swap(x, axis):
    peers = lax.axis_size(axis)
    return lax.ppermute(x, axis, [(i, ((i + 1) ^ 1) - 1) for i in range(1, peers - 1)])


def edge_order(inner, outer, axis):
    odd = (lax.axis_index(axis) & 1) != 0
    return jnp.where(odd, inner, outer), jnp.where(odd, outer, inner)


def edges(x, axis, dim):
    inner, outer = edge_sends(x, axis, dim)
    return edge_order(swap(inner, axis, 1), outer_swap(outer, axis), axis)


def between(x, sides, dim):
    return jnp.concatenate([sides[0], x, sides[1]], axis=dim)


def gelu_parts(hidden):
    normal_cdf = 0.5 * (1.0 + jax.scipy.special.erf(hidden * (1.0 / math.sqrt(2.0))))
    density = jnp.exp(-0.5 * hidden * hidden) * (1.0 / math.sqrt(2.0 * math.pi))
    return (hidden * normal_cdf, normal_cdf + hidden * density)


def pair_gather(x, axis, bit):
    mine = (lax.axis_index(axis) & bit) != 0
    other = swap(x, axis, bit)
    return jnp.concatenate([jnp.where(mine, other, x), jnp.where(mine, x, other)], axis=1)


def quad_select(x, axis, unit):
    me = (lax.axis_index(axis) // unit) % 4
    parts = [x] + [swap(x, axis, flip * unit) for flip in (1, 2, 3)]
    low, high = (me & 1) != 0, (me & 2) != 0
    pairs = [(parts[0], parts[1]), (parts[2], parts[3])]
    ordered = [(jnp.where(low, q, p), jnp.where(low, p, q)) for p, q in pairs]
    first, second = ordered
    low_half = [jnp.where(high, q, p) for p, q in zip(first, second)]
    high_half = [jnp.where(high, p, q) for p, q in zip(first, second)]
    return jnp.concatenate(low_half + high_half, axis=1)


def quad_gather(x, axis, extra=None):
    me = lax.axis_index(axis)
    rows, channels = x.shape[1:]
    others = []
    for flip in (1, 2, 3):
        if flip == 1 and extra is not None:
            got = swap(jnp.concatenate([x.reshape(2 * rows, channels), extra], 0), axis, flip)
            others.append(got[: 2 * rows].reshape(x.shape))
            extra = got[2 * rows :]
        else:
            others.append(swap(x, axis, flip))
    full = jnp.zeros((x.shape[0], 4 * rows, channels), x.dtype)
    for flip, piece in zip((0, 1, 2, 3), [x] + others):
        full = lax.dynamic_update_slice_in_dim(full, piece, (me ^ flip) * rows, axis=1)
    return full if extra is None else (full, extra)


def local_call(kernel, index, outs, *arrays, scratch=(), flops=1_000_000):
    moved = sum(math.prod(a.shape) * a.dtype.itemsize for a in list(arrays) + list(outs))
    return pl.pallas_call(
        kernel,
        out_shape=outs,
        in_specs=[pl.BlockSpec(memory_space=pltpu.SMEM)]
        + [pl.BlockSpec(memory_space=pltpu.VMEM)] * len(arrays),
        out_specs=[pl.BlockSpec(memory_space=pltpu.VMEM)] * len(outs),
        scratch_shapes=list(scratch),
        cost_estimate=pl.CostEstimate(flops=flops, bytes_accessed=moved, transcendentals=0),
        compiler_params=pltpu.CompilerParams(vmem_limit_bytes=32 * 2**20),
    )(index, *arrays)


def shape(*dims, dtype=F4):
    return jax.ShapeDtypeStruct(dims, dtype)


SMALL = 64


def norm_back(
    index, normed_grad, mixed, back, conv, gain, padded, cot, feature, scale, b_out, bias,
    low, message, outer, block_out, grads, wide, sums,
):
    rows, cols, channels = low.shape
    pixels = rows * cols

    def flat(x):
        return x.reshape(pixels, channels)

    taken = flat(conv[...])
    centered = taken - jnp.mean(taken, -1, keepdims=True)
    inv_std = lax.rsqrt(jnp.mean(centered * centered, -1, keepdims=True) + 1e-06)
    unit = centered * inv_std
    grad = normed_grad[0:pixels, :] + back[1].astype(F4)
    scaled = grad * gain[...]
    grad_conv = inv_std * (
        scaled
        - jnp.mean(scaled, -1, keepdims=True)
        - unit * jnp.mean(scaled * unit, -1, keepdims=True)
    )
    grads[...] = grad_conv.reshape(rows, cols, channels)
    low[...] = grad_conv.reshape(rows, cols, channels).astype(BF)
    sums[...] = jnp.zeros_like(sums)
    sums[49:50, :] = jnp.sum(grad * unit, 0, keepdims=True)
    sums[50:51, :] = jnp.sum(grad, 0, keepdims=True)
    full = mixed[0:pixels, :] + back[0].astype(F4) + b_out[...]
    flow = flat(cot[...].astype(F4))
    sums[51:52, :] = jnp.sum(flow * scale[...], 0, keepdims=True)
    sums[52:53, :] = jnp.sum(flow * full, 0, keepdims=True)
    sums[53:57, :] = bias[...]
    block_out[...] = (
        (flat(feature[...].astype(F4)) + scale[...] * full).astype(BF).reshape(rows, cols, channels)
    )
    for r in range(rows + 6):
        wide[r, 0 : cols + 6, :] = padded[r].astype(F4)
    for j in range(7):
        total = [jnp.zeros((8, channels), F4) for _ in range(7)]
        for r in range(rows + 6):
            slab = wide[r, j : j + cols, :]
            for p in range(max(0, r - 6), min(rows, r + 1)):
                term = slab * grads[p]
                term = tree([term[8 * k : 8 * k + 8] for k in range(cols // 8)])
                total[r - p] = total[r - p] + term
        for i in range(7):
            sums[7 * i + j : 7 * i + j + 1, :] = jnp.sum(total[i], 0, keepdims=True)
    message[0:SMALL, :] = sums[...].astype(BF)
    odd = index[0] != 0
    first, last = grads[0:3], grads[rows - 3 : rows]
    message[SMALL : SMALL + 3 * cols, :] = (
        jnp.where(odd, first, last).astype(BF).reshape(3 * cols, channels)
    )
    outer[...] = jnp.where(odd, last, first).astype(BF)


def first_fan(index, win, wout, mine, theirs, one, two, three, shared):
    rows = win.shape[0] // 4
    shared[...] = (mine[0:SMALL, :].astype(F4) + theirs[0:SMALL, :].astype(F4)).astype(BF)
    for flip, message in ((1, one), (2, two), (3, three)):
        at = pl.multiple_of((index[1] ^ flip) * rows, rows)
        message[0:rows, :] = win[pl.ds(at, rows), :].astype(BF)
        message[rows : 2 * rows, :] = wout[pl.ds(at, rows), :].astype(BF)
        message[2 * rows :, :] = shared[...]


def second_fan(index, win, wout, mine, g1, g2, g3, total, one, two, three, shared):
    rows = win.shape[0] // 4
    at = pl.multiple_of(index[1] * rows, rows)
    for k, term in enumerate((win, wout)):
        own = term[pl.ds(at, rows), :]
        got = [g[k * rows : (k + 1) * rows, :].astype(F4) for g in (g1, g2, g3)]
        total[k] = tree([own] + got)
    small = tree([mine[...].astype(F4)] + [g[2 * rows :, :].astype(F4) for g in (g1, g2, g3)])
    shared[...] = small.astype(BF)
    part = rows // 4
    for flip, message in ((1, one), (2, two), (3, three)):
        at = pl.multiple_of((index[2] ^ flip) * part, part)
        for k in range(2):
            message[k * part : (k + 1) * part, :] = total[k, pl.ds(at, part), :].astype(BF)
        message[2 * part :, :] = shared[...]


def up16(n):
    return -(-n // 16) * 16


def send_half(total, k, bit, message):
    half = total.shape[1] // 2
    block = up16(half)
    value = jnp.where(bit, total[k, 0:half, :], total[k, half : 2 * half, :])
    message[k * block : k * block + half, :] = value.astype(BF)


def third_fan(index, before, mine, g1, g2, g3, total, message, shared):
    rows = before.shape[1] // 4
    at = pl.multiple_of(index[2] * rows, rows)
    for k in range(2):
        got = [g[k * rows : (k + 1) * rows, :].astype(F4) for g in (g1, g2, g3)]
        total[k] = tree([before[k, pl.ds(at, rows), :]] + got)
    small = tree([mine[...].astype(F4)] + [g[2 * rows :, :].astype(F4) for g in (g1, g2, g3)])
    shared[...] = small.astype(BF)
    held = message.shape[0] - SMALL
    for k in range(2):
        send_half(total, k, index[3] != 0, message)
    message[held:, :] = shared[...]


def pair_step(here, after, index, before, mine, got, total, message, shared):
    half = before.shape[1] // 2
    block = up16(half)
    bit = index[here] != 0
    for k in range(2):
        own = jnp.where(bit, before[k, half : 2 * half, :], before[k, 0:half, :])
        total[k] = own + got[k * block : k * block + half, :].astype(F4)
    shared[...] = (mine[...].astype(F4) + got[2 * block :, :].astype(F4)).astype(BF)
    for k in range(2):
        send_half(total, k, index[after] != 0, message)
    message[message.shape[0] - SMALL :, :] = shared[...]


def pair_end(here, index, before, mine, got, win, wout, small, bias):
    half = before.shape[1] // 2
    block = up16(half)
    bit = index[here] != 0
    for k, out in ((0, win), (1, wout)):
        own = jnp.where(bit, before[k, half : 2 * half, :], before[k, 0:half, :])
        out[...] = own + got[k * block : k * block + half, :].astype(F4)
    total = mine[...].astype(F4) + got[2 * block :, :].astype(F4)
    small[...] = total[0:53, :]
    bias[...] = total[53:57, :]


def tree(parts):
    while len(parts) > 1:
        parts = [p + q for p, q in zip(parts[::2], parts[1::2])]
    return parts[0]


def on_device(
    feature_map, kernel, ln_gain, ln_bias, w_in, b_in, w_out, b_out, layer_scale, cotangent
):
    row_count, col_count, channels = feature_map.shape
    pixels = row_count * col_count
    hidden_count = b_in.shape[0]
    contract_last = (((1,), (1,)), ((), ()))
    contract_first = (((0,), (0,)), ((), ()))

    weights = jnp.stack([w_in.T, w_out], 0)
    weights = quad_select(weights, "z", 2)
    weights = pair_gather(weights, "z", 1)
    rows = edges(feature_map, ROW, 0)
    weights, feature_map, cotangent, rows = lax.optimization_barrier(
        (weights, feature_map, cotangent, rows)
    )
    tall = between(feature_map, rows, 0)
    inner, outer = edge_sends(tall, COL, 1)
    outer_got = outer_swap(outer, COL)
    weights, inner_got = quad_gather(weights, Y, inner.reshape(-1, channels))
    columns = edge_order(inner_got.reshape(inner.shape), outer_got, COL)
    weights, tall, columns, cotangent, kernel = lax.optimization_barrier(
        (weights, tall, columns, cotangent, kernel)
    )
    weights = quad_gather(weights, "x")
    w_in_t, w_out_mine = weights[0], weights[1]
    core = lax.axis_index("c")
    half = hidden_count // 2
    z = lax.axis_index("z")
    units = hidden_count // 256
    b_order = (
        b_in.reshape(2, 2, 2, 2, 2, 4, 2, units).transpose(4, 5, 3, 6, 2, 0, 1, 7).reshape(hidden_count)
    )
    b_mine = lax.dynamic_slice_in_dim(b_order, core * half, half)
    grad_flow = cotangent.astype(F4).reshape(pixels, channels)
    grad_mixed = grad_flow * layer_scale

    padded_low = between(tall, columns, 1)
    padded = padded_low.astype(F4)
    conv = jnp.zeros((row_count, col_count, channels), F4)
    for tap_row in range(7):
        for tap_col in range(7):
            conv = (
                conv
                + padded[tap_row : tap_row + row_count, tap_col : tap_col + col_count]
                * kernel[tap_row, tap_col]
            )
    average = jnp.mean(conv, -1, keepdims=True)
    centered = conv - average
    variance = jnp.mean(centered * centered, -1, keepdims=True)
    inv_std = lax.rsqrt(variance + 1e-06)
    unit_scaled = centered * inv_std
    normed = (unit_scaled * ln_gain + ln_bias).astype(BF).reshape(pixels, channels)
    ours = jnp.stack([normed, grad_mixed.astype(BF)], 0)
    theirs = swap(ours, "c", 1)
    normed_two = jnp.concatenate([ours[0], theirs[0]], 0)
    mixed_low = jnp.concatenate([ours[1], theirs[1]], 0)
    hidden = lax.dot_general(normed_two, w_in_t, contract_last, preferred_element_type=F4) + b_mine
    act_value, slope = gelu_parts(hidden)
    activated = act_value.astype(BF)
    grad_act = lax.dot_general(mixed_low, w_out_mine, contract_last, preferred_element_type=F4)
    grad_hidden = (grad_act * slope).astype(BF)
    grad_normed = jnp.dot(grad_hidden, w_in_t, preferred_element_type=F4)
    mixed = jnp.dot(activated, w_out_mine, preferred_element_type=F4)
    back = swap(jnp.stack([mixed[pixels:], grad_normed[pixels:]], 0).astype(BF), "c", 1)
    wout_term = lax.dot_general(activated, mixed_low, contract_first, preferred_element_type=F4)
    win_term = lax.dot_general(grad_hidden, normed_two, contract_first, preferred_element_type=F4)

    bias_mine = jnp.sum(grad_hidden.astype(F4), 0)
    bias_local = jnp.where(jnp.arange(2)[:, None] == core, bias_mine, 0.0)
    bias_local = (
        bias_local.reshape(2, 4, 2, 2, 2, 2, 2, units)
        .transpose(5, 6, 4, 2, 0, 1, 3, 7)
        .reshape(hidden_count // channels, channels)
    )
    index = jnp.stack(
        [core, lax.axis_index("x"), lax.axis_index(Y), z & 1, (z // 4) & 1, (z // 2) & 1]
    ).astype(jnp.int32)
    grad_low, mine, outer, block_out = local_call(
        norm_back,
        index,
        [
            shape(row_count, col_count, channels, dtype=BF),
            shape(SMALL + 3 * col_count, channels, dtype=BF),
            shape(3, col_count, channels, dtype=BF),
            shape(row_count, col_count, channels, dtype=BF),
        ],
        grad_normed, mixed, back, conv, ln_gain[None], padded_low, cotangent, feature_map,
        layer_scale[None], b_out[None], bias_local,
        scratch=[
            pltpu.VMEM((row_count, col_count, channels), F4),
            pltpu.VMEM((row_count + 6, col_count + 8, channels), F4),
            pltpu.VMEM((SMALL, channels), F4),
        ],
        flops=110 * pixels * channels,
    )
    theirs = swap(mine, "c", 1)
    outer_got = outer_swap(outer, ROW)
    rows = edge_order(theirs[SMALL:].reshape(3, col_count, channels), outer_got, ROW)
    low_tall = between(grad_low, rows, 0)

    small_shape = shape(SMALL, channels, dtype=BF)

    def message_of(rows, block=None):
        return shape(2 * (block or rows) + SMALL, channels, dtype=BF)

    def fan(messages, axis):
        return [swap(m, axis, flip) for m, flip in zip(messages, (1, 2, 3))]

    piece = half // 4
    *messages, shared = local_call(
        first_fan, index, [message_of(piece)] * 3 + [small_shape], win_term, wout_term, mine, theirs
    )
    got = fan(messages, "x")
    got, low_tall = lax.optimization_barrier((got, low_tall))
    total, *messages, shared = local_call(
        second_fan,
        index,
        [shape(2, piece, channels)] + [message_of(piece // 4)] * 3 + [small_shape],
        win_term, wout_term, shared, *got,
    )
    piece = piece // 4
    got = fan(messages, Y)
    columns = edges(low_tall, COL, 1)
    grad_pad = between(low_tall, columns, 1).astype(F4)
    total, message, shared = local_call(
        third_fan,
        index,
        [shape(2, piece, channels), message_of(up16(piece // 2)), small_shape],
        total, shared, *got,
    )
    for here, after, unit in ((3, 4, 1), (4, 5, 4)):
        piece = piece // 2
        got = swap(message, "z", unit)
        total, message, shared = local_call(
            functools.partial(pair_step, here, after),
            index,
            [shape(2, piece, channels), message_of(up16(piece // 2)), small_shape],
            total, shared, got,
        )
    got = swap(message, "z", 2)
    win_t, grad_w_out, small_grads, bias_rows = local_call(
        functools.partial(pair_end, 5),
        index,
        [shape(units, channels), shape(units, channels), shape(53, channels), shape(4, channels)],
        total, shared, got,
    )
    back_conv = jnp.zeros((row_count, col_count, channels), F4)
    for tap_row in range(7):
        for tap_col in range(7):
            back_conv = (
                back_conv
                + grad_pad[
                    6 - tap_row : 6 - tap_row + row_count, 6 - tap_col : 6 - tap_col + col_count
                ]
                * kernel[tap_row, tap_col]
            )
    grad_input = (cotangent.astype(F4) + back_conv).astype(BF)
    grad_b_in = bias_rows.reshape(hidden_count)
    return (block_out, grad_input, win_t.T, grad_w_out, small_grads, grad_b_in)


def solution(mesh):
    fine = Mesh(mesh.devices.reshape(8, 2, 2, 4, 2), ("z", "yh", "c", "x", "yl"))
    every = ROW + COL
    placed = (
        P(ROW, COL, None),
        P(),
        P(),
        P(),
        P(None, every),
        P(),
        P(every, None),
        P(),
        P(),
        P(ROW, COL, None),
    )
    return jax.shard_map(
        on_device,
        mesh=fine,
        in_specs=placed,
        out_specs=(
            P(ROW, COL, None),
            P(ROW, COL, None),
            P(None, every),
            P(every, None),
            P(),
            P(),
        ),
        check_vma=False,
    )
```

time: 158 us -> 125 us (0.79)
  starting transfers between devices: 75.7 us -> 51.1 us
  Pallas kernels: 0 us -> 8.15 us
  other arithmetic: 19.2 us -> 13 us
  local copies, waits for them, and re-layouts: 12.4 us -> 7.17 us
  matrix products: 8.12 us -> 5.05 us
    ppermute x8 -> x4, starting transfers between devices: 20.4 us -> 7.28 us  [outer_swap(): lax.ppermute(x, axis, [(i, (i + 1 ^ 1) - 1) for i in range(1, peers - 1)])]
    ppermute x28 -> x24, starting transfers between devices: 55.3 us -> 43.8 us  [swap(): return lax.ppermute(x, axis, [(i, i ^ flip) for i in range(count)])]
    pallas_call x0 -> x7, Pallas kernels: none -> 8.15 us  [local_call(): pl.pallas_call(kernel, out_shape=outs, in_specs=[pl.BlockSpec(memory_spac...]
    reduce_sum x4 -> x0, other arithmetic: 4.29 us -> none  [the longest x3 3.29 us: on_device(): jnp.sum(padded[tap_row:tap_row + row_count, tap_col:tap_col + col_count]...]
    add x14 -> x0, other arithmetic: 3.26 us -> none  [the longest x6 3.15 us: fan_reduce(): total = total + g.astype(F4)]
    slice x3, local copies, waits for them, and re-layouts: 3.99 us -> 0.86 us  [on_device(): kernel[tap_row, tap_col]]
    broadcast_in_dim x6 -> x11, local copies, waits for them, and re-layouts: 0.66 us -> 3.41 us  [the longest x6 1.23 us: on_device(): bias_local = jnp.where(jnp.arange(2)[:, None] == core, bias_mine, 0.0)]
    select_n x1 -> x9, other arithmetic: 0.22 us -> 2.57 us  [the longest x3 1.05 us: edge_sends(): return (jnp.where(odd, first, last), jnp.where(odd, last, first))]
  transfers between devices with their start and end apart: 36 -> 28, of which waited for: 9 -> 12; matrix products, arithmetic and copies ran while one was open for 17% -> 16% of each run, Pallas kernels for 0% -> 1%
where the time goes in v2:
time: 125 us; the launch traced here: 124 us
  starting transfers between devices  51.1 us (41%)
  waiting for transfers between devices  37.3 us (30%)
  other arithmetic  13 us (10%)
  Pallas kernels  8.15 us (7%)
  local copies, waits for them, and re-layouts  7.17 us (6%)
  matrix products  5.05 us (4%)
  between operations  2.48 us (2%)
    ppermute x24, starting transfers between devices, swap(): return lax.ppermute(x, axis, [(i, i ^ flip) for i in range(count)])  43.8 us
    ppermute x24, waiting for transfers between devices, swap(): return lax.ppermute(x, axis, [(i, i ^ flip) for i in range(count)])  35.6 us
    pallas_call x7, Pallas kernels, local_call(): pl.pallas_call(kernel, out_shape=outs, in_specs=[pl.BlockSpec(memory_spac...  8.15 us
    ppermute x4, starting transfers between devices, outer_swap(): lax.ppermute(x, axis, [(i, (i + 1 ^ 1) - 1) for i in range(1, peers - 1)])  7.28 us
    convert_element_type x1, other arithmetic, on_device(): grad_input = (cotangent.astype(F4) + back_conv).astype(BF)  4.18 us
    reduce_sum x1, other arithmetic, on_device(): average = jnp.mean(conv, -1, keepdims=True)  3.83 us
  transfers between devices with their start and end apart: 28, of which 12 were waited for; matrix products, arithmetic and copies ran while one was open for 16% of the time, Pallas kernels for 1%

profile of v2, /device:TPU:6, one launch (start us, length us, event | category | flops | bytes accessed | tf_op | source)
XLA Modules:
  0.0 124.3 jit_solution(1632437381858361296)
XLA Ops:
  0.6 0.8 pad_maximum_fusion.13
  1.4 6.4 %collective-permute-start = (bf16[2,6,384]{2,1,0:T(8,128)(2,1)S(1)}, bf16[2,6,384]{2,1,0:T(8,128)(2,1)S(1)}, u32[]{:S(2)}, u32[]{:S(2)}) collective-permute-start(bf16[2,6,384]{2,1,0:T(8,128)(2,1)S(1)} %pad_maximum_fusion.13), channel_id=1, source_target_pairs={{0,192},{32,224},{64,128},{96,160},{128,64},{160,96},{192,0},{224,... | collective-permute-start | bytes 27656 | tf_op jit(solution)/shard_map/ppermute | solution.py:21
  7.8 1.0 collective-permute-start.1
  8.8 1.5 %collective-permute-start.2 = (bf16[2,6,384]{2,1,0:T(8,128)(2,1)S(1)}, bf16[2,6,384]{2,1,0:T(8,128)(2,1)S(1)}, u32[]{:S(2)}, u32[]{:S(2)}) collective-permute-start(bf16[2,6,384]{2,1,0:T(8,128)(2,1)S(1)} %pad_maximum_fusion.13), channel_id=1, source_target_pairs={{0,64},{32,96},{64,0},{96,32},{128,192},{160,224},{192,128},{224,1... | collective-permute-start | bytes 27656 | tf_op jit(solution)/shard_map/ppermute | solution.py:21
  10.2 0.9 broadcast_select_fusion.4
  11.2 0.7 collective-permute-start.5
  11.8 4.6 %collective-permute-start.4 = (bf16[3,32,384]{2,1,0:T(8,128)(2,1)S(1)}, bf16[3,32,384]{2,1,0:T(8,128)(2,1)S(1)}, u32[]{:S(2)}, u32[]{:S(2)}) collective-permute-start(bf16[3,32,384]{2,1,0:T(8,128)(2,1)S(1)} %get-tuple-element.148), channel_id=1, source_target_pairs={{0,8},{8,0},{16,24},{24,16},{32,40},{40,32},{48,56},{56,48},{64,72... | collective-permute-start | bytes 221192 | tf_op jit(solution)/shard_map/ppermute | solution.py:21
  16.5 0.7 broadcast_select_fusion.23
  17.3 1.1 collective-permute-start.3
  18.4 0.9 reshape.114
  19.6 0.7 broadcast_in_dim.50.gain
  20.3 0.7 broadcast_in_dim.51.scale
  21.0 0.7 broadcast_in_dim.52.b_out
  21.8 0.7 broadcast_in_dim.54
  22.8 2.2 %collective-permute-start.7 = (bf16[2,48,384]{2,1,0:T(8,128)(2,1)S(1)}, bf16[2,48,384]{2,1,0:T(8,128)(2,1)S(1)}, u32[]{:S(2)}, u32[]{:S(2)}) collective-permute-start(bf16[2,48,384]{2,1,0:T(8,128)(2,1)S(1)} %pad_maximum_fusion.11), channel_id=1, source_target_pairs={{0,16},{1,17},{16,0},{17,1},{2,18},{3,19},{18,2},{19,3},{4,20},{5,... | collective-permute-start | bytes 221192 | tf_op jit(solution)/shard_map/ppermute | solution.py:21
  24.9 1.3 %collective-permute-start.8 = (bf16[2,48,384]{2,1,0:T(8,128)(2,1)S(1)}, bf16[2,48,384]{2,1,0:T(8,128)(2,1)S(1)}, u32[]{:S(2)}, u32[]{:S(2)}) collective-permute-start(bf16[2,48,384]{2,1,0:T(8,128)(2,1)S(1)} %pad_maximum_fusion.11), channel_id=1, source_target_pairs={{0,17},{1,16},{16,1},{17,0},{2,19},{3,18},{18,3},{19,2},{4,21},{5,... | collective-permute-start | bytes 221192 | tf_op jit(solution)/shard_map/ppermute | solution.py:21
  26.4 0.2 collective-permute-start.6
  26.6 4.0 %collective-permute-start.9 = (bf16[14,3,384]{2,1,0:T(4,128)(2,1)S(1)}, bf16[14,3,384]{2,1,0:T(4,128)(2,1)S(1)}, u32[]{:S(2)}, u32[]{:S(2)}) collective-permute-start(bf16[14,3,384]{2,1,0:T(4,128)(2,1)S(1)} %get-tuple-element.145), channel_id=1, source_target_pairs={{1,2},{2,1},{3,4},{4,3},{5,6},{6,5},{9,10},{10,9},{11,12},{12,11},... | collective-permute-start | bytes 96776 | tf_op jit(solution)/shard_map/ppermute | solution.py:34
  30.8 0.9 collective-permute-done.6
  31.8 1.7 %collective-permute-done.9 = bf16[14,3,384]{2,1,0:T(4,128)(2,1)S(1)} collective-permute-done((bf16[14,3,384]{2,1,0:T(4,128)(2,1)S(1)}, bf16[14,3,384]{2,1,0:T(4,128)(2,1)S(1)}, u32[]{:S(2)}, u32[]{:S(2)}) %collective-permute-start.9) | collective-permute-done | bytes 32288 | tf_op jit(solution)/shard_map/ppermute | solution.py:34
  33.6 0.9 collective-permute-start.11
  34.5 0.7 collective-permute-start.12
  35.2 3.2 %collective-permute-start.13 = (bf16[2,192,384]{2,1,0:T(8,128)(2,1)S(1)}, bf16[2,192,384]{2,1,0:T(8,128)(2,1)S(1)}, u32[]{:S(2)}, u32[]{:S(2)}) collective-permute-start(bf16[2,192,384]{2,1,0:T(8,128)(2,1)S(1)} %constant_dynamic-update-slice_fusion.7), channel_id=1, source_target_pairs={{0,6},{2,4},{4,2},{6,0},{1,7},{3,5},{5,3},{7,1},{8,14},{10,12},{12... | collective-permute-start | bytes 884744 | tf_op jit(solution)/shard_map/ppermute | solution.py:21
  38.9 0.7 slice_reduce_fusion.46
  39.9 3.8 %fusion.117 = (f32[8,32]{1,0:T(8,128)S(1)}, f32[8,32,384]{2,1,0:T(8,128)S(1)}) fusion(f32[384]{0:T(512)S(1)} %get-tuple-element.89, f32[14,38,384]{2,1,0:T(8,128)S(1)} %get-tuple-element.140, f32[384]{0:T(512)S(1)} %get-tuple-element.90, f32[384]{0:T(512)S(1)} %get-tuple-element.91, f32[384]{0:T(512)S(1)} %get-tuple-element.92, ...), kind=kLoop, calls=%fused_computation.329 | loop fusion | flops 9633536 | bytes 19737088 | tf_op jit(solution)/shard_map/reduce_sum | solution.py:298
  44.6 0.3 collective-permute-start.10
  45.1 1.6 %collective-permute-done.12 = bf16[2,192,384]{2,1,0:T(8,128)(2,1)S(1)} collective-permute-done((bf16[2,192,384]{2,1,0:T(8,128)(2,1)S(1)}, bf16[2,192,384]{2,1,0:T(8,128)(2,1)S(1)}, u32[]{:S(2)}, u32[]{:S(2)}) %collective-permute-start.12) | collective-permute-done | bytes 294944 | tf_op jit(solution)/shard_map/ppermute | solution.py:21
  46.8 2.6 %collective-permute-done.13 = bf16[2,192,384]{2,1,0:T(8,128)(2,1)S(1)} collective-permute-done((bf16[2,192,384]{2,1,0:T(8,128)(2,1)S(1)}, bf16[2,192,384]{2,1,0:T(8,128)(2,1)S(1)}, u32[]{:S(2)}, u32[]{:S(2)}) %collective-permute-start.13) | collective-permute-done | bytes 294944 | tf_op jit(solution)/shard_map/ppermute | solution.py:21
  49.6 0.7 multiply_convert_fusion
  50.3 0.9 convert_reduce_fusion
  51.1 0.6 fusion.7.normed_grad
  51.7 0.6 fusion.6.mixed
  52.4 0.8 pad_maximum_fusion.4
  53.6 0.7 broadcast_select_fusion.24.bias
  54.3 1.8 %fusion.108.win = f32[768,384]{1,0:T(8,128)S(1)} fusion(bf16[512,768]{1,0:T(8,128)(2,1)} %copy-done.4, bf16[256,384]{1,0:T(8,128)(2,1)} %copy-done.9, bf16[256,384]{1,0:T(8,128)(2,1)S(1)} %bitcast.53), kind=kOutput, calls=%fused_computation.226 | convolution fusion | flops 302776320 | bytes 2359296 | tf_op jit(solution)/shard_map/dot_general | solution.py:317
  56.1 3.7 %shard_map.145 = (bf16[8,32,384]{2,1,0:T(8,128)(2,1)S(1)}, bf16[160,384]{1,0:T(8,128)(2,1)S(1)}, bf16[3,32,384]{2,1,0:T(8,128)(2,1)S(1)}, bf16[8,32,384]{2,1,0:T(8,128)(2,1)}) custom-call(s32[6]{0:T(128)S(1)} %stack.52.index, f32[512,384]{1,0:T(8,128)S(1)} %fusion.7.normed_grad, f32[512,384]{1,0:T(8,128)S(1)} %fusion.6.mixed, ...), custom_call_target="tpu_custom_call" | custom-call | flops 10813440 | bytes 3761664 | tf_op jit(solution)/shard_map/pallas_call | solution.py:94
  59.8 0.6 collective-permute-start.15
  60.4 0.7 collective-permute-start.19
  61.1 0.6 fusion.109.wout
  61.7 0.7 shard_map.146
  62.5 4.4 %collective-permute-start.17 = (bf16[448,384]{1,0:T(8,128)(2,1)S(1)}, bf16[448,384]{1,0:T(8,128)(2,1)S(1)}, u32[]{:S(2)}, u32[]{:S(2)}) collective-permute-start(bf16[448,384]{1,0:T(8,128)(2,1)S(1)} %get-tuple-element.61), channel_id=1, source_target_pairs={{0,4},{2,6},{4,0},{6,2},{1,5},{3,7},{5,1},{7,3},{8,12},{10,14},{12... | collective-permute-start | bytes 1032200 | tf_op jit(solution)/shard_map/ppermute | solution.py:21
  66.9 0.3 collective-permute-start.18
  67.3 4.0 %collective-permute-done.16.g1 = bf16[448,384]{1,0:T(8,128)(2,1)S(1)} collective-permute-done((bf16[448,384]{1,0:T(8,128)(2,1)S(1)}, bf16[448,384]{1,0:T(8,128)(2,1)S(1)}, u32[]{:S(2)}, u32[]{:S(2)}) %collective-permute-start.16) | collective-permute-done | bytes 344096 | tf_op jit(solution)/shard_map/ppermute | solution.py:21
  71.3 9.8 %collective-permute-done.17.g2 = bf16[448,384]{1,0:T(8,128)(2,1)S(1)} collective-permute-done((bf16[448,384]{1,0:T(8,128)(2,1)S(1)}, bf16[448,384]{1,0:T(8,128)(2,1)S(1)}, u32[]{:S(2)}, u32[]{:S(2)}) %collective-permute-start.17) | collective-permute-done | bytes 344096 | tf_op jit(solution)/shard_map/ppermute | solution.py:21
  81.1 3.7 %collective-permute-done.18.g3 = bf16[448,384]{1,0:T(8,128)(2,1)S(1)} collective-permute-done((bf16[448,384]{1,0:T(8,128)(2,1)S(1)}, bf16[448,384]{1,0:T(8,128)(2,1)S(1)}, u32[]{:S(2)}, u32[]{:S(2)}) %collective-permute-start.18) | collective-permute-done | bytes 344096 | tf_op jit(solution)/shard_map/ppermute | solution.py:21
  84.8 0.8 shard_map.147
  85.6 2.2 %collective-permute-start.22 = (bf16[160,384]{1,0:T(8,128)(2,1)S(1)}, bf16[160,384]{1,0:T(8,128)(2,1)S(1)}, u32[]{:S(2)}, u32[]{:S(2)}) collective-permute-start(bf16[160,384]{1,0:T(8,128)(2,1)S(1)} %get-tuple-element.72), channel_id=1, source_target_pairs={{0,1},{1,0},{16,17},{17,16},{2,3},{3,2},{18,19},{19,18},{4,5},{5,4... | collective-permute-start | bytes 368648 | tf_op jit(solution)/shard_map/ppermute | solution.py:21
  87.8 4.7 %collective-permute-start.23 = (bf16[160,384]{1,0:T(8,128)(2,1)S(1)}, bf16[160,384]{1,0:T(8,128)(2,1)S(1)}, u32[]{:S(2)}, u32[]{:S(2)}) collective-permute-start(bf16[160,384]{1,0:T(8,128)(2,1)S(1)} %get-tuple-element.73), channel_id=1, source_target_pairs={{0,16},{1,17},{16,0},{17,1},{2,18},{3,19},{18,2},{19,3},{4,20},{5,... | collective-permute-start | bytes 368648 | tf_op jit(solution)/shard_map/ppermute | solution.py:21
  92.8 0.3 collective-permute-start.24
  93.3 1.9 %collective-permute-start.21 = (bf16[14,3,384]{2,1,0:T(4,128)(2,1)S(1)}, bf16[14,3,384]{2,1,0:T(4,128)(2,1)S(1)}, u32[]{:S(2)}, u32[]{:S(2)}) collective-permute-start(bf16[14,3,384]{2,1,0:T(4,128)(2,1)S(1)} %get-tuple-element.144), channel_id=1, source_target_pairs={{1,2},{2,1},{3,4},{4,3},{5,6},{6,5},{9,10},{10,9},{11,12},{12,11},... | collective-permute-start | bytes 96776 | tf_op jit(solution)/shard_map/ppermute | solution.py:34
  95.2 3.1 %collective-permute-done.23.g2 = bf16[160,384]{1,0:T(8,128)(2,1)S(1)} collective-permute-done((bf16[160,384]{1,0:T(8,128)(2,1)S(1)}, bf16[160,384]{1,0:T(8,128)(2,1)S(1)}, u32[]{:S(2)}, u32[]{:S(2)}) %collective-permute-start.23) | collective-permute-done | bytes 122912 | tf_op jit(solution)/shard_map/ppermute | solution.py:21
  98.3 1.8 %collective-permute-done.24.g3 = bf16[160,384]{1,0:T(8,128)(2,1)S(1)} collective-permute-done((bf16[160,384]{1,0:T(8,128)(2,1)S(1)}, bf16[160,384]{1,0:T(8,128)(2,1)S(1)}, u32[]{:S(2)}, u32[]{:S(2)}) %collective-permute-start.24) | collective-permute-done | bytes 122912 | tf_op jit(solution)/shard_map/ppermute | solution.py:21
  100.1 0.6 shard_map.148
  100.7 2.3 %collective-permute-start.25 = (bf16[128,384]{1,0:T(8,128)(2,1)S(1)}, bf16[128,384]{1,0:T(8,128)(2,1)S(1)}, u32[]{:S(2)}, u32[]{:S(2)}) collective-permute-start(bf16[128,384]{1,0:T(8,128)(2,1)S(1)} %get-tuple-element.77), channel_id=1, source_target_pairs={{0,32},{32,0},{64,96},{96,64},{128,160},{160,128},{192,224},{224,1... | collective-permute-start | bytes 294920 | tf_op jit(solution)/shard_map/ppermute | solution.py:21
  103.1 2.9 %collective-permute-done.25.got = bf16[128,384]{1,0:T(8,128)(2,1)S(1)} collective-permute-done((bf16[128,384]{1,0:T(8,128)(2,1)S(1)}, bf16[128,384]{1,0:T(8,128)(2,1)S(1)}, u32[]{:S(2)}, u32[]{:S(2)}) %collective-permute-start.25) | collective-permute-done | bytes 98336 | tf_op jit(solution)/shard_map/ppermute | solution.py:21
  106.0 0.6 shard_map.149
  106.6 4.4 %collective-permute-start.26 = (bf16[96,384]{1,0:T(8,128)(2,1)S(1)}, bf16[96,384]{1,0:T(8,128)(2,1)S(1)}, u32[]{:S(2)}, u32[]{:S(2)}) collective-permute-start(bf16[96,384]{1,0:T(8,128)(2,1)S(1)} %get-tuple-element.80), channel_id=1, source_target_pairs={{0,128},{32,160},{64,192},{96,224},{128,0},{160,32},{192,64},{224,... | collective-permute-start | bytes 221192 | tf_op jit(solution)/shard_map/ppermute | solution.py:21
  111.2 4.6 %collective-permute-done.26.got = bf16[96,384]{1,0:T(8,128)(2,1)S(1)} collective-permute-done((bf16[96,384]{1,0:T(8,128)(2,1)S(1)}, bf16[96,384]{1,0:T(8,128)(2,1)S(1)}, u32[]{:S(2)}, u32[]{:S(2)}) %collective-permute-start.26) | collective-permute-done | bytes 73760 | tf_op jit(solution)/shard_map/ppermute | solution.py:21
  115.8 0.6 shard_map.150
  116.4 1.1 collective-permute-start.27
  117.8 4.2 %fusion.10 = bf16[8,32,384]{2,1,0:T(8,128)(2,1)} fusion(f32[14,38,384]{2,1,0:T(8,128)S(1)} %maximum_convert_fusion, f32[384]{0:T(512)S(1)} %get-tuple-element.89, f32[384]{0:T(512)S(1)} %get-tuple-element.90, f32[384]{0:T(512)S(1)} %get-tuple-element.91, f32[384]{0:T(512)S(1)} %get-tuple-element.92, f32[384]{0:T(512)S(1)} %copy-done.13, ...), kind=kLoop, calls=%fused_computation.20 | loop fusion | flops 9830400 | bytes 19736064 | tf_op jit(solution)/shard_map/convert_element_type | solution.py:408
  122.0 0.5 collective-permute-done.27.got
  122.5 1.2 shard_map.151
  123.7 0.6 reshape.117
  (256 shorter events, 3.6 us)
Async XLA Ops:
  0.6 25.6 %copy-start.1 = (bf16[8,32,384]{2,1,0:T(8,128)(2,1)S(1)}, bf16[8,32,384]{2,1,0:T(8,128)(2,1)}, u32[]{:S(2)}) copy-start(bf16[8,32,384]{2,1,0:T(8,128)(2,1)} %feature) | copy-start | bytes 589828
  1.4 15.1 %collective-permute-start = (bf16[2,6,384]{2,1,0:T(8,128)(2,1)S(1)}, bf16[2,6,384]{2,1,0:T(8,128)(2,1)S(1)}, u32[]{:S(2)}, u32[]{:S(2)}) collective-permute-start(bf16[2,6,384]{2,1,0:T(8,128)(2,1)S(1)} %pad_maximum_fusion.13), channel_id=1, source_target_pairs={{0,192},{32,224},{64,128},{96,160},{128,64},{160,96},{192,0},{224,... | collective-permute-start | bytes 27656 | tf_op jit(solution)/shard_map/ppermute | solution.py:21
  7.8 8.7 %collective-permute-start.1 = (bf16[2,6,384]{2,1,0:T(8,128)(2,1)S(1)}, bf16[2,6,384]{2,1,0:T(8,128)(2,1)S(1)}, u32[]{:S(2)}, u32[]{:S(2)}) collective-permute-start(bf16[2,6,384]{2,1,0:T(8,128)(2,1)S(1)} %pad_maximum_fusion.13), channel_id=1, source_target_pairs={{0,128},{32,160},{64,192},{96,224},{128,0},{160,32},{192,64},{224,... | collective-permute-start | bytes 27656 | tf_op jit(solution)/shard_map/ppermute | solution.py:21
  8.8 7.7 %collective-permute-start.2 = (bf16[2,6,384]{2,1,0:T(8,128)(2,1)S(1)}, bf16[2,6,384]{2,1,0:T(8,128)(2,1)S(1)}, u32[]{:S(2)}, u32[]{:S(2)}) collective-permute-start(bf16[2,6,384]{2,1,0:T(8,128)(2,1)S(1)} %pad_maximum_fusion.13), channel_id=1, source_target_pairs={{0,64},{32,96},{64,0},{96,32},{128,192},{160,224},{192,128},{224,1... | collective-permute-start | bytes 27656 | tf_op jit(solution)/shard_map/ppermute | solution.py:21
  11.2 11.5 %collective-permute-start.5 = (bf16[3,32,384]{2,1,0:T(8,128)(2,1)S(1)}, bf16[3,32,384]{2,1,0:T(8,128)(2,1)S(1)}, u32[]{:S(2)}, u32[]{:S(2)}) collective-permute-start(bf16[3,32,384]{2,1,0:T(8,128)(2,1)S(1)} %get-tuple-element.147), channel_id=1, source_target_pairs={{8,16},{16,8},{24,32},{32,24},{40,48},{48,40},{56,64},{64,56},{72,... | collective-permute-start | bytes 221192 | tf_op jit(solution)/shard_map/ppermute | solution.py:34
  11.8 10.9 %collective-permute-start.4 = (bf16[3,32,384]{2,1,0:T(8,128)(2,1)S(1)}, bf16[3,32,384]{2,1,0:T(8,128)(2,1)S(1)}, u32[]{:S(2)}, u32[]{:S(2)}) collective-permute-start(bf16[3,32,384]{2,1,0:T(8,128)(2,1)S(1)} %get-tuple-element.148), channel_id=1, source_target_pairs={{0,8},{8,0},{16,24},{24,16},{32,40},{40,32},{48,56},{56,48},{64,72... | collective-permute-start | bytes 221192 | tf_op jit(solution)/shard_map/ppermute | solution.py:21
  17.3 5.4 %collective-permute-start.3 = (bf16[2,24,384]{2,1,0:T(8,128)(2,1)S(1)}, bf16[2,24,384]{2,1,0:T(8,128)(2,1)S(1)}, u32[]{:S(2)}, u32[]{:S(2)}) collective-permute-start(bf16[2,24,384]{2,1,0:T(8,128)(2,1)S(1)} %pad_maximum_fusion.12), channel_id=1, source_target_pairs={{0,32},{32,0},{64,96},{96,64},{128,160},{160,128},{192,224},{224,1... | collective-permute-start | bytes 110600 | tf_op jit(solution)/shard_map/ppermute | solution.py:21
  22.8 10.8 %collective-permute-start.7 = (bf16[2,48,384]{2,1,0:T(8,128)(2,1)S(1)}, bf16[2,48,384]{2,1,0:T(8,128)(2,1)S(1)}, u32[]{:S(2)}, u32[]{:S(2)}) collective-permute-start(bf16[2,48,384]{2,1,0:T(8,128)(2,1)S(1)} %pad_maximum_fusion.11), channel_id=1, source_target_pairs={{0,16},{1,17},{16,0},{17,1},{2,18},{3,19},{18,2},{19,3},{4,20},{5,... | collective-permute-start | bytes 221192 | tf_op jit(solution)/shard_map/ppermute | solution.py:21
  24.9 8.6 %collective-permute-start.8 = (bf16[2,48,384]{2,1,0:T(8,128)(2,1)S(1)}, bf16[2,48,384]{2,1,0:T(8,128)(2,1)S(1)}, u32[]{:S(2)}, u32[]{:S(2)}) collective-permute-start(bf16[2,48,384]{2,1,0:T(8,128)(2,1)S(1)} %pad_maximum_fusion.11), channel_id=1, source_target_pairs={{0,17},{1,16},{16,1},{17,0},{2,19},{3,18},{18,3},{19,2},{4,21},{5,... | collective-permute-start | bytes 221192 | tf_op jit(solution)/shard_map/ppermute | solution.py:21
  26.4 5.3 %collective-permute-start.6 = (bf16[138,384]{1,0:T(8,128)(2,1)S(1)}, bf16[138,384]{1,0:T(8,128)(2,1)S(1)}, u32[]{:S(2)}, u32[]{:S(2)}) collective-permute-start(bf16[138,384]{1,0:T(8,128)(2,1)S(1)} %pad_maximum_fusion.10), channel_id=1, source_target_pairs={{0,1},{1,0},{16,17},{17,16},{2,3},{3,2},{18,19},{19,18},{4,5},{5,4... | collective-permute-start | bytes 317960 | tf_op jit(solution)/shard_map/ppermute | solution.py:21
  26.6 6.8 %collective-permute-start.9 = (bf16[14,3,384]{2,1,0:T(4,128)(2,1)S(1)}, bf16[14,3,384]{2,1,0:T(4,128)(2,1)S(1)}, u32[]{:S(2)}, u32[]{:S(2)}) collective-permute-start(bf16[14,3,384]{2,1,0:T(4,128)(2,1)S(1)} %get-tuple-element.145), channel_id=1, source_target_pairs={{1,2},{2,1},{3,4},{4,3},{5,6},{6,5},{9,10},{10,9},{11,12},{12,11},... | collective-permute-start | bytes 96776 | tf_op jit(solution)/shard_map/ppermute | solution.py:34
  33.6 11.4 %collective-permute-start.11 = (bf16[2,192,384]{2,1,0:T(8,128)(2,1)S(1)}, bf16[2,192,384]{2,1,0:T(8,128)(2,1)S(1)}, u32[]{:S(2)}, u32[]{:S(2)}) collective-permute-start(bf16[2,192,384]{2,1,0:T(8,128)(2,1)S(1)} %constant_dynamic-update-slice_fusion.7), channel_id=1, source_target_pairs={{0,2},{2,0},{4,6},{6,4},{1,3},{3,1},{5,7},{7,5},{8,10},{10,8},{12,... | collective-permute-start | bytes 884744 | tf_op jit(solution)/shard_map/ppermute | solution.py:21
  34.5 12.2 %collective-permute-start.12 = (bf16[2,192,384]{2,1,0:T(8,128)(2,1)S(1)}, bf16[2,192,384]{2,1,0:T(8,128)(2,1)S(1)}, u32[]{:S(2)}, u32[]{:S(2)}) collective-permute-start(bf16[2,192,384]{2,1,0:T(8,128)(2,1)S(1)} %constant_dynamic-update-slice_fusion.7), channel_id=1, source_target_pairs={{0,4},{2,6},{4,0},{6,2},{1,5},{3,7},{5,1},{7,3},{8,12},{10,14},{12... | collective-permute-start | bytes 884744 | tf_op jit(solution)/shard_map/ppermute | solution.py:21
  35.2 14.2 %collective-permute-start.13 = (bf16[2,192,384]{2,1,0:T(8,128)(2,1)S(1)}, bf16[2,192,384]{2,1,0:T(8,128)(2,1)S(1)}, u32[]{:S(2)}, u32[]{:S(2)}) collective-permute-start(bf16[2,192,384]{2,1,0:T(8,128)(2,1)S(1)} %constant_dynamic-update-slice_fusion.7), channel_id=1, source_target_pairs={{0,6},{2,4},{4,2},{6,0},{1,7},{3,5},{5,3},{7,1},{8,14},{10,12},{12... | collective-permute-start | bytes 884744 | tf_op jit(solution)/shard_map/ppermute | solution.py:21
  44.6 4.9 %collective-permute-start.10 = (bf16[2,256,384]{2,1,0:T(8,128)(2,1)S(1)}, bf16[2,256,384]{2,1,0:T(8,128)(2,1)S(1)}, u32[]{:S(2)}, u32[]{:S(2)}) collective-permute-start(bf16[2,256,384]{2,1,0:T(8,128)(2,1)S(1)} %pad_maximum_fusion.1), channel_id=1, source_target_pairs={{0,8},{8,0},{1,9},{9,1},{2,10},{10,2},{3,11},{11,3},{4,12},{12,4},... | collective-permute-start | bytes 1179656 | tf_op jit(solution)/shard_map/ppermute | solution.py:21
  53.2 2.9 %collective-permute-start.14 = (bf16[2,256,384]{2,1,0:T(8,128)(2,1)}, bf16[2,256,384]{2,1,0:T(8,128)(2,1)S(1)}, u32[]{:S(2)}, u32[]{:S(2)}) collective-permute-start(bf16[2,256,384]{2,1,0:T(8,128)(2,1)} %pad_maximum_fusion.4), channel_id=1, source_target_pairs={{0,8},{8,0},{1,9},{9,1},{2,10},{10,2},{3,11},{11,3},{4,12},{12,4},... | collective-permute-start | bytes 1179656 | tf_op jit(solution)/shard_map/ppermute | solution.py:21
  59.8 1.9 %collective-permute-start.15 = (bf16[160,384]{1,0:T(8,128)(2,1)S(1)}, bf16[160,384]{1,0:T(8,128)(2,1)S(1)}, u32[]{:S(2)}, u32[]{:S(2)}) collective-permute-start(bf16[160,384]{1,0:T(8,128)(2,1)S(1)} %get-tuple-element.59.mine), channel_id=1, source_target_pairs={{0,8},{8,0},{1,9},{9,1},{2,10},{10,2},{3,11},{11,3},{4,12},{12,4},... | collective-permute-start | bytes 368648 | tf_op jit(solution)/shard_map/ppermute | solution.py:21
  60.4 6.8 %collective-permute-start.19 = (bf16[3,32,384]{2,1,0:T(8,128)(2,1)S(1)}, bf16[3,32,384]{2,1,0:T(8,128)(2,1)S(1)}, u32[]{:S(2)}, u32[]{:S(2)}) collective-permute-start(bf16[3,32,384]{2,1,0:T(8,128)(2,1)S(1)} %get-tuple-element.63), channel_id=1, source_target_pairs={{8,16},{16,8},{24,32},{32,24},{40,48},{48,40},{56,64},{64,56},{72,... | collective-permute-start | bytes 221192 | tf_op jit(solution)/shard_map/ppermute | solution.py:34
  62.4 8.9 %collective-permute-start.16 = (bf16[448,384]{1,0:T(8,128)(2,1)S(1)}, bf16[448,384]{1,0:T(8,128)(2,1)S(1)}, u32[]{:S(2)}, u32[]{:S(2)}) collective-permute-start(bf16[448,384]{1,0:T(8,128)(2,1)S(1)} %get-tuple-element.60), channel_id=1, source_target_pairs={{0,2},{2,0},{4,6},{6,4},{1,3},{3,1},{5,7},{7,5},{8,10},{10,8},{12,... | collective-permute-start | bytes 1032200 | tf_op jit(solution)/shard_map/ppermute | solution.py:21
  62.5 18.6 %collective-permute-start.17 = (bf16[448,384]{1,0:T(8,128)(2,1)S(1)}, bf16[448,384]{1,0:T(8,128)(2,1)S(1)}, u32[]{:S(2)}, u32[]{:S(2)}) collective-permute-start(bf16[448,384]{1,0:T(8,128)(2,1)S(1)} %get-tuple-element.61), channel_id=1, source_target_pairs={{0,4},{2,6},{4,0},{6,2},{1,5},{3,7},{5,1},{7,3},{8,12},{10,14},{12... | collective-permute-start | bytes 1032200 | tf_op jit(solution)/shard_map/ppermute | solution.py:21
  66.9 17.9 %collective-permute-start.18 = (bf16[448,384]{1,0:T(8,128)(2,1)S(1)}, bf16[448,384]{1,0:T(8,128)(2,1)S(1)}, u32[]{:S(2)}, u32[]{:S(2)}) collective-permute-start(bf16[448,384]{1,0:T(8,128)(2,1)S(1)} %get-tuple-element.62), channel_id=1, source_target_pairs={{0,6},{2,4},{4,2},{6,0},{1,7},{3,5},{5,3},{7,1},{8,14},{10,12},{12... | collective-permute-start | bytes 1032200 | tf_op jit(solution)/shard_map/ppermute | solution.py:21
  85.6 9.7 %collective-permute-start.22 = (bf16[160,384]{1,0:T(8,128)(2,1)S(1)}, bf16[160,384]{1,0:T(8,128)(2,1)S(1)}, u32[]{:S(2)}, u32[]{:S(2)}) collective-permute-start(bf16[160,384]{1,0:T(8,128)(2,1)S(1)} %get-tuple-element.72), channel_id=1, source_target_pairs={{0,1},{1,0},{16,17},{17,16},{2,3},{3,2},{18,19},{19,18},{4,5},{5,4... | collective-permute-start | bytes 368648 | tf_op jit(solution)/shard_map/ppermute | solution.py:21
  87.8 10.6 %collective-permute-start.23 = (bf16[160,384]{1,0:T(8,128)(2,1)S(1)}, bf16[160,384]{1,0:T(8,128)(2,1)S(1)}, u32[]{:S(2)}, u32[]{:S(2)}) collective-permute-start(bf16[160,384]{1,0:T(8,128)(2,1)S(1)} %get-tuple-element.73), channel_id=1, source_target_pairs={{0,16},{1,17},{16,0},{17,1},{2,18},{3,19},{18,2},{19,3},{4,20},{5,... | collective-permute-start | bytes 368648 | tf_op jit(solution)/shard_map/ppermute | solution.py:21
  92.5 25.0 %copy-start.21 = (f32[384]{0:T(512)S(1)}, f32[384]{0:T(512)}, u32[]{:S(2)}) copy-start(f32[384]{0:T(512)} %copy-done.20) | copy-start | bytes 4612
  92.5 25.0 %copy-start.23 = (f32[384]{0:T(512)S(1)}, f32[384]{0:T(512)}, u32[]{:S(2)}) copy-start(f32[384]{0:T(512)} %copy-done.22) | copy-start | bytes 4612
  92.5 25.0 %copy-start.25 = (f32[384]{0:T(512)S(1)}, f32[384]{0:T(512)}, u32[]{:S(2)}) copy-start(f32[384]{0:T(512)} %copy-done.24) | copy-start | bytes 4612
  92.5 25.0 %copy-start.27 = (f32[384]{0:T(512)S(1)}, f32[384]{0:T(512)}, u32[]{:S(2)}) copy-start(f32[384]{0:T(512)} %copy-done.26) | copy-start | bytes 4612
  92.5 25.0 %copy-start.29 = (f32[384]{0:T(512)S(1)}, f32[384]{0:T(512)}, u32[]{:S(2)}) copy-start(f32[384]{0:T(512)} %copy-done.28) | copy-start | bytes 4612
  92.5 25.0 %copy-start.31 = (f32[384]{0:T(512)S(1)}, f32[384]{0:T(512)}, u32[]{:S(2)}) copy-start(f32[384]{0:T(512)} %copy-done.30) | copy-start | bytes 4612
  92.5 25.0 %copy-start.33 = (f32[384]{0:T(512)S(1)}, f32[384]{0:T(512)}, u32[]{:S(2)}) copy-start(f32[384]{0:T(512)} %copy-done.32) | copy-start | bytes 4612
  92.5 25.0 %copy-start.35 = (f32[384]{0:T(512)S(1)}, f32[384]{0:T(512)}, u32[]{:S(2)}) copy-start(f32[384]{0:T(512)} %copy-done.34) | copy-start | bytes 4612
  92.6 25.0 %copy-start.37 = (f32[384]{0:T(512)S(1)}, f32[384]{0:T(512)}, u32[]{:S(2)}) copy-start(f32[384]{0:T(512)} %copy-done.36) | copy-start | bytes 4612
  92.6 25.0 %copy-start.39 = (f32[384]{0:T(512)S(1)}, f32[384]{0:T(512)}, u32[]{:S(2)}) copy-start(f32[384]{0:T(512)} %copy-done.38) | copy-start | bytes 4612
  92.6 25.0 %copy-start.41 = (f32[384]{0:T(512)S(1)}, f32[384]{0:T(512)}, u32[]{:S(2)}) copy-start(f32[384]{0:T(512)} %copy-done.40) | copy-start | bytes 4612
  92.6 25.0 %copy-start.43 = (f32[384]{0:T(512)S(1)}, f32[384]{0:T(512)}, u32[]{:S(2)}) copy-start(f32[384]{0:T(512)} %copy-done.42) | copy-start | bytes 4612
  92.6 25.0 %copy-start.45 = (f32[384]{0:T(512)S(1)}, f32[384]{0:T(512)}, u32[]{:S(2)}) copy-start(f32[384]{0:T(512)} %copy-done.44) | copy-start | bytes 4612
  92.6 25.0 %copy-start.47 = (f32[384]{0:T(512)S(1)}, f32[384]{0:T(512)}, u32[]{:S(2)}) copy-start(f32[384]{0:T(512)} %copy-done.46) | copy-start | bytes 4612
  92.6 25.0 %copy-start.49 = (f32[384]{0:T(512)S(1)}, f32[384]{0:T(512)}, u32[]{:S(2)}) copy-start(f32[384]{0:T(512)} %copy-done.48) | copy-start | bytes 4612
  92.6 25.0 %copy-start.51 = (f32[384]{0:T(512)S(1)}, f32[384]{0:T(512)}, u32[]{:S(2)}) copy-start(f32[384]{0:T(512)} %copy-done.50) | copy-start | bytes 4612
  92.6 25.0 %copy-start.53 = (f32[384]{0:T(512)S(1)}, f32[384]{0:T(512)}, u32[]{:S(2)}) copy-start(f32[384]{0:T(512)} %copy-done.52) | copy-start | bytes 4612
  92.6 25.0 %copy-start.55 = (f32[384]{0:T(512)S(1)}, f32[384]{0:T(512)}, u32[]{:S(2)}) copy-start(f32[384]{0:T(512)} %copy-done.54) | copy-start | bytes 4612
  92.7 25.0 %copy-start.57 = (f32[384]{0:T(512)S(1)}, f32[384]{0:T(512)}, u32[]{:S(2)}) copy-start(f32[384]{0:T(512)} %copy-done.56) | copy-start | bytes 4612
  92.7 25.0 %copy-start.59 = (f32[384]{0:T(512)S(1)}, f32[384]{0:T(512)}, u32[]{:S(2)}) copy-start(f32[384]{0:T(512)} %copy-done.58) | copy-start | bytes 4612
  92.7 25.0 %copy-start.61 = (f32[384]{0:T(512)S(1)}, f32[384]{0:T(512)}, u32[]{:S(2)}) copy-start(f32[384]{0:T(512)} %copy-done.60) | copy-start | bytes 4612
  92.7 25.0 %copy-start.63 = (f32[384]{0:T(512)S(1)}, f32[384]{0:T(512)}, u32[]{:S(2)}) copy-start(f32[384]{0:T(512)} %copy-done.62) | copy-start | bytes 4612
  92.7 25.0 %copy-start.65 = (f32[384]{0:T(512)S(1)}, f32[384]{0:T(512)}, u32[]{:S(2)}) copy-start(f32[384]{0:T(512)} %copy-done.64) | copy-start | bytes 4612
  92.7 25.0 %copy-start.67 = (f32[384]{0:T(512)S(1)}, f32[384]{0:T(512)}, u32[]{:S(2)}) copy-start(f32[384]{0:T(512)} %copy-done.66) | copy-start | bytes 4612
  92.7 25.0 %copy-start.69 = (f32[384]{0:T(512)S(1)}, f32[384]{0:T(512)}, u32[]{:S(2)}) copy-start(f32[384]{0:T(512)} %copy-done.68) | copy-start | bytes 4612
  92.7 25.0 %copy-start.71 = (f32[384]{0:T(512)S(1)}, f32[384]{0:T(512)}, u32[]{:S(2)}) copy-start(f32[384]{0:T(512)} %copy-done.70) | copy-start | bytes 4612
  92.7 25.0 %copy-start.73 = (f32[384]{0:T(512)S(1)}, f32[384]{0:T(512)}, u32[]{:S(2)}) copy-start(f32[384]{0:T(512)} %copy-done.72) | copy-start | bytes 4612
  92.7 25.0 %copy-start.75 = (f32[384]{0:T(512)S(1)}, f32[384]{0:T(512)}, u32[]{:S(2)}) copy-start(f32[384]{0:T(512)} %copy-done.74) | copy-start | bytes 4612
  92.8 25.0 %copy-start.77 = (f32[384]{0:T(512)S(1)}, f32[384]{0:T(512)}, u32[]{:S(2)}) copy-start(f32[384]{0:T(512)} %copy-done.76) | copy-start | bytes 4612
  92.8 25.0 %copy-start.79 = (f32[384]{0:T(512)S(1)}, f32[384]{0:T(512)}, u32[]{:S(2)}) copy-start(f32[384]{0:T(512)} %copy-done.78) | copy-start | bytes 4612
  92.8 25.0 %copy-start.81 = (f32[384]{0:T(512)S(1)}, f32[384]{0:T(512)}, u32[]{:S(2)}) copy-start(f32[384]{0:T(512)} %copy-done.80) | copy-start | bytes 4612
  92.8 25.0 %copy-start.83 = (f32[384]{0:T(512)S(1)}, f32[384]{0:T(512)}, u32[]{:S(2)}) copy-start(f32[384]{0:T(512)} %copy-done.82) | copy-start | bytes 4612
  92.8 25.0 %copy-start.85 = (f32[384]{0:T(512)S(1)}, f32[384]{0:T(512)}, u32[]{:S(2)}) copy-start(f32[384]{0:T(512)} %copy-done.84) | copy-start | bytes 4612
  92.8 25.0 %copy-start.87 = (f32[384]{0:T(512)S(1)}, f32[384]{0:T(512)}, u32[]{:S(2)}) copy-start(f32[384]{0:T(512)} %copy-done.86) | copy-start | bytes 4612
  92.8 25.0 %copy-start.89 = (f32[384]{0:T(512)S(1)}, f32[384]{0:T(512)}, u32[]{:S(2)}) copy-start(f32[384]{0:T(512)} %copy-done.88) | copy-start | bytes 4612
  92.8 7.3 %collective-permute-start.24 = (bf16[160,384]{1,0:T(8,128)(2,1)S(1)}, bf16[160,384]{1,0:T(8,128)(2,1)S(1)}, u32[]{:S(2)}, u32[]{:S(2)}) collective-permute-start(bf16[160,384]{1,0:T(8,128)(2,1)S(1)} %get-tuple-element.74), channel_id=1, source_target_pairs={{0,17},{1,16},{16,1},{17,0},{2,19},{3,18},{18,3},{19,2},{4,21},{5,... | collective-permute-start | bytes 368648 | tf_op jit(solution)/shard_map/ppermute | solution.py:21
  93.2 9.9 %collective-permute-start.20 = (bf16[14,3,384]{2,1,0:T(4,128)(2,1)S(1)}, bf16[14,3,384]{2,1,0:T(4,128)(2,1)S(1)}, u32[]{:S(2)}, u32[]{:S(2)}) collective-permute-start(bf16[14,3,384]{2,1,0:T(4,128)(2,1)S(1)} %get-tuple-element.143), channel_id=1, source_target_pairs={{0,1},{1,0},{2,3},{3,2},{4,5},{5,4},{6,7},{7,6},{8,9},{9,8},{10,11... | collective-permute-start | bytes 96776 | tf_op jit(solution)/shard_map/ppermute | solution.py:21
  93.3 9.8 %collective-permute-start.21 = (bf16[14,3,384]{2,1,0:T(4,128)(2,1)S(1)}, bf16[14,3,384]{2,1,0:T(4,128)(2,1)S(1)}, u32[]{:S(2)}, u32[]{:S(2)}) collective-permute-start(bf16[14,3,384]{2,1,0:T(4,128)(2,1)S(1)} %get-tuple-element.144), channel_id=1, source_target_pairs={{1,2},{2,1},{3,4},{4,3},{5,6},{6,5},{9,10},{10,9},{11,12},{12,11},... | collective-permute-start | bytes 96776 | tf_op jit(solution)/shard_map/ppermute | solution.py:34
  100.7 5.3 %collective-permute-start.25 = (bf16[128,384]{1,0:T(8,128)(2,1)S(1)}, bf16[128,384]{1,0:T(8,128)(2,1)S(1)}, u32[]{:S(2)}, u32[]{:S(2)}) collective-permute-start(bf16[128,384]{1,0:T(8,128)(2,1)S(1)} %get-tuple-element.77), channel_id=1, source_target_pairs={{0,32},{32,0},{64,96},{96,64},{128,160},{160,128},{192,224},{224,1... | collective-permute-start | bytes 294920 | tf_op jit(solution)/shard_map/ppermute | solution.py:21
  106.6 9.1 %collective-permute-start.26 = (bf16[96,384]{1,0:T(8,128)(2,1)S(1)}, bf16[96,384]{1,0:T(8,128)(2,1)S(1)}, u32[]{:S(2)}, u32[]{:S(2)}) collective-permute-start(bf16[96,384]{1,0:T(8,128)(2,1)S(1)} %get-tuple-element.80), channel_id=1, source_target_pairs={{0,128},{32,160},{64,192},{96,224},{128,0},{160,32},{192,64},{224,... | collective-permute-start | bytes 221192 | tf_op jit(solution)/shard_map/ppermute | solution.py:21
  116.4 6.1 %collective-permute-start.27 = (bf16[96,384]{1,0:T(8,128)(2,1)S(1)}, bf16[96,384]{1,0:T(8,128)(2,1)S(1)}, u32[]{:S(2)}, u32[]{:S(2)}) collective-permute-start(bf16[96,384]{1,0:T(8,128)(2,1)S(1)} %get-tuple-element.83), channel_id=1, source_target_pairs={{0,64},{32,96},{64,0},{96,32},{128,192},{160,224},{192,128},{224,1... | collective-permute-start | bytes 221192 | tf_op jit(solution)/shard_map/ppermute | solution.py:21
  (56 other events, 377.7 us)

commit v3 on v2

--- a/solution.py
+++ b/solution.py
@@ -99,7 +99,7 @@
         out_specs=[pl.BlockSpec(memory_space=pltpu.VMEM)] * len(outs),
         scratch_shapes=list(scratch),
         cost_estimate=pl.CostEstimate(flops=flops, bytes_accessed=moved, transcendentals=0),
-        compiler_params=pltpu.CompilerParams(vmem_limit_bytes=32 * 2**20),
+        compiler_params=pltpu.CompilerParams(vmem_limit_bytes=8 * 2**20),
     )(index, *arrays)
 
 
@@ -108,6 +108,16 @@
 
 
 SMALL = 64
+
+
+def put_two(ref, at, value):
+    high = value.astype(BF)
+    ref[at : at + SMALL, :] = high
+    ref[at + SMALL : at + 2 * SMALL, :] = (value - high.astype(F4)).astype(BF)
+
+
+def get_two(ref, at):
+    return ref[at : at + SMALL, :].astype(F4) + ref[at + SMALL : at + 2 * SMALL, :].astype(F4)
 
 
 def norm_back(
@@ -156,10 +166,10 @@
                 total[r - p] = total[r - p] + term
         for i in range(7):
             sums[7 * i + j : 7 * i + j + 1, :] = jnp.sum(total[i], 0, keepdims=True)
-    message[0:SMALL, :] = sums[...].astype(BF)
+    put_two(message, 0, sums[...])
     odd = index[0] != 0
     first, last = grads[0:3], grads[rows - 3 : rows]
-    message[SMALL : SMALL + 3 * cols, :] = (
+    message[2 * SMALL : 2 * SMALL + 3 * cols, :] = (
         jnp.where(odd, first, last).astype(BF).reshape(3 * cols, channels)
     )
     outer[...] = jnp.where(odd, last, first).astype(BF)
@@ -167,7 +177,7 @@
 
 def first_fan(index, win, wout, mine, theirs, one, two, three, shared):
     rows = win.shape[0] // 4
-    shared[...] = (mine[0:SMALL, :].astype(F4) + theirs[0:SMALL, :].astype(F4)).astype(BF)
+    shared[...] = (get_two(mine, 0) + get_two(theirs, 0)).astype(BF)
     for flip, message in ((1, one), (2, two), (3, three)):
         at = pl.multiple_of((index[1] ^ flip) * rows, rows)
         message[0:rows, :] = win[pl.ds(at, rows), :].astype(BF)
@@ -210,36 +220,65 @@
         got = [g[k * rows : (k + 1) * rows, :].astype(F4) for g in (g1, g2, g3)]
         total[k] = tree([before[k, pl.ds(at, rows), :]] + got)
     small = tree([mine[...].astype(F4)] + [g[2 * rows :, :].astype(F4) for g in (g1, g2, g3)])
-    shared[...] = small.astype(BF)
-    held = message.shape[0] - SMALL
+    put_two(shared, 0, small)
+    held = message.shape[0] - 2 * SMALL
     for k in range(2):
         send_half(total, k, index[3] != 0, message)
     message[held:, :] = shared[...]
 
 
-def pair_step(here, after, index, before, mine, got, total, message, shared):
+def quarter(ref, k, which):
+    rows = ref.shape[1] // 4
+    parts = [ref[k, i * rows : (i + 1) * rows, :] for i in range(4)]
+    low = [jnp.where((which & 1) != 0, q, p) for p, q in (parts[:2], parts[2:])]
+    return jnp.where((which & 2) != 0, low[1], low[0])
+
+
+def fourth_fan(index, before, mine, got, total, one, two, three, shared):
     half = before.shape[1] // 2
     block = up16(half)
-    bit = index[here] != 0
+    bit = index[3] != 0
     for k in range(2):
         own = jnp.where(bit, before[k, half : 2 * half, :], before[k, 0:half, :])
         total[k] = own + got[k * block : k * block + half, :].astype(F4)
-    shared[...] = (mine[...].astype(F4) + got[2 * block :, :].astype(F4)).astype(BF)
-    for k in range(2):
-        send_half(total, k, index[after] != 0, message)
-    message[message.shape[0] - SMALL :, :] = shared[...]
-
-
-def pair_end(here, index, before, mine, got, win, wout, small, bias):
-    half = before.shape[1] // 2
-    block = up16(half)
-    bit = index[here] != 0
+    shared[...] = (get_two(mine, 0) + get_two(got, 2 * block)).astype(BF)
+    rows = half // 4
+    block = up16(rows)
+    for flip, message in ((1, one), (2, two), (3, three)):
+        for k in range(2):
+            message[k * block : k * block + rows, :] = quarter(total, k, index[4] ^ flip).astype(BF)
+        message[2 * block :, :] = shared[...]
+
+
+def last_sum(index, before, mine, g1, g2, g3, win, wout, small, bias):
+    rows = before.shape[1] // 4
+    block = up16(rows)
     for k, out in ((0, win), (1, wout)):
-        own = jnp.where(bit, before[k, half : 2 * half, :], before[k, 0:half, :])
-        out[...] = own + got[k * block : k * block + half, :].astype(F4)
-    total = mine[...].astype(F4) + got[2 * block :, :].astype(F4)
+        got = [g[k * block : k * block + rows, :].astype(F4) for g in (g1, g2, g3)]
+        out[...] = tree([quarter(before, k, index[4])] + got)
+    total = tree([mine[...].astype(F4)] + [g[2 * block :, :].astype(F4) for g in (g1, g2, g3)])
     small[...] = total[0:53, :]
-    bias[...] = total[53:57, :]
+    wide = total.shape[1]
+    for i in range(4):
+        bias[i * wide : (i + 1) * wide] = total[53 + i]
+
+
+def conv_back(index, tall, left, right, taps, cot, out, wide):
+    rows, cols, channels = out.shape
+    for r in range(rows + 6):
+        wide[r, 8 : 8 + cols, :] = tall[r].astype(F4)
+        wide[r, 5:8, :] = left[r].astype(F4)
+        wide[r, 8 + cols : 11 + cols, :] = right[r].astype(F4)
+    for lane in range(0, channels, 128):
+        total = [cot[p, :, lane : lane + 128].astype(F4) for p in range(rows)]
+        for j in range(7):
+            weights = [taps[7 * i + j : 7 * i + j + 1, lane : lane + 128] for i in range(7)]
+            for r in range(rows + 6):
+                slab = wide[r, 11 - j : 11 - j + cols, lane : lane + 128]
+                for p in range(max(0, r - 6), min(rows, r + 1)):
+                    total[p] = total[p] + slab * weights[6 - (r - p)]
+        for p in range(rows):
+            out[p, :, lane : lane + 128] = total[p].astype(BF)
 
 
 def tree(parts):
@@ -269,8 +308,8 @@
     outer_got = outer_swap(outer, COL)
     weights, inner_got = quad_gather(weights, Y, inner.reshape(-1, channels))
     columns = edge_order(inner_got.reshape(inner.shape), outer_got, COL)
-    weights, tall, columns, cotangent, kernel = lax.optimization_barrier(
-        (weights, tall, columns, cotangent, kernel)
+    weights, tall, columns, cotangent, kernel, ln_gain, layer_scale, b_out = lax.optimization_barrier(
+        (weights, tall, columns, cotangent, kernel, ln_gain, layer_scale, b_out)
     )
     weights = quad_gather(weights, "x")
     w_in_t, w_out_mine = weights[0], weights[1]
@@ -285,6 +324,7 @@
     grad_flow = cotangent.astype(F4).reshape(pixels, channels)
     grad_mixed = grad_flow * layer_scale
 
+    taps = kernel.reshape(-1, channels)
     padded_low = between(tall, columns, 1)
     padded = padded_low.astype(F4)
     conv = jnp.zeros((row_count, col_count, channels), F4)
@@ -324,14 +364,14 @@
         .reshape(hidden_count // channels, channels)
     )
     index = jnp.stack(
-        [core, lax.axis_index("x"), lax.axis_index(Y), z & 1, (z // 4) & 1, (z // 2) & 1]
+        [core, lax.axis_index("x"), lax.axis_index(Y), z & 1, z // 2]
     ).astype(jnp.int32)
     grad_low, mine, outer, block_out = local_call(
         norm_back,
         index,
         [
             shape(row_count, col_count, channels, dtype=BF),
-            shape(SMALL + 3 * col_count, channels, dtype=BF),
+            shape(2 * SMALL + 3 * col_count, channels, dtype=BF),
             shape(3, col_count, channels, dtype=BF),
             shape(row_count, col_count, channels, dtype=BF),
         ],
@@ -345,24 +385,25 @@
         flops=110 * pixels * channels,
     )
     theirs = swap(mine, "c", 1)
-    outer_got = outer_swap(outer, ROW)
-    rows = edge_order(theirs[SMALL:].reshape(3, col_count, channels), outer_got, ROW)
-    low_tall = between(grad_low, rows, 0)
-
     small_shape = shape(SMALL, channels, dtype=BF)
 
-    def message_of(rows, block=None):
-        return shape(2 * (block or rows) + SMALL, channels, dtype=BF)
-
-    def fan(messages, axis):
-        return [swap(m, axis, flip) for m, flip in zip(messages, (1, 2, 3))]
+    def message_of(rows, smalls=1):
+        return shape(2 * rows + smalls * SMALL, channels, dtype=BF)
+
+    def fan(messages, axis, unit=1):
+        return [swap(m, axis, flip * unit) for m, flip in zip(messages, (1, 2, 3))]
 
     piece = half // 4
     *messages, shared = local_call(
         first_fan, index, [message_of(piece)] * 3 + [small_shape], win_term, wout_term, mine, theirs
     )
     got = fan(messages, "x")
-    got, low_tall = lax.optimization_barrier((got, low_tall))
+    first_got, outer = lax.optimization_barrier((got[0], outer))
+    got[0] = first_got
+    outer_got = outer_swap(outer, ROW)
+    rows = edge_order(theirs[2 * SMALL :].reshape(3, col_count, channels), outer_got, ROW)
+    low_tall = between(grad_low, rows, 0)
+    columns = edges(low_tall, COL, 1)
     total, *messages, shared = local_call(
         second_fan,
         index,
@@ -371,42 +412,39 @@
     )
     piece = piece // 4
     got = fan(messages, Y)
-    columns = edges(low_tall, COL, 1)
-    grad_pad = between(low_tall, columns, 1).astype(F4)
     total, message, shared = local_call(
         third_fan,
         index,
-        [shape(2, piece, channels), message_of(up16(piece // 2)), small_shape],
+        [
+            shape(2, piece, channels),
+            message_of(up16(piece // 2), 2),
+            shape(2 * SMALL, channels, dtype=BF),
+        ],
         total, shared, *got,
     )
-    for here, after, unit in ((3, 4, 1), (4, 5, 4)):
-        piece = piece // 2
-        got = swap(message, "z", unit)
-        total, message, shared = local_call(
-            functools.partial(pair_step, here, after),
-            index,
-            [shape(2, piece, channels), message_of(up16(piece // 2)), small_shape],
-            total, shared, got,
-        )
-    got = swap(message, "z", 2)
-    win_t, grad_w_out, small_grads, bias_rows = local_call(
-        functools.partial(pair_end, 5),
-        index,
-        [shape(units, channels), shape(units, channels), shape(53, channels), shape(4, channels)],
+    piece = piece // 2
+    got = swap(message, "z", 1)
+    total, *messages, shared = local_call(
+        fourth_fan,
+        index,
+        [shape(2, piece, channels)] + [message_of(up16(units))] * 3 + [small_shape],
         total, shared, got,
     )
-    back_conv = jnp.zeros((row_count, col_count, channels), F4)
-    for tap_row in range(7):
-        for tap_col in range(7):
-            back_conv = (
-                back_conv
-                + grad_pad[
-                    6 - tap_row : 6 - tap_row + row_count, 6 - tap_col : 6 - tap_col + col_count
-                ]
-                * kernel[tap_row, tap_col]
-            )
-    grad_input = (cotangent.astype(F4) + back_conv).astype(BF)
-    grad_b_in = bias_rows.reshape(hidden_count)
+    got = fan(messages, "z", 2)
+    win_t, grad_w_out, small_grads, grad_b_in = local_call(
+        last_sum,
+        index,
+        [shape(units, channels), shape(units, channels), shape(53, channels), shape(hidden_count)],
+        total, shared, *got,
+    )
+    (grad_input,) = local_call(
+        conv_back,
+        index,
+        [shape(row_count, col_count, channels, dtype=BF)],
+        low_tall, *columns, taps, cotangent,
+        scratch=[pltpu.VMEM((row_count + 6, col_count + 16, channels), F4)],
+        flops=98 * pixels * channels,
+    )
     return (block_out, grad_input, win_t.T, grad_w_out, small_grads, grad_b_in)
 
 

time: 125 us -> 114 us (0.912)
  other arithmetic: 13 us -> 7.39 us
  local copies, waits for them, and re-layouts: 7.17 us -> 3.14 us
  Pallas kernels: 8.15 us -> 11.5 us
  starting transfers between devices: 51.1 us -> 48.7 us
  waiting for transfers between devices: 37.3 us -> 35.8 us
    convert_element_type x2 -> x0, other arithmetic: 4.31 us -> none  [the longest x1 4.18 us: on_device(): grad_input = (cotangent.astype(F4) + back_conv).astype(BF)]
    pallas_call x7, Pallas kernels: 8.15 us -> 11.5 us  [local_call(): pl.pallas_call(kernel, out_shape=outs, in_specs=[pl.BlockSpec(memory_spac...]
    ppermute x24 -> x25, starting transfers between devices: 43.8 us -> 41.4 us  [swap(): return lax.ppermute(x, axis, [(i, i ^ flip) for i in range(count)])]
    ppermute x24 -> x25, waiting for transfers between devices: 35.6 us -> 34.1 us  [swap(): return lax.ppermute(x, axis, [(i, i ^ flip) for i in range(count)])]
  transfers between devices with their start and end apart: 28 -> 29, of which waited for: 12 -> 15; matrix products, arithmetic and copies ran while one was open for 16% -> 10% of each run, Pallas kernels for 1% -> 5%
where the time goes in v3:
time: 114 us; the launch traced here: 113 us
  starting transfers between devices  48.7 us (43%)
  waiting for transfers between devices  35.8 us (31%)
  Pallas kernels  11.5 us (10%)
  other arithmetic  7.39 us (6%)
  matrix products  5.06 us (4%)
  local copies, waits for them, and re-layouts  3.14 us (3%)
  between operations  1.34 us (1%)
    ppermute x25, starting transfers between devices, swap(): return lax.ppermute(x, axis, [(i, i ^ flip) for i in range(count)])  41.4 us
    ppermute x25, waiting for transfers between devices, swap(): return lax.ppermute(x, axis, [(i, i ^ flip) for i in range(count)])  34.1 us
    pallas_call x7, Pallas kernels, local_call(): pl.pallas_call(kernel, out_shape=outs, in_specs=[pl.BlockSpec(memory_spac...  11.5 us
    ppermute x4, starting transfers between devices, outer_swap(): lax.ppermute(x, axis, [(i, (i + 1 ^ 1) - 1) for i in range(1, peers - 1)])  7.29 us
    reduce_sum x1, other arithmetic, on_device(): average = jnp.mean(conv, -1, keepdims=True)  3.15 us
  transfers between devices with their start and end apart: 29, of which 15 were waited for; matrix products, arithmetic and copies ran while one was open for 10% of the time, Pallas kernels for 5%

profile of v3, /device:TPU:6, one launch (start us, length us, event | category | flops | bytes accessed | tf_op | source)
XLA Modules:
  0.0 113.0 jit_solution(15104073968713918065)
XLA Ops:
  0.6 0.8 pad_maximum_fusion.13
  1.4 6.4 %collective-permute-start = (bf16[2,6,384]{2,1,0:T(8,128)(2,1)S(1)}, bf16[2,6,384]{2,1,0:T(8,128)(2,1)S(1)}, u32[]{:S(2)}, u32[]{:S(2)}) collective-permute-start(bf16[2,6,384]{2,1,0:T(8,128)(2,1)S(1)} %pad_maximum_fusion.13), channel_id=1, source_target_pairs={{0,192},{32,224},{64,128},{96,160},{128,64},{160,96},{192,0},{224,... | collective-permute-start | bytes 27656 | tf_op jit(solution)/shard_map/ppermute | solution.py:21
  7.8 1.0 collective-permute-start.1
  8.8 1.5 %collective-permute-start.2 = (bf16[2,6,384]{2,1,0:T(8,128)(2,1)S(1)}, bf16[2,6,384]{2,1,0:T(8,128)(2,1)S(1)}, u32[]{:S(2)}, u32[]{:S(2)}) collective-permute-start(bf16[2,6,384]{2,1,0:T(8,128)(2,1)S(1)} %pad_maximum_fusion.13), channel_id=1, source_target_pairs={{0,64},{32,96},{64,0},{96,32},{128,192},{160,224},{192,128},{224,1... | collective-permute-start | bytes 27656 | tf_op jit(solution)/shard_map/ppermute | solution.py:21
  10.2 0.9 broadcast_select_fusion.4
  11.2 0.7 collective-permute-start.5
  11.8 4.6 %collective-permute-start.4 = (bf16[3,32,384]{2,1,0:T(8,128)(2,1)S(1)}, bf16[3,32,384]{2,1,0:T(8,128)(2,1)S(1)}, u32[]{:S(2)}, u32[]{:S(2)}) collective-permute-start(bf16[3,32,384]{2,1,0:T(8,128)(2,1)S(1)} %get-tuple-element.148), channel_id=1, source_target_pairs={{0,8},{8,0},{16,24},{24,16},{32,40},{40,32},{48,56},{56,48},{64,72... | collective-permute-start | bytes 221192 | tf_op jit(solution)/shard_map/ppermute | solution.py:21
  16.5 0.7 broadcast_select_fusion.23
  17.3 1.1 collective-permute-start.3
  18.4 0.9 reshape.114
  19.4 0.2 reshape.115
  20.0 1.3 %collective-permute-done.3 = bf16[2,24,384]{2,1,0:T(8,128)(2,1)S(1)} collective-permute-done((bf16[2,24,384]{2,1,0:T(8,128)(2,1)S(1)}, bf16[2,24,384]{2,1,0:T(8,128)(2,1)S(1)}, u32[]{:S(2)}, u32[]{:S(2)}) %collective-permute-start.3) | collective-permute-done | bytes 36896 | tf_op jit(solution)/shard_map/ppermute | solution.py:21
  21.4 2.2 %collective-permute-start.7 = (bf16[2,48,384]{2,1,0:T(8,128)(2,1)S(1)}, bf16[2,48,384]{2,1,0:T(8,128)(2,1)S(1)}, u32[]{:S(2)}, u32[]{:S(2)}) collective-permute-start(bf16[2,48,384]{2,1,0:T(8,128)(2,1)S(1)} %pad_maximum_fusion.11), channel_id=1, source_target_pairs={{0,16},{1,17},{16,0},{17,1},{2,18},{3,19},{18,2},{19,3},{4,20},{5,... | collective-permute-start | bytes 221192 | tf_op jit(solution)/shard_map/ppermute | solution.py:21
  23.6 1.3 %collective-permute-start.8 = (bf16[2,48,384]{2,1,0:T(8,128)(2,1)S(1)}, bf16[2,48,384]{2,1,0:T(8,128)(2,1)S(1)}, u32[]{:S(2)}, u32[]{:S(2)}) collective-permute-start(bf16[2,48,384]{2,1,0:T(8,128)(2,1)S(1)} %pad_maximum_fusion.11), channel_id=1, source_target_pairs={{0,17},{1,16},{16,1},{17,0},{2,19},{3,18},{18,3},{19,2},{4,21},{5,... | collective-permute-start | bytes 221192 | tf_op jit(solution)/shard_map/ppermute | solution.py:21
  25.1 0.2 collective-permute-start.6
  25.3 4.0 %collective-permute-start.9 = (bf16[14,3,384]{2,1,0:T(4,128)(2,1)S(1)}, bf16[14,3,384]{2,1,0:T(4,128)(2,1)S(1)}, u32[]{:S(2)}, u32[]{:S(2)}) collective-permute-start(bf16[14,3,384]{2,1,0:T(4,128)(2,1)S(1)} %get-tuple-element.145), channel_id=1, source_target_pairs={{1,2},{2,1},{3,4},{4,3},{5,6},{6,5},{9,10},{10,9},{11,12},{12,11},... | collective-permute-start | bytes 96776 | tf_op jit(solution)/shard_map/ppermute | solution.py:34
  29.4 0.9 collective-permute-done.6
  30.4 1.7 %collective-permute-done.9 = bf16[14,3,384]{2,1,0:T(4,128)(2,1)S(1)} collective-permute-done((bf16[14,3,384]{2,1,0:T(4,128)(2,1)S(1)}, bf16[14,3,384]{2,1,0:T(4,128)(2,1)S(1)}, u32[]{:S(2)}, u32[]{:S(2)}) %collective-permute-start.9) | collective-permute-done | bytes 32288 | tf_op jit(solution)/shard_map/ppermute | solution.py:34
  32.2 0.9 collective-permute-start.11
  33.2 0.7 collective-permute-start.12
  33.8 3.2 %collective-permute-start.13 = (bf16[2,192,384]{2,1,0:T(8,128)(2,1)S(1)}, bf16[2,192,384]{2,1,0:T(8,128)(2,1)S(1)}, u32[]{:S(2)}, u32[]{:S(2)}) collective-permute-start(bf16[2,192,384]{2,1,0:T(8,128)(2,1)S(1)} %constant_dynamic-update-slice_fusion.7), channel_id=1, source_target_pairs={{0,6},{2,4},{4,2},{6,0},{1,7},{3,5},{5,3},{7,1},{8,14},{10,12},{12... | collective-permute-start | bytes 884744 | tf_op jit(solution)/shard_map/ppermute | solution.py:21
  37.3 0.2 pad_maximum_fusion
  37.5 3.2 %fusion.67 = (f32[8,32]{1,0:T(8,128)S(1)}, f32[8,32,384]{2,1,0:T(8,128)S(1)}) fusion(f32[384]{0:T(512)S(1)} %get-tuple-element.89, f32[14,38,384]{2,1,0:T(8,128)S(1)} %get-tuple-element.140, f32[384]{0:T(512)S(1)} %get-tuple-element.90, f32[384]{0:T(512)S(1)} %get-tuple-element.91, f32[384]{0:T(512)S(1)} %get-tuple-element.92, ...), kind=kLoop, calls=%fused_computation.229 | loop fusion | flops 9633536 | bytes 19737088 | tf_op jit(solution)/shard_map/reduce_sum | solution.py:338
  40.7 0.2 multiply_reduce_fusion
  41.3 0.3 collective-permute-start.10
  41.9 3.1 %collective-permute-done.12 = bf16[2,192,384]{2,1,0:T(8,128)(2,1)S(1)} collective-permute-done((bf16[2,192,384]{2,1,0:T(8,128)(2,1)S(1)}, bf16[2,192,384]{2,1,0:T(8,128)(2,1)S(1)}, u32[]{:S(2)}, u32[]{:S(2)}) %collective-permute-start.12) | collective-permute-done | bytes 294944 | tf_op jit(solution)/shard_map/ppermute | solution.py:21
  45.0 2.2 %collective-permute-done.13 = bf16[2,192,384]{2,1,0:T(8,128)(2,1)S(1)} collective-permute-done((bf16[2,192,384]{2,1,0:T(8,128)(2,1)S(1)}, bf16[2,192,384]{2,1,0:T(8,128)(2,1)S(1)}, u32[]{:S(2)}, u32[]{:S(2)}) %collective-permute-start.13) | collective-permute-done | bytes 294944 | tf_op jit(solution)/shard_map/ppermute | solution.py:21
  47.3 0.7 multiply_convert_fusion
  48.0 0.9 convert_reduce_fusion
  48.9 0.6 fusion.7.normed_grad
  49.5 0.6 fusion.6.mixed
  50.2 0.8 pad_maximum_fusion.4
  51.0 0.2 broadcast_in_dim.56
  51.2 0.2 broadcast_in_dim.59
  51.4 1.8 %fusion.58.win = f32[768,384]{1,0:T(8,128)S(1)} fusion(bf16[512,768]{1,0:T(8,128)(2,1)} %copy-done.4, bf16[256,384]{1,0:T(8,128)(2,1)} %copy-done.9, bf16[256,384]{1,0:T(8,128)(2,1)S(1)} %bitcast.52), kind=kOutput, calls=%fused_computation.126 | convolution fusion | flops 302776320 | bytes 2359296 | tf_op jit(solution)/shard_map/dot_general | solution.py:357
  53.2 3.7 %shard_map.145 = (bf16[8,32,384]{2,1,0:T(8,128)(2,1)S(1)}, bf16[224,384]{1,0:T(8,128)(2,1)S(1)}, bf16[3,32,384]{2,1,0:T(8,128)(2,1)S(1)}, bf16[8,32,384]{2,1,0:T(8,128)(2,1)}) custom-call(s32[5]{0:T(128)S(1)} %stack.48.index, f32[512,384]{1,0:T(8,128)S(1)} %fusion.7.normed_grad, f32[512,384]{1,0:T(8,128)S(1)} %fusion.6.mixed, ...), custom_call_target="tpu_custom_call" | custom-call | flops 10813440 | bytes 3810816 | tf_op jit(solution)/shard_map/pallas_call | solution.py:94
  57.0 0.6 collective-permute-start.15
  57.6 0.6 fusion.59.wout
  58.2 0.4 collective-permute-done.15.theirs
  58.6 0.7 shard_map.146
  59.4 4.4 %collective-permute-start.20 = (bf16[448,384]{1,0:T(8,128)(2,1)S(1)}, bf16[448,384]{1,0:T(8,128)(2,1)S(1)}, u32[]{:S(2)}, u32[]{:S(2)}) collective-permute-start(bf16[448,384]{1,0:T(8,128)(2,1)S(1)} %get-tuple-element.69), channel_id=1, source_target_pairs={{0,4},{2,6},{4,0},{6,2},{1,5},{3,7},{5,1},{7,3},{8,12},{10,14},{12... | collective-permute-start | bytes 1032200 | tf_op jit(solution)/shard_map/ppermute | solution.py:21
  63.8 0.3 collective-permute-start.21
  64.1 6.2 %collective-permute-done.16.g1 = bf16[448,384]{1,0:T(8,128)(2,1)S(1)} collective-permute-done((bf16[448,384]{1,0:T(8,128)(2,1)S(1)}, bf16[448,384]{1,0:T(8,128)(2,1)S(1)}, u32[]{:S(2)}, u32[]{:S(2)}) %collective-permute-start.16) | collective-permute-done | bytes 344096 | tf_op jit(solution)/shard_map/ppermute | solution.py:21
  70.3 0.7 collective-permute-start.17
  71.0 8.6 %collective-permute-done.20.g2 = bf16[448,384]{1,0:T(8,128)(2,1)S(1)} collective-permute-done((bf16[448,384]{1,0:T(8,128)(2,1)S(1)}, bf16[448,384]{1,0:T(8,128)(2,1)S(1)}, u32[]{:S(2)}, u32[]{:S(2)}) %collective-permute-start.20) | collective-permute-done | bytes 344096 | tf_op jit(solution)/shard_map/ppermute | solution.py:21
  79.5 2.6 %collective-permute-done.21.g3 = bf16[448,384]{1,0:T(8,128)(2,1)S(1)} collective-permute-done((bf16[448,384]{1,0:T(8,128)(2,1)S(1)}, bf16[448,384]{1,0:T(8,128)(2,1)S(1)}, u32[]{:S(2)}, u32[]{:S(2)}) %collective-permute-start.21) | collective-permute-done | bytes 344096 | tf_op jit(solution)/shard_map/ppermute | solution.py:21
  82.1 0.8 shard_map.148
  82.9 0.9 collective-permute-start.22
  83.8 1.8 %collective-permute-start.23 = (bf16[160,384]{1,0:T(8,128)(2,1)S(1)}, bf16[160,384]{1,0:T(8,128)(2,1)S(1)}, u32[]{:S(2)}, u32[]{:S(2)}) collective-permute-start(bf16[160,384]{1,0:T(8,128)(2,1)S(1)} %get-tuple-element.74), channel_id=1, source_target_pairs={{0,16},{1,17},{16,0},{17,1},{2,18},{3,19},{18,2},{19,3},{4,20},{5,... | collective-permute-start | bytes 368648 | tf_op jit(solution)/shard_map/ppermute | solution.py:21
  85.6 2.1 %collective-permute-start.24 = (bf16[160,384]{1,0:T(8,128)(2,1)S(1)}, bf16[160,384]{1,0:T(8,128)(2,1)S(1)}, u32[]{:S(2)}, u32[]{:S(2)}) collective-permute-start(bf16[160,384]{1,0:T(8,128)(2,1)S(1)} %get-tuple-element.75), channel_id=1, source_target_pairs={{0,17},{1,16},{16,1},{17,0},{2,19},{3,18},{18,3},{19,2},{4,21},{5,... | collective-permute-start | bytes 368648 | tf_op jit(solution)/shard_map/ppermute | solution.py:21
  87.8 0.9 collective-permute-done.22.g1
  88.7 1.9 %collective-permute-done.23.g2 = bf16[160,384]{1,0:T(8,128)(2,1)S(1)} collective-permute-done((bf16[160,384]{1,0:T(8,128)(2,1)S(1)}, bf16[160,384]{1,0:T(8,128)(2,1)S(1)}, u32[]{:S(2)}, u32[]{:S(2)}) %collective-permute-start.23) | collective-permute-done | bytes 122912 | tf_op jit(solution)/shard_map/ppermute | solution.py:21
  90.6 1.7 %collective-permute-done.24.g3 = bf16[160,384]{1,0:T(8,128)(2,1)S(1)} collective-permute-done((bf16[160,384]{1,0:T(8,128)(2,1)S(1)}, bf16[160,384]{1,0:T(8,128)(2,1)S(1)}, u32[]{:S(2)}, u32[]{:S(2)}) %collective-permute-start.24) | collective-permute-done | bytes 122912 | tf_op jit(solution)/shard_map/ppermute | solution.py:21
  92.3 0.6 shard_map.149
  92.9 1.2 %collective-permute-start.25 = (bf16[192,384]{1,0:T(8,128)(2,1)S(1)}, bf16[192,384]{1,0:T(8,128)(2,1)S(1)}, u32[]{:S(2)}, u32[]{:S(2)}) collective-permute-start(bf16[192,384]{1,0:T(8,128)(2,1)S(1)} %get-tuple-element.78), channel_id=1, source_target_pairs={{0,32},{32,0},{64,96},{96,64},{128,160},{160,128},{192,224},{224,1... | collective-permute-start | bytes 442376 | tf_op jit(solution)/shard_map/ppermute | solution.py:21
  94.2 1.9 %collective-permute-start.19 = (bf16[14,3,384]{2,1,0:T(4,128)(2,1)S(1)}, bf16[14,3,384]{2,1,0:T(4,128)(2,1)S(1)}, u32[]{:S(2)}, u32[]{:S(2)}) collective-permute-start(bf16[14,3,384]{2,1,0:T(4,128)(2,1)S(1)} %get-tuple-element.143), channel_id=1, source_target_pairs={{1,2},{2,1},{3,4},{4,3},{5,6},{6,5},{9,10},{10,9},{11,12},{12,11},... | collective-permute-start | bytes 96776 | tf_op jit(solution)/shard_map/ppermute | solution.py:34
  96.2 1.9 %collective-permute-done.25.got = bf16[192,384]{1,0:T(8,128)(2,1)S(1)} collective-permute-done((bf16[192,384]{1,0:T(8,128)(2,1)S(1)}, bf16[192,384]{1,0:T(8,128)(2,1)S(1)}, u32[]{:S(2)}, u32[]{:S(2)}) %collective-permute-start.25) | collective-permute-done | bytes 147488 | tf_op jit(solution)/shard_map/ppermute | solution.py:21
  98.2 0.6 shard_map.150
  98.8 2.9 %collective-permute-start.26 = (bf16[96,384]{1,0:T(8,128)(2,1)S(1)}, bf16[96,384]{1,0:T(8,128)(2,1)S(1)}, u32[]{:S(2)}, u32[]{:S(2)}) collective-permute-start(bf16[96,384]{1,0:T(8,128)(2,1)S(1)} %get-tuple-element.81), channel_id=1, source_target_pairs={{0,64},{32,96},{64,0},{96,32},{128,192},{160,224},{192,128},{224,1... | collective-permute-start | bytes 221192 | tf_op jit(solution)/shard_map/ppermute | solution.py:21
  101.6 3.6 %collective-permute-start.27 = (bf16[96,384]{1,0:T(8,128)(2,1)S(1)}, bf16[96,384]{1,0:T(8,128)(2,1)S(1)}, u32[]{:S(2)}, u32[]{:S(2)}) collective-permute-start(bf16[96,384]{1,0:T(8,128)(2,1)S(1)} %get-tuple-element.82), channel_id=1, source_target_pairs={{0,128},{32,160},{64,192},{96,224},{128,0},{160,32},{192,64},{224,... | collective-permute-start | bytes 221192 | tf_op jit(solution)/shard_map/ppermute | solution.py:21
  105.4 3.9 %shard_map.147 = bf16[8,32,384]{2,1,0:T(8,128)(2,1)} custom-call(s32[5]{0:T(128)S(1)} %stack.48.index, bf16[14,32,384]{2,1,0:T(8,128)(2,1)S(1)} %pad_maximum_fusion.5.tall, bf16[14,3,384]{2,1,0:T(4,128)(2,1)S(1)} %get-tuple-element.154.left, bf16[14,3,384]{2,1,0:T(4,128)(2,1)S(1)} %get-tuple-element.153.right, f32[49,384]{1,0:T(8,128)S(1)} %reshape.117.taps, ...), custom_call_target="tpu_custom_call" | custom-call | flops 9633792 | bytes 877056 | tf_op jit(solution)/shard_map/pallas_call | solution.py:94
  109.3 0.7 collective-permute-done.27.g2
  110.0 1.7 %collective-permute-done.28.g3 = bf16[96,384]{1,0:T(8,128)(2,1)S(1)} collective-permute-done((bf16[96,384]{1,0:T(8,128)(2,1)S(1)}, bf16[96,384]{1,0:T(8,128)(2,1)S(1)}, u32[]{:S(2)}, u32[]{:S(2)}) %collective-permute-start.28) | collective-permute-done | bytes 73760 | tf_op jit(solution)/shard_map/ppermute | solution.py:21
  111.7 1.2 %shard_map.151 = (f32[6,384]{1,0:T(8,128)}, f32[6,384]{1,0:T(8,128)}, f32[53,384]{1,0:T(8,128)}, f32[1536]{0:T(1024)}) custom-call(s32[5]{0:T(128)S(1)} %stack.48.index, f32[2,24,384]{2,1,0:T(8,128)S(1)} %get-tuple-element.79.before, bf16[64,384]{1,0:T(8,128)(2,1)S(1)} %get-tuple-element.80.mine, bf16[96,384]{1,0:T(8,128)(2,1)S(1)} %collective-permute-done.26.g1, ...), custom_call_target="tpu_custom_call" | custom-call | flops 1000000 | bytes 450048 | tf_op jit(solution)/shard_map/pallas_call | solution.py:94
  (104 shorter events, 2.7 us)
Async XLA Ops:
  0.6 24.2 %copy-start.1 = (bf16[8,32,384]{2,1,0:T(8,128)(2,1)S(1)}, bf16[8,32,384]{2,1,0:T(8,128)(2,1)}, u32[]{:S(2)}) copy-start(bf16[8,32,384]{2,1,0:T(8,128)(2,1)} %feature) | copy-start | bytes 589828
  1.4 15.1 %collective-permute-start = (bf16[2,6,384]{2,1,0:T(8,128)(2,1)S(1)}, bf16[2,6,384]{2,1,0:T(8,128)(2,1)S(1)}, u32[]{:S(2)}, u32[]{:S(2)}) collective-permute-start(bf16[2,6,384]{2,1,0:T(8,128)(2,1)S(1)} %pad_maximum_fusion.13), channel_id=1, source_target_pairs={{0,192},{32,224},{64,128},{96,160},{128,64},{160,96},{192,0},{224,... | collective-permute-start | bytes 27656 | tf_op jit(solution)/shard_map/ppermute | solution.py:21
  7.8 8.7 %collective-permute-start.1 = (bf16[2,6,384]{2,1,0:T(8,128)(2,1)S(1)}, bf16[2,6,384]{2,1,0:T(8,128)(2,1)S(1)}, u32[]{:S(2)}, u32[]{:S(2)}) collective-permute-start(bf16[2,6,384]{2,1,0:T(8,128)(2,1)S(1)} %pad_maximum_fusion.13), channel_id=1, source_target_pairs={{0,128},{32,160},{64,192},{96,224},{128,0},{160,32},{192,64},{224,... | collective-permute-start | bytes 27656 | tf_op jit(solution)/shard_map/ppermute | solution.py:21
  8.8 7.7 %collective-permute-start.2 = (bf16[2,6,384]{2,1,0:T(8,128)(2,1)S(1)}, bf16[2,6,384]{2,1,0:T(8,128)(2,1)S(1)}, u32[]{:S(2)}, u32[]{:S(2)}) collective-permute-start(bf16[2,6,384]{2,1,0:T(8,128)(2,1)S(1)} %pad_maximum_fusion.13), channel_id=1, source_target_pairs={{0,64},{32,96},{64,0},{96,32},{128,192},{160,224},{192,128},{224,1... | collective-permute-start | bytes 27656 | tf_op jit(solution)/shard_map/ppermute | solution.py:21
  11.2 10.2 %collective-permute-start.5 = (bf16[3,32,384]{2,1,0:T(8,128)(2,1)S(1)}, bf16[3,32,384]{2,1,0:T(8,128)(2,1)S(1)}, u32[]{:S(2)}, u32[]{:S(2)}) collective-permute-start(bf16[3,32,384]{2,1,0:T(8,128)(2,1)S(1)} %get-tuple-element.147), channel_id=1, source_target_pairs={{8,16},{16,8},{24,32},{32,24},{40,48},{48,40},{56,64},{64,56},{72,... | collective-permute-start | bytes 221192 | tf_op jit(solution)/shard_map/ppermute | solution.py:34
  11.8 9.5 %collective-permute-start.4 = (bf16[3,32,384]{2,1,0:T(8,128)(2,1)S(1)}, bf16[3,32,384]{2,1,0:T(8,128)(2,1)S(1)}, u32[]{:S(2)}, u32[]{:S(2)}) collective-permute-start(bf16[3,32,384]{2,1,0:T(8,128)(2,1)S(1)} %get-tuple-element.148), channel_id=1, source_target_pairs={{0,8},{8,0},{16,24},{24,16},{32,40},{40,32},{48,56},{56,48},{64,72... | collective-permute-start | bytes 221192 | tf_op jit(solution)/shard_map/ppermute | solution.py:21
  17.3 4.0 %collective-permute-start.3 = (bf16[2,24,384]{2,1,0:T(8,128)(2,1)S(1)}, bf16[2,24,384]{2,1,0:T(8,128)(2,1)S(1)}, u32[]{:S(2)}, u32[]{:S(2)}) collective-permute-start(bf16[2,24,384]{2,1,0:T(8,128)(2,1)S(1)} %pad_maximum_fusion.12), channel_id=1, source_target_pairs={{0,32},{32,0},{64,96},{96,64},{128,160},{160,128},{192,224},{224,1... | collective-permute-start | bytes 110600 | tf_op jit(solution)/shard_map/ppermute | solution.py:21
  20.0 17.0 %copy-start.10 = (f32[7,7,384]{2,1,0:T(8,128)S(1)}, f32[7,7,384]{2,1,0:T(8,128)}, u32[]{:S(2)}) copy-start(f32[7,7,384]{2,1,0:T(8,128)} %param.11) | copy-start | bytes 225796
  21.3 16.0 %copy-start = (bf16[8,32,384]{2,1,0:T(8,128)(2,1)S(1)}, bf16[8,32,384]{2,1,0:T(8,128)(2,1)}, u32[]{:S(2)}) copy-start(bf16[8,32,384]{2,1,0:T(8,128)(2,1)} %cot.1) | copy-start | bytes 589828
  21.4 10.7 %collective-permute-start.7 = (bf16[2,48,384]{2,1,0:T(8,128)(2,1)S(1)}, bf16[2,48,384]{2,1,0:T(8,128)(2,1)S(1)}, u32[]{:S(2)}, u32[]{:S(2)}) collective-permute-start(bf16[2,48,384]{2,1,0:T(8,128)(2,1)S(1)} %pad_maximum_fusion.11), channel_id=1, source_target_pairs={{0,16},{1,17},{16,0},{17,1},{2,18},{3,19},{18,2},{19,3},{4,20},{5,... | collective-permute-start | bytes 221192 | tf_op jit(solution)/shard_map/ppermute | solution.py:21
  23.6 8.6 %collective-permute-start.8 = (bf16[2,48,384]{2,1,0:T(8,128)(2,1)S(1)}, bf16[2,48,384]{2,1,0:T(8,128)(2,1)S(1)}, u32[]{:S(2)}, u32[]{:S(2)}) collective-permute-start(bf16[2,48,384]{2,1,0:T(8,128)(2,1)S(1)} %pad_maximum_fusion.11), channel_id=1, source_target_pairs={{0,17},{1,16},{16,1},{17,0},{2,19},{3,18},{18,3},{19,2},{4,21},{5,... | collective-permute-start | bytes 221192 | tf_op jit(solution)/shard_map/ppermute | solution.py:21
  25.1 5.3 %collective-permute-start.6 = (bf16[138,384]{1,0:T(8,128)(2,1)S(1)}, bf16[138,384]{1,0:T(8,128)(2,1)S(1)}, u32[]{:S(2)}, u32[]{:S(2)}) collective-permute-start(bf16[138,384]{1,0:T(8,128)(2,1)S(1)} %pad_maximum_fusion.10), channel_id=1, source_target_pairs={{0,1},{1,0},{16,17},{17,16},{2,3},{3,2},{18,19},{19,18},{4,5},{5,4... | collective-permute-start | bytes 317960 | tf_op jit(solution)/shard_map/ppermute | solution.py:21
  25.3 6.8 %collective-permute-start.9 = (bf16[14,3,384]{2,1,0:T(4,128)(2,1)S(1)}, bf16[14,3,384]{2,1,0:T(4,128)(2,1)S(1)}, u32[]{:S(2)}, u32[]{:S(2)}) collective-permute-start(bf16[14,3,384]{2,1,0:T(4,128)(2,1)S(1)} %get-tuple-element.145), channel_id=1, source_target_pairs={{1,2},{2,1},{3,4},{4,3},{5,6},{6,5},{9,10},{10,9},{11,12},{12,11},... | collective-permute-start | bytes 96776 | tf_op jit(solution)/shard_map/ppermute | solution.py:34
  32.2 9.6 %collective-permute-start.11 = (bf16[2,192,384]{2,1,0:T(8,128)(2,1)S(1)}, bf16[2,192,384]{2,1,0:T(8,128)(2,1)S(1)}, u32[]{:S(2)}, u32[]{:S(2)}) collective-permute-start(bf16[2,192,384]{2,1,0:T(8,128)(2,1)S(1)} %constant_dynamic-update-slice_fusion.7), channel_id=1, source_target_pairs={{0,2},{2,0},{4,6},{6,4},{1,3},{3,1},{5,7},{7,5},{8,10},{10,8},{12,... | collective-permute-start | bytes 884744 | tf_op jit(solution)/shard_map/ppermute | solution.py:21
  33.2 11.8 %collective-permute-start.12 = (bf16[2,192,384]{2,1,0:T(8,128)(2,1)S(1)}, bf16[2,192,384]{2,1,0:T(8,128)(2,1)S(1)}, u32[]{:S(2)}, u32[]{:S(2)}) collective-permute-start(bf16[2,192,384]{2,1,0:T(8,128)(2,1)S(1)} %constant_dynamic-update-slice_fusion.7), channel_id=1, source_target_pairs={{0,4},{2,6},{4,0},{6,2},{1,5},{3,7},{5,1},{7,3},{8,12},{10,14},{12... | collective-permute-start | bytes 884744 | tf_op jit(solution)/shard_map/ppermute | solution.py:21
  33.8 13.4 %collective-permute-start.13 = (bf16[2,192,384]{2,1,0:T(8,128)(2,1)S(1)}, bf16[2,192,384]{2,1,0:T(8,128)(2,1)S(1)}, u32[]{:S(2)}, u32[]{:S(2)}) collective-permute-start(bf16[2,192,384]{2,1,0:T(8,128)(2,1)S(1)} %constant_dynamic-update-slice_fusion.7), channel_id=1, source_target_pairs={{0,6},{2,4},{4,2},{6,0},{1,7},{3,5},{5,3},{7,1},{8,14},{10,12},{12... | collective-permute-start | bytes 884744 | tf_op jit(solution)/shard_map/ppermute | solution.py:21
  37.5 3.4 %copy-start.12 = (f32[384]{0:T(512)S(1)}, f32[384]{0:T(512)}, u32[]{:S(2)}) copy-start(f32[384]{0:T(512)} %param.18) | copy-start | bytes 4612
  37.5 3.4 %copy-start.13 = (f32[384]{0:T(512)S(1)}, f32[384]{0:T(512)}, u32[]{:S(2)}) copy-start(f32[384]{0:T(512)} %param.12) | copy-start | bytes 4612
  37.5 3.4 %copy-start.14 = (f32[384]{0:T(512)S(1)}, f32[384]{0:T(512)}, u32[]{:S(2)}) copy-start(f32[384]{0:T(512)} %param.13) | copy-start | bytes 4612
  41.1 0.7 copy-start.15
  41.2 6.8 %copy-start.5 = (bf16[256,384]{1,0:T(8,128)(2,1)}, bf16[256,384]{1,0:T(8,128)(2,1)S(1)}, u32[]{:S(2)}) copy-start(bf16[256,384]{1,0:T(8,128)(2,1)S(1)} %fusion.57) | copy-start | bytes 589828
  41.3 6.0 %collective-permute-start.10 = (bf16[2,256,384]{2,1,0:T(8,128)(2,1)S(1)}, bf16[2,256,384]{2,1,0:T(8,128)(2,1)S(1)}, u32[]{:S(2)}, u32[]{:S(2)}) collective-permute-start(bf16[2,256,384]{2,1,0:T(8,128)(2,1)S(1)} %pad_maximum_fusion.1), channel_id=1, source_target_pairs={{0,8},{8,0},{1,9},{9,1},{2,10},{10,2},{3,11},{11,3},{4,12},{12,4},... | collective-permute-start | bytes 1179656 | tf_op jit(solution)/shard_map/ppermute | solution.py:21
  47.3 0.7 copy-start.7
  47.3 1.6 %copy-start.9 = (bf16[256,384]{1,0:T(8,128)(2,1)}, bf16[256,384]{1,0:T(8,128)(2,1)S(1)}, u32[]{:S(2)}) copy-start(bf16[256,384]{1,0:T(8,128)(2,1)S(1)} %get-tuple-element.142) | copy-start | bytes 589828
  48.0 1.5 %copy-start.2 = (bf16[512,768]{1,0:T(8,128)(2,1)}, bf16[512,768]{1,0:T(8,128)(2,1)S(1)}, u32[]{:S(2)}) copy-start(bf16[512,768]{1,0:T(8,128)(2,1)S(1)} %get-tuple-element.163) | copy-start | bytes 2359300
  48.9 1.2 %copy-start.4 = (bf16[512,768]{1,0:T(8,128)(2,1)}, bf16[512,768]{1,0:T(8,128)(2,1)S(1)}, u32[]{:S(2)}) copy-start(bf16[512,768]{1,0:T(8,128)(2,1)S(1)} %get-tuple-element.166) | copy-start | bytes 2359300
  51.0 2.2 %collective-permute-start.14 = (bf16[2,256,384]{2,1,0:T(8,128)(2,1)}, bf16[2,256,384]{2,1,0:T(8,128)(2,1)S(1)}, u32[]{:S(2)}, u32[]{:S(2)}) collective-permute-start(bf16[2,256,384]{2,1,0:T(8,128)(2,1)} %pad_maximum_fusion.4), channel_id=1, source_target_pairs={{0,8},{8,0},{1,9},{9,1},{2,10},{10,2},{3,11},{11,3},{4,12},{12,4},... | collective-permute-start | bytes 1179656 | tf_op jit(solution)/shard_map/ppermute | solution.py:21
  53.2 4.4 %copy-start.3 = (bf16[512,768]{1,0:T(8,128)(2,1)S(1)}, bf16[512,768]{1,0:T(8,128)(2,1)}, u32[]{:S(2)}) copy-start(bf16[512,768]{1,0:T(8,128)(2,1)} %copy-done.2) | copy-start | bytes 2359300
  53.2 4.4 %copy-start.6 = (bf16[256,384]{1,0:T(8,128)(2,1)S(1)}, bf16[256,384]{1,0:T(8,128)(2,1)}, u32[]{:S(2)}) copy-start(bf16[256,384]{1,0:T(8,128)(2,1)} %copy-done.5) | copy-start | bytes 589828
  53.2 4.4 %copy-start.8 = (bf16[256,384]{1,0:T(8,128)(2,1)S(1)}, bf16[256,384]{1,0:T(8,128)(2,1)}, u32[]{:S(2)}) copy-start(bf16[256,384]{1,0:T(8,128)(2,1)} %copy-done.7) | copy-start | bytes 589828
  57.0 1.6 %collective-permute-start.15 = (bf16[224,384]{1,0:T(8,128)(2,1)S(1)}, bf16[224,384]{1,0:T(8,128)(2,1)S(1)}, u32[]{:S(2)}, u32[]{:S(2)}) collective-permute-start(bf16[224,384]{1,0:T(8,128)(2,1)S(1)} %get-tuple-element.62.mine), channel_id=1, source_target_pairs={{0,8},{8,0},{1,9},{9,1},{2,10},{10,2},{3,11},{11,3},{4,12},{12,4},... | collective-permute-start | bytes 516104 | tf_op jit(solution)/shard_map/ppermute | solution.py:21
  59.3 11.0 %collective-permute-start.16 = (bf16[448,384]{1,0:T(8,128)(2,1)S(1)}, bf16[448,384]{1,0:T(8,128)(2,1)S(1)}, u32[]{:S(2)}, u32[]{:S(2)}) collective-permute-start(bf16[448,384]{1,0:T(8,128)(2,1)S(1)} %get-tuple-element.63), channel_id=1, source_target_pairs={{0,2},{2,0},{4,6},{6,4},{1,3},{3,1},{5,7},{7,5},{8,10},{10,8},{12,... | collective-permute-start | bytes 1032200 | tf_op jit(solution)/shard_map/ppermute | solution.py:21
  59.4 20.1 %collective-permute-start.20 = (bf16[448,384]{1,0:T(8,128)(2,1)S(1)}, bf16[448,384]{1,0:T(8,128)(2,1)S(1)}, u32[]{:S(2)}, u32[]{:S(2)}) collective-permute-start(bf16[448,384]{1,0:T(8,128)(2,1)S(1)} %get-tuple-element.69), channel_id=1, source_target_pairs={{0,4},{2,6},{4,0},{6,2},{1,5},{3,7},{5,1},{7,3},{8,12},{10,14},{12... | collective-permute-start | bytes 1032200 | tf_op jit(solution)/shard_map/ppermute | solution.py:21
  63.8 18.3 %collective-permute-start.21 = (bf16[448,384]{1,0:T(8,128)(2,1)S(1)}, bf16[448,384]{1,0:T(8,128)(2,1)S(1)}, u32[]{:S(2)}, u32[]{:S(2)}) collective-permute-start(bf16[448,384]{1,0:T(8,128)(2,1)S(1)} %get-tuple-element.70), channel_id=1, source_target_pairs={{0,6},{2,4},{4,2},{6,0},{1,7},{3,5},{5,3},{7,1},{8,14},{10,12},{12... | collective-permute-start | bytes 1032200 | tf_op jit(solution)/shard_map/ppermute | solution.py:21
  70.3 17.4 %collective-permute-start.17 = (bf16[3,32,384]{2,1,0:T(8,128)(2,1)S(1)}, bf16[3,32,384]{2,1,0:T(8,128)(2,1)S(1)}, u32[]{:S(2)}, u32[]{:S(2)}) collective-permute-start(bf16[3,32,384]{2,1,0:T(8,128)(2,1)S(1)} %get-tuple-element.65), channel_id=1, source_target_pairs={{8,16},{16,8},{24,32},{32,24},{40,48},{48,40},{56,64},{64,56},{72,... | collective-permute-start | bytes 221192 | tf_op jit(solution)/shard_map/ppermute | solution.py:34
  82.9 13.3 %copy-start.11 = (f32[7,7,384]{2,1,0:T(8,128)S(1)}, f32[7,7,384]{2,1,0:T(8,128)}, u32[]{:S(2)}) copy-start(f32[7,7,384]{2,1,0:T(8,128)} %param.11) | copy-start | bytes 225796
  82.9 5.8 %collective-permute-start.22 = (bf16[160,384]{1,0:T(8,128)(2,1)S(1)}, bf16[160,384]{1,0:T(8,128)(2,1)S(1)}, u32[]{:S(2)}, u32[]{:S(2)}) collective-permute-start(bf16[160,384]{1,0:T(8,128)(2,1)S(1)} %get-tuple-element.73), channel_id=1, source_target_pairs={{0,1},{1,0},{16,17},{17,16},{2,3},{3,2},{18,19},{19,18},{4,5},{5,4... | collective-permute-start | bytes 368648 | tf_op jit(solution)/shard_map/ppermute | solution.py:21
  83.8 6.8 %collective-permute-start.23 = (bf16[160,384]{1,0:T(8,128)(2,1)S(1)}, bf16[160,384]{1,0:T(8,128)(2,1)S(1)}, u32[]{:S(2)}, u32[]{:S(2)}) collective-permute-start(bf16[160,384]{1,0:T(8,128)(2,1)S(1)} %get-tuple-element.74), channel_id=1, source_target_pairs={{0,16},{1,17},{16,0},{17,1},{2,18},{3,19},{18,2},{19,3},{4,20},{5,... | collective-permute-start | bytes 368648 | tf_op jit(solution)/shard_map/ppermute | solution.py:21
  85.6 6.7 %collective-permute-start.24 = (bf16[160,384]{1,0:T(8,128)(2,1)S(1)}, bf16[160,384]{1,0:T(8,128)(2,1)S(1)}, u32[]{:S(2)}, u32[]{:S(2)}) collective-permute-start(bf16[160,384]{1,0:T(8,128)(2,1)S(1)} %get-tuple-element.75), channel_id=1, source_target_pairs={{0,17},{1,16},{16,1},{17,0},{2,19},{3,18},{18,3},{19,2},{4,21},{5,... | collective-permute-start | bytes 368648 | tf_op jit(solution)/shard_map/ppermute | solution.py:21
  92.9 5.2 %collective-permute-start.25 = (bf16[192,384]{1,0:T(8,128)(2,1)S(1)}, bf16[192,384]{1,0:T(8,128)(2,1)S(1)}, u32[]{:S(2)}, u32[]{:S(2)}) collective-permute-start(bf16[192,384]{1,0:T(8,128)(2,1)S(1)} %get-tuple-element.78), channel_id=1, source_target_pairs={{0,32},{32,0},{64,96},{96,64},{128,160},{160,128},{192,224},{224,1... | collective-permute-start | bytes 442376 | tf_op jit(solution)/shard_map/ppermute | solution.py:21
  94.2 11.2 %collective-permute-start.19 = (bf16[14,3,384]{2,1,0:T(4,128)(2,1)S(1)}, bf16[14,3,384]{2,1,0:T(4,128)(2,1)S(1)}, u32[]{:S(2)}, u32[]{:S(2)}) collective-permute-start(bf16[14,3,384]{2,1,0:T(4,128)(2,1)S(1)} %get-tuple-element.143), channel_id=1, source_target_pairs={{1,2},{2,1},{3,4},{4,3},{5,6},{6,5},{9,10},{10,9},{11,12},{12,11},... | collective-permute-start | bytes 96776 | tf_op jit(solution)/shard_map/ppermute | solution.py:34
  96.1 9.2 %collective-permute-start.18 = (bf16[14,3,384]{2,1,0:T(4,128)(2,1)S(1)}, bf16[14,3,384]{2,1,0:T(4,128)(2,1)S(1)}, u32[]{:S(2)}, u32[]{:S(2)}) collective-permute-start(bf16[14,3,384]{2,1,0:T(4,128)(2,1)S(1)} %get-tuple-element.144), channel_id=1, source_target_pairs={{0,1},{1,0},{2,3},{3,2},{4,5},{5,4},{6,7},{7,6},{8,9},{9,8},{10,11... | collective-permute-start | bytes 96776 | tf_op jit(solution)/shard_map/ppermute | solution.py:21
  98.8 10.5 %collective-permute-start.26 = (bf16[96,384]{1,0:T(8,128)(2,1)S(1)}, bf16[96,384]{1,0:T(8,128)(2,1)S(1)}, u32[]{:S(2)}, u32[]{:S(2)}) collective-permute-start(bf16[96,384]{1,0:T(8,128)(2,1)S(1)} %get-tuple-element.81), channel_id=1, source_target_pairs={{0,64},{32,96},{64,0},{96,32},{128,192},{160,224},{192,128},{224,1... | collective-permute-start | bytes 221192 | tf_op jit(solution)/shard_map/ppermute | solution.py:21
  101.6 8.3 %collective-permute-start.27 = (bf16[96,384]{1,0:T(8,128)(2,1)S(1)}, bf16[96,384]{1,0:T(8,128)(2,1)S(1)}, u32[]{:S(2)}, u32[]{:S(2)}) collective-permute-start(bf16[96,384]{1,0:T(8,128)(2,1)S(1)} %get-tuple-element.82), channel_id=1, source_target_pairs={{0,128},{32,160},{64,192},{96,224},{128,0},{160,32},{192,64},{224,... | collective-permute-start | bytes 221192 | tf_op jit(solution)/shard_map/ppermute | solution.py:21
  105.3 6.5 %collective-permute-start.28 = (bf16[96,384]{1,0:T(8,128)(2,1)S(1)}, bf16[96,384]{1,0:T(8,128)(2,1)S(1)}, u32[]{:S(2)}, u32[]{:S(2)}) collective-permute-start(bf16[96,384]{1,0:T(8,128)(2,1)S(1)} %get-tuple-element.83), channel_id=1, source_target_pairs={{0,192},{32,224},{64,128},{96,160},{128,64},{160,96},{192,0},{224,... | collective-permute-start | bytes 221192 | tf_op jit(solution)/shard_map/ppermute | solution.py:21

commit v4 on v3

--- a/solution.py
+++ b/solution.py
@@ -75,16 +75,16 @@
 def quad_gather(x, axis, extra=None):
     me = lax.axis_index(axis)
     rows, channels = x.shape[1:]
-    others = []
-    for flip in (1, 2, 3):
+    others = {}
+    for flip in (1, 3, 2):
         if flip == 1 and extra is not None:
             got = swap(jnp.concatenate([x.reshape(2 * rows, channels), extra], 0), axis, flip)
-            others.append(got[: 2 * rows].reshape(x.shape))
+            others[flip] = got[: 2 * rows].reshape(x.shape)
             extra = got[2 * rows :]
         else:
-            others.append(swap(x, axis, flip))
+            others[flip] = swap(x, axis, flip)
     full = jnp.zeros((x.shape[0], 4 * rows, channels), x.dtype)
-    for flip, piece in zip((0, 1, 2, 3), [x] + others):
+    for flip, piece in ((0, x), (1, others[1]), (3, others[3]), (2, others[2])):
         full = lax.dynamic_update_slice_in_dim(full, piece, (me ^ flip) * rows, axis=1)
     return full if extra is None else (full, extra)
 
@@ -175,17 +175,17 @@
     outer[...] = jnp.where(odd, last, first).astype(BF)
 
 
-def first_fan(index, win, wout, mine, theirs, one, two, three, shared):
+def first_fan(index, win, wout, mine, theirs, one, three, two, shared):
     rows = win.shape[0] // 4
     shared[...] = (get_two(mine, 0) + get_two(theirs, 0)).astype(BF)
-    for flip, message in ((1, one), (2, two), (3, three)):
+    for flip, message in ((1, one), (3, three), (2, two)):
         at = pl.multiple_of((index[1] ^ flip) * rows, rows)
         message[0:rows, :] = win[pl.ds(at, rows), :].astype(BF)
         message[rows : 2 * rows, :] = wout[pl.ds(at, rows), :].astype(BF)
         message[2 * rows :, :] = shared[...]
 
 
-def second_fan(index, win, wout, mine, g1, g2, g3, total, one, two, three, shared):
+def second_fan(index, win, wout, mine, g1, g3, g2, total, one, three, two, shared):
     rows = win.shape[0] // 4
     at = pl.multiple_of(index[1] * rows, rows)
     for k, term in enumerate((win, wout)):
@@ -195,7 +195,7 @@
     small = tree([mine[...].astype(F4)] + [g[2 * rows :, :].astype(F4) for g in (g1, g2, g3)])
     shared[...] = small.astype(BF)
     part = rows // 4
-    for flip, message in ((1, one), (2, two), (3, three)):
+    for flip, message in ((1, one), (3, three), (2, two)):
         at = pl.multiple_of((index[2] ^ flip) * part, part)
         for k in range(2):
             message[k * part : (k + 1) * part, :] = total[k, pl.ds(at, part), :].astype(BF)
@@ -213,7 +213,7 @@
     message[k * block : k * block + half, :] = value.astype(BF)
 
 
-def third_fan(index, before, mine, g1, g2, g3, total, message, shared):
+def third_fan(index, before, mine, g1, g3, g2, total, message, shared):
     rows = before.shape[1] // 4
     at = pl.multiple_of(index[2] * rows, rows)
     for k in range(2):
@@ -234,7 +234,7 @@
     return jnp.where((which & 2) != 0, low[1], low[0])
 
 
-def fourth_fan(index, before, mine, got, total, one, two, three, shared):
+def fourth_fan(index, before, mine, got, total, one, three, two, shared):
     half = before.shape[1] // 2
     block = up16(half)
     bit = index[3] != 0
@@ -244,13 +244,13 @@
     shared[...] = (get_two(mine, 0) + get_two(got, 2 * block)).astype(BF)
     rows = half // 4
     block = up16(rows)
-    for flip, message in ((1, one), (2, two), (3, three)):
+    for flip, message in ((1, one), (3, three), (2, two)):
         for k in range(2):
             message[k * block : k * block + rows, :] = quarter(total, k, index[4] ^ flip).astype(BF)
         message[2 * block :, :] = shared[...]
 
 
-def last_sum(index, before, mine, g1, g2, g3, win, wout, small, bias):
+def last_sum(index, before, mine, g1, g3, g2, win, wout, small, bias):
     rows = before.shape[1] // 4
     block = up16(rows)
     for k, out in ((0, win), (1, wout)):
@@ -308,8 +308,8 @@
     outer_got = outer_swap(outer, COL)
     weights, inner_got = quad_gather(weights, Y, inner.reshape(-1, channels))
     columns = edge_order(inner_got.reshape(inner.shape), outer_got, COL)
-    weights, tall, columns, cotangent, kernel, ln_gain, layer_scale, b_out = lax.optimization_barrier(
-        (weights, tall, columns, cotangent, kernel, ln_gain, layer_scale, b_out)
+    weights, tall, cotangent, kernel, ln_gain, layer_scale, b_out = lax.optimization_barrier(
+        (weights, tall, cotangent, kernel, ln_gain, layer_scale, b_out)
     )
     weights = quad_gather(weights, "x")
     w_in_t, w_out_mine = weights[0], weights[1]
@@ -391,15 +391,14 @@
         return shape(2 * rows + smalls * SMALL, channels, dtype=BF)
 
     def fan(messages, axis, unit=1):
-        return [swap(m, axis, flip * unit) for m, flip in zip(messages, (1, 2, 3))]
+        return [swap(m, axis, flip * unit) for m, flip in zip(messages, (1, 3, 2))]
 
     piece = half // 4
     *messages, shared = local_call(
         first_fan, index, [message_of(piece)] * 3 + [small_shape], win_term, wout_term, mine, theirs
     )
+    messages[2], outer = lax.optimization_barrier((messages[2], outer))
     got = fan(messages, "x")
-    first_got, outer = lax.optimization_barrier((got[0], outer))
-    got[0] = first_got
     outer_got = outer_swap(outer, ROW)
     rows = edge_order(theirs[2 * SMALL :].reshape(3, col_count, channels), outer_got, ROW)
     low_tall = between(grad_low, rows, 0)

time: 114 us -> 111 us (0.974)
  waiting for transfers between devices: 35.8 us -> 33.4 us
  starting transfers between devices: 48.7 us -> 46.6 us
  local copies, waits for them, and re-layouts: 3.14 us -> 5.07 us
    dynamic_update_slice x8, local copies, waits for them, and re-layouts: 0.28 us -> 2.21 us  [quad_gather(): lax.dynamic_update_slice_in_dim(full, piece, (me ^ flip) * rows, axis=1)]
    ppermute x4, waiting for transfers between devices: 1.69 us -> 0.01 us  [outer_swap(): lax.ppermute(x, axis, [(i, (i + 1 ^ 1) - 1) for i in range(1, peers - 1)])]
    ppermute x4, starting transfers between devices: 7.29 us -> 6.08 us  [outer_swap(): lax.ppermute(x, axis, [(i, (i + 1 ^ 1) - 1) for i in range(1, peers - 1)])]
  transfers between devices with their start and end apart: 29 -> 29, of which waited for: 15 -> 11; matrix products, arithmetic and copies ran while one was open for 10% -> 12% of each run, Pallas kernels for 5% -> 5%
where the time goes in v4:
time: 111 us
  starting transfers between devices  46.6 us (42%)
  waiting for transfers between devices  33.4 us (30%)
  Pallas kernels  11.5 us (10%)
  other arithmetic  7.4 us (7%)
  local copies, waits for them, and re-layouts  5.07 us (5%)
  matrix products  5.05 us (5%)
  between operations  1.37 us (1%)
    ppermute x25, starting transfers between devices, swap(): return lax.ppermute(x, axis, [(i, i ^ flip) for i in range(count)])  40.6 us
    ppermute x25, waiting for transfers between devices, swap(): return lax.ppermute(x, axis, [(i, i ^ flip) for i in range(count)])  33.4 us
    pallas_call x7, Pallas kernels, local_call(): pl.pallas_call(kernel, out_shape=outs, in_specs=[pl.BlockSpec(memory_spac...  11.5 us
    ppermute x4, starting transfers between devices, outer_swap(): lax.ppermute(x, axis, [(i, (i + 1 ^ 1) - 1) for i in range(1, peers - 1)])  6.08 us
    reduce_sum x1, other arithmetic, on_device(): average = jnp.mean(conv, -1, keepdims=True)  3.15 us
  transfers between devices with their start and end apart: 29, of which 11 were waited for; matrix products, arithmetic and copies ran while one was open for 12% of the time, Pallas kernels for 5%

profile of v4, /device:TPU:6, one launch (start us, length us, event | category | flops | bytes accessed | tf_op | source)
XLA Modules:
  0.0 110.5 jit_solution(14142292745803441183)
XLA Ops:
  0.6 0.8 pad_maximum_fusion.13
  1.4 6.4 %collective-permute-start = (bf16[2,6,384]{2,1,0:T(8,128)(2,1)S(1)}, bf16[2,6,384]{2,1,0:T(8,128)(2,1)S(1)}, u32[]{:S(2)}, u32[]{:S(2)}) collective-permute-start(bf16[2,6,384]{2,1,0:T(8,128)(2,1)S(1)} %pad_maximum_fusion.13), channel_id=1, source_target_pairs={{0,192},{32,224},{64,128},{96,160},{128,64},{160,96},{192,0},{224,... | collective-permute-start | bytes 27656 | tf_op jit(solution)/shard_map/ppermute | solution.py:21
  7.8 1.0 collective-permute-start.1
  8.8 1.5 %collective-permute-start.2 = (bf16[2,6,384]{2,1,0:T(8,128)(2,1)S(1)}, bf16[2,6,384]{2,1,0:T(8,128)(2,1)S(1)}, u32[]{:S(2)}, u32[]{:S(2)}) collective-permute-start(bf16[2,6,384]{2,1,0:T(8,128)(2,1)S(1)} %pad_maximum_fusion.13), channel_id=1, source_target_pairs={{0,64},{32,96},{64,0},{96,32},{128,192},{160,224},{192,128},{224,1... | collective-permute-start | bytes 27656 | tf_op jit(solution)/shard_map/ppermute | solution.py:21
  10.2 0.9 broadcast_select_fusion.4
  11.2 0.7 collective-permute-start.5
  11.8 4.6 %collective-permute-start.4 = (bf16[3,32,384]{2,1,0:T(8,128)(2,1)S(1)}, bf16[3,32,384]{2,1,0:T(8,128)(2,1)S(1)}, u32[]{:S(2)}, u32[]{:S(2)}) collective-permute-start(bf16[3,32,384]{2,1,0:T(8,128)(2,1)S(1)} %get-tuple-element.144), channel_id=1, source_target_pairs={{0,8},{8,0},{16,24},{24,16},{32,40},{40,32},{48,56},{56,48},{64,72... | collective-permute-start | bytes 221192 | tf_op jit(solution)/shard_map/ppermute | solution.py:21
  16.5 0.7 broadcast_select_fusion.23
  17.3 1.1 collective-permute-start.3
  18.4 0.9 reshape.114
  19.4 0.2 reshape.115
  20.0 1.3 %collective-permute-done.3 = bf16[2,24,384]{2,1,0:T(8,128)(2,1)S(1)} collective-permute-done((bf16[2,24,384]{2,1,0:T(8,128)(2,1)S(1)}, bf16[2,24,384]{2,1,0:T(8,128)(2,1)S(1)}, u32[]{:S(2)}, u32[]{:S(2)}) %collective-permute-start.3) | collective-permute-done | bytes 36896 | tf_op jit(solution)/shard_map/ppermute | solution.py:21
  21.4 2.0 %collective-permute-start.7 = (bf16[2,48,384]{2,1,0:T(8,128)(2,1)S(1)}, bf16[2,48,384]{2,1,0:T(8,128)(2,1)S(1)}, u32[]{:S(2)}, u32[]{:S(2)}) collective-permute-start(bf16[2,48,384]{2,1,0:T(8,128)(2,1)S(1)} %pad_maximum_fusion.11), channel_id=1, source_target_pairs={{0,17},{1,16},{16,1},{17,0},{2,19},{3,18},{18,3},{19,2},{4,21},{5,... | collective-permute-start | bytes 221192 | tf_op jit(solution)/shard_map/ppermute | solution.py:21
  23.4 0.9 collective-permute-start.8
  24.5 1.4 %collective-permute-start.6 = (bf16[138,384]{1,0:T(8,128)(2,1)S(1)}, bf16[138,384]{1,0:T(8,128)(2,1)S(1)}, u32[]{:S(2)}, u32[]{:S(2)}) collective-permute-start(bf16[138,384]{1,0:T(8,128)(2,1)S(1)} %pad_maximum_fusion.10), channel_id=1, source_target_pairs={{0,1},{1,0},{16,17},{17,16},{2,3},{3,2},{18,19},{19,18},{4,5},{5,4... | collective-permute-start | bytes 317960 | tf_op jit(solution)/shard_map/ppermute | solution.py:21
  25.9 2.8 %collective-permute-start.9 = (bf16[14,3,384]{2,1,0:T(4,128)(2,1)S(1)}, bf16[14,3,384]{2,1,0:T(4,128)(2,1)S(1)}, u32[]{:S(2)}, u32[]{:S(2)}) collective-permute-start(bf16[14,3,384]{2,1,0:T(4,128)(2,1)S(1)} %get-tuple-element.141), channel_id=1, source_target_pairs={{1,2},{2,1},{3,4},{4,3},{5,6},{6,5},{9,10},{10,9},{11,12},{12,11},... | collective-permute-start | bytes 96776 | tf_op jit(solution)/shard_map/ppermute | solution.py:34
  28.8 0.5 collective-permute-done.6
  29.4 0.9 collective-permute-start.11
  30.3 1.1 %collective-permute-start.12 = (bf16[2,192,384]{2,1,0:T(8,128)(2,1)S(1)}, bf16[2,192,384]{2,1,0:T(8,128)(2,1)}, u32[]{:S(2)}, u32[]{:S(2)}) collective-permute-start(bf16[2,192,384]{2,1,0:T(8,128)(2,1)S(1)} %constant_dynamic-update-slice_fusion.7), channel_id=1, source_target_pairs={{0,6},{2,4},{4,2},{6,0},{1,7},{3,5},{5,3},{7,1},{8,14},{10,12},{12... | collective-permute-start | bytes 884744 | tf_op jit(solution)/shard_map/ppermute | solution.py:21
  31.5 2.1 %collective-permute-start.13 = (bf16[2,192,384]{2,1,0:T(8,128)(2,1)S(1)}, bf16[2,192,384]{2,1,0:T(8,128)(2,1)S(1)}, u32[]{:S(2)}, u32[]{:S(2)}) collective-permute-start(bf16[2,192,384]{2,1,0:T(8,128)(2,1)S(1)} %constant_dynamic-update-slice_fusion.7), channel_id=1, source_target_pairs={{0,4},{2,6},{4,0},{6,2},{1,5},{3,7},{5,1},{7,3},{8,12},{10,14},{12... | collective-permute-start | bytes 884744 | tf_op jit(solution)/shard_map/ppermute | solution.py:21
  34.0 0.2 pad_maximum_fusion
  34.2 3.2 %fusion.67 = (f32[8,32]{1,0:T(8,128)S(1)}, f32[8,32,384]{2,1,0:T(8,128)S(1)}) fusion(f32[384]{0:T(512)S(1)} %get-tuple-element.85, f32[14,38,384]{2,1,0:T(8,128)S(1)} %get-tuple-element.136, f32[384]{0:T(512)S(1)} %get-tuple-element.86, f32[384]{0:T(512)S(1)} %get-tuple-element.87, f32[384]{0:T(512)S(1)} %get-tuple-element.88, ...), kind=kLoop, calls=%fused_computation.229 | loop fusion | flops 9633536 | bytes 19737088 | tf_op jit(solution)/shard_map/reduce_sum | solution.py:338
  37.4 0.2 multiply_reduce_fusion
  37.6 0.1 add_convert_fusion
  37.9 0.3 collective-permute-start.10
  38.5 0.8 collective-permute-done.11
  39.3 1.0 constant_dynamic-update-slice_fusion.5
  40.3 3.9 %collective-permute-done.12 = bf16[2,192,384]{2,1,0:T(8,128)(2,1)} collective-permute-done((bf16[2,192,384]{2,1,0:T(8,128)(2,1)S(1)}, bf16[2,192,384]{2,1,0:T(8,128)(2,1)}, u32[]{:S(2)}, u32[]{:S(2)}) %collective-permute-start.12) | collective-permute-done | bytes 294944 | tf_op jit(solution)/shard_map/ppermute | solution.py:21
  44.2 1.0 constant_dynamic-update-slice_fusion.4
  45.4 0.7 multiply_convert_fusion
  46.1 0.9 convert_reduce_fusion
  47.0 0.6 fusion.7.normed_grad
  47.5 0.6 fusion.6.mixed
  48.2 0.8 pad_maximum_fusion.4
  49.0 0.2 broadcast_in_dim.56
  49.2 0.2 broadcast_in_dim.59
  49.4 1.8 %fusion.58.win = f32[768,384]{1,0:T(8,128)S(1)} fusion(bf16[512,768]{1,0:T(8,128)(2,1)} %copy-done.4, bf16[256,384]{1,0:T(8,128)(2,1)} %copy-done.9, bf16[256,384]{1,0:T(8,128)(2,1)S(1)} %bitcast.52), kind=kOutput, calls=%fused_computation.126 | convolution fusion | flops 302776320 | bytes 2359296 | tf_op jit(solution)/shard_map/dot_general | solution.py:357
  51.3 3.7 %shard_map.145 = (bf16[8,32,384]{2,1,0:T(8,128)(2,1)S(1)}, bf16[224,384]{1,0:T(8,128)(2,1)S(1)}, bf16[3,32,384]{2,1,0:T(8,128)(2,1)S(1)}, bf16[8,32,384]{2,1,0:T(8,128)(2,1)}) custom-call(s32[5]{0:T(128)S(1)} %stack.48.index, f32[512,384]{1,0:T(8,128)S(1)} %fusion.7.normed_grad, f32[512,384]{1,0:T(8,128)S(1)} %fusion.6.mixed, ...), custom_call_target="tpu_custom_call" | custom-call | flops 10813440 | bytes 3810816 | tf_op jit(solution)/shard_map/pallas_call | solution.py:94
  55.0 0.6 collective-permute-start.15
  55.6 0.6 fusion.59.wout
  56.2 0.4 collective-permute-done.15.theirs
  56.6 0.7 shard_map.146
  57.4 1.2 %collective-permute-start.20 = (bf16[448,384]{1,0:T(8,128)(2,1)S(1)}, bf16[448,384]{1,0:T(8,128)(2,1)S(1)}, u32[]{:S(2)}, u32[]{:S(2)}) collective-permute-start(bf16[448,384]{1,0:T(8,128)(2,1)S(1)} %get-tuple-element.65), channel_id=1, source_target_pairs={{0,6},{2,4},{4,2},{6,0},{1,7},{3,5},{5,3},{7,1},{8,14},{10,12},{12... | collective-permute-start | bytes 1032200 | tf_op jit(solution)/shard_map/ppermute | solution.py:21
  58.6 2.9 %collective-permute-start.21 = (bf16[448,384]{1,0:T(8,128)(2,1)S(1)}, bf16[448,384]{1,0:T(8,128)(2,1)S(1)}, u32[]{:S(2)}, u32[]{:S(2)}) collective-permute-start(bf16[448,384]{1,0:T(8,128)(2,1)S(1)} %get-tuple-element.66), channel_id=1, source_target_pairs={{0,4},{2,6},{4,0},{6,2},{1,5},{3,7},{5,1},{7,3},{8,12},{10,14},{12... | collective-permute-start | bytes 1032200 | tf_op jit(solution)/shard_map/ppermute | solution.py:21
  61.5 0.7 collective-permute-start.16
  62.2 6.1 %collective-permute-done.19.g1 = bf16[448,384]{1,0:T(8,128)(2,1)S(1)} collective-permute-done((bf16[448,384]{1,0:T(8,128)(2,1)S(1)}, bf16[448,384]{1,0:T(8,128)(2,1)S(1)}, u32[]{:S(2)}, u32[]{:S(2)}) %collective-permute-start.19) | collective-permute-done | bytes 344096 | tf_op jit(solution)/shard_map/ppermute | solution.py:21
  68.3 8.1 %collective-permute-done.20.g3 = bf16[448,384]{1,0:T(8,128)(2,1)S(1)} collective-permute-done((bf16[448,384]{1,0:T(8,128)(2,1)S(1)}, bf16[448,384]{1,0:T(8,128)(2,1)S(1)}, u32[]{:S(2)}, u32[]{:S(2)}) %collective-permute-start.20) | collective-permute-done | bytes 344096 | tf_op jit(solution)/shard_map/ppermute | solution.py:21
  76.4 0.8 shard_map.148
  77.2 1.5 %collective-permute-start.22 = (bf16[160,384]{1,0:T(8,128)(2,1)S(1)}, bf16[160,384]{1,0:T(8,128)(2,1)S(1)}, u32[]{:S(2)}, u32[]{:S(2)}) collective-permute-start(bf16[160,384]{1,0:T(8,128)(2,1)S(1)} %get-tuple-element.69), channel_id=1, source_target_pairs={{0,1},{1,0},{16,17},{17,16},{2,3},{3,2},{18,19},{19,18},{4,5},{5,4... | collective-permute-start | bytes 368648 | tf_op jit(solution)/shard_map/ppermute | solution.py:21
  78.7 1.4 %collective-permute-start.23 = (bf16[160,384]{1,0:T(8,128)(2,1)S(1)}, bf16[160,384]{1,0:T(8,128)(2,1)S(1)}, u32[]{:S(2)}, u32[]{:S(2)}) collective-permute-start(bf16[160,384]{1,0:T(8,128)(2,1)S(1)} %get-tuple-element.70), channel_id=1, source_target_pairs={{0,17},{1,16},{16,1},{17,0},{2,19},{3,18},{18,3},{19,2},{4,21},{5,... | collective-permute-start | bytes 368648 | tf_op jit(solution)/shard_map/ppermute | solution.py:21
  80.1 1.3 %collective-permute-start.24 = (bf16[160,384]{1,0:T(8,128)(2,1)S(1)}, bf16[160,384]{1,0:T(8,128)(2,1)S(1)}, u32[]{:S(2)}, u32[]{:S(2)}) collective-permute-start(bf16[160,384]{1,0:T(8,128)(2,1)S(1)} %get-tuple-element.71), channel_id=1, source_target_pairs={{0,16},{1,17},{16,0},{17,1},{2,18},{3,19},{18,2},{19,3},{4,20},{5,... | collective-permute-start | bytes 368648 | tf_op jit(solution)/shard_map/ppermute | solution.py:21
  81.5 0.7 collective-permute-done.22.g1
  82.2 4.7 %collective-permute-done.23.g3 = bf16[160,384]{1,0:T(8,128)(2,1)S(1)} collective-permute-done((bf16[160,384]{1,0:T(8,128)(2,1)S(1)}, bf16[160,384]{1,0:T(8,128)(2,1)S(1)}, u32[]{:S(2)}, u32[]{:S(2)}) %collective-permute-start.23) | collective-permute-done | bytes 122912 | tf_op jit(solution)/shard_map/ppermute | solution.py:21
  87.0 0.6 shard_map.149
  87.6 1.1 collective-permute-start.25
  88.8 1.9 %collective-permute-start.18 = (bf16[14,3,384]{2,1,0:T(4,128)(2,1)S(1)}, bf16[14,3,384]{2,1,0:T(4,128)(2,1)S(1)}, u32[]{:S(2)}, u32[]{:S(2)}) collective-permute-start(bf16[14,3,384]{2,1,0:T(4,128)(2,1)S(1)} %get-tuple-element.139), channel_id=1, source_target_pairs={{1,2},{2,1},{3,4},{4,3},{5,6},{6,5},{9,10},{10,9},{11,12},{12,11},... | collective-permute-start | bytes 96776 | tf_op jit(solution)/shard_map/ppermute | solution.py:34
  90.8 2.0 %collective-permute-done.25.got = bf16[192,384]{1,0:T(8,128)(2,1)S(1)} collective-permute-done((bf16[192,384]{1,0:T(8,128)(2,1)S(1)}, bf16[192,384]{1,0:T(8,128)(2,1)S(1)}, u32[]{:S(2)}, u32[]{:S(2)}) %collective-permute-start.25) | collective-permute-done | bytes 147488 | tf_op jit(solution)/shard_map/ppermute | solution.py:21
  92.8 0.6 shard_map.150
  93.5 3.4 %collective-permute-start.26 = (bf16[96,384]{1,0:T(8,128)(2,1)S(1)}, bf16[96,384]{1,0:T(8,128)(2,1)S(1)}, u32[]{:S(2)}, u32[]{:S(2)}) collective-permute-start(bf16[96,384]{1,0:T(8,128)(2,1)S(1)} %get-tuple-element.77), channel_id=1, source_target_pairs={{0,64},{32,96},{64,0},{96,32},{128,192},{160,224},{192,128},{224,1... | collective-permute-start | bytes 221192 | tf_op jit(solution)/shard_map/ppermute | solution.py:21
  96.9 3.3 %collective-permute-start.27 = (bf16[96,384]{1,0:T(8,128)(2,1)S(1)}, bf16[96,384]{1,0:T(8,128)(2,1)S(1)}, u32[]{:S(2)}, u32[]{:S(2)}) collective-permute-start(bf16[96,384]{1,0:T(8,128)(2,1)S(1)} %get-tuple-element.78), channel_id=1, source_target_pairs={{0,192},{32,224},{64,128},{96,160},{128,64},{160,96},{192,0},{224,... | collective-permute-start | bytes 221192 | tf_op jit(solution)/shard_map/ppermute | solution.py:21
  100.2 0.3 collective-permute-start.28
  100.6 3.9 %shard_map.147 = bf16[8,32,384]{2,1,0:T(8,128)(2,1)} custom-call(s32[5]{0:T(128)S(1)} %stack.48.index, bf16[14,32,384]{2,1,0:T(8,128)(2,1)S(1)} %pad_maximum_fusion.5.tall, bf16[14,3,384]{2,1,0:T(4,128)(2,1)S(1)} %get-tuple-element.150.left, bf16[14,3,384]{2,1,0:T(4,128)(2,1)S(1)} %get-tuple-element.149.right, f32[49,384]{1,0:T(8,128)S(1)} %reshape.117.taps, ...), custom_call_target="tpu_custom_call" | custom-call | flops 9633792 | bytes 877056 | tf_op jit(solution)/shard_map/pallas_call | solution.py:94
  104.5 4.8 %collective-permute-done.28.g2 = bf16[96,384]{1,0:T(8,128)(2,1)S(1)} collective-permute-done((bf16[96,384]{1,0:T(8,128)(2,1)S(1)}, bf16[96,384]{1,0:T(8,128)(2,1)S(1)}, u32[]{:S(2)}, u32[]{:S(2)}) %collective-permute-start.28) | collective-permute-done | bytes 73760 | tf_op jit(solution)/shard_map/ppermute | solution.py:21
  109.3 1.2 %shard_map.151 = (f32[6,384]{1,0:T(8,128)}, f32[6,384]{1,0:T(8,128)}, f32[53,384]{1,0:T(8,128)}, f32[1536]{0:T(1024)}) custom-call(s32[5]{0:T(128)S(1)} %stack.48.index, f32[2,24,384]{2,1,0:T(8,128)S(1)} %get-tuple-element.75.before, bf16[64,384]{1,0:T(8,128)(2,1)S(1)} %get-tuple-element.76.mine, bf16[96,384]{1,0:T(8,128)(2,1)S(1)} %collective-permute-done.26.g1, ...), custom_call_target="tpu_custom_call" | custom-call | flops 1000000 | bytes 450048 | tf_op jit(solution)/shard_map/pallas_call | solution.py:94
  (104 shorter events, 2.4 us)
Async XLA Ops:
  0.6 23.6 %copy-start.1 = (bf16[8,32,384]{2,1,0:T(8,128)(2,1)S(1)}, bf16[8,32,384]{2,1,0:T(8,128)(2,1)}, u32[]{:S(2)}) copy-start(bf16[8,32,384]{2,1,0:T(8,128)(2,1)} %feature) | copy-start | bytes 589828
  1.4 15.1 %collective-permute-start = (bf16[2,6,384]{2,1,0:T(8,128)(2,1)S(1)}, bf16[2,6,384]{2,1,0:T(8,128)(2,1)S(1)}, u32[]{:S(2)}, u32[]{:S(2)}) collective-permute-start(bf16[2,6,384]{2,1,0:T(8,128)(2,1)S(1)} %pad_maximum_fusion.13), channel_id=1, source_target_pairs={{0,192},{32,224},{64,128},{96,160},{128,64},{160,96},{192,0},{224,... | collective-permute-start | bytes 27656 | tf_op jit(solution)/shard_map/ppermute | solution.py:21
  7.8 8.7 %collective-permute-start.1 = (bf16[2,6,384]{2,1,0:T(8,128)(2,1)S(1)}, bf16[2,6,384]{2,1,0:T(8,128)(2,1)S(1)}, u32[]{:S(2)}, u32[]{:S(2)}) collective-permute-start(bf16[2,6,384]{2,1,0:T(8,128)(2,1)S(1)} %pad_maximum_fusion.13), channel_id=1, source_target_pairs={{0,128},{32,160},{64,192},{96,224},{128,0},{160,32},{192,64},{224,... | collective-permute-start | bytes 27656 | tf_op jit(solution)/shard_map/ppermute | solution.py:21
  8.8 7.7 %collective-permute-start.2 = (bf16[2,6,384]{2,1,0:T(8,128)(2,1)S(1)}, bf16[2,6,384]{2,1,0:T(8,128)(2,1)S(1)}, u32[]{:S(2)}, u32[]{:S(2)}) collective-permute-start(bf16[2,6,384]{2,1,0:T(8,128)(2,1)S(1)} %pad_maximum_fusion.13), channel_id=1, source_target_pairs={{0,64},{32,96},{64,0},{96,32},{128,192},{160,224},{192,128},{224,1... | collective-permute-start | bytes 27656 | tf_op jit(solution)/shard_map/ppermute | solution.py:21
  11.2 10.2 %collective-permute-start.5 = (bf16[3,32,384]{2,1,0:T(8,128)(2,1)S(1)}, bf16[3,32,384]{2,1,0:T(8,128)(2,1)S(1)}, u32[]{:S(2)}, u32[]{:S(2)}) collective-permute-start(bf16[3,32,384]{2,1,0:T(8,128)(2,1)S(1)} %get-tuple-element.143), channel_id=1, source_target_pairs={{8,16},{16,8},{24,32},{32,24},{40,48},{48,40},{56,64},{64,56},{72,... | collective-permute-start | bytes 221192 | tf_op jit(solution)/shard_map/ppermute | solution.py:34
  11.8 9.5 %collective-permute-start.4 = (bf16[3,32,384]{2,1,0:T(8,128)(2,1)S(1)}, bf16[3,32,384]{2,1,0:T(8,128)(2,1)S(1)}, u32[]{:S(2)}, u32[]{:S(2)}) collective-permute-start(bf16[3,32,384]{2,1,0:T(8,128)(2,1)S(1)} %get-tuple-element.144), channel_id=1, source_target_pairs={{0,8},{8,0},{16,24},{24,16},{32,40},{40,32},{48,56},{56,48},{64,72... | collective-permute-start | bytes 221192 | tf_op jit(solution)/shard_map/ppermute | solution.py:21
  17.3 4.0 %collective-permute-start.3 = (bf16[2,24,384]{2,1,0:T(8,128)(2,1)S(1)}, bf16[2,24,384]{2,1,0:T(8,128)(2,1)S(1)}, u32[]{:S(2)}, u32[]{:S(2)}) collective-permute-start(bf16[2,24,384]{2,1,0:T(8,128)(2,1)S(1)} %pad_maximum_fusion.12), channel_id=1, source_target_pairs={{0,32},{32,0},{64,96},{96,64},{128,160},{160,128},{192,224},{224,1... | collective-permute-start | bytes 110600 | tf_op jit(solution)/shard_map/ppermute | solution.py:21
  19.4 14.2 %copy-start.10 = (f32[7,7,384]{2,1,0:T(8,128)S(1)}, f32[7,7,384]{2,1,0:T(8,128)}, u32[]{:S(2)}) copy-start(f32[7,7,384]{2,1,0:T(8,128)} %param.11) | copy-start | bytes 225796
  19.4 14.4 %copy-start = (bf16[8,32,384]{2,1,0:T(8,128)(2,1)S(1)}, bf16[8,32,384]{2,1,0:T(8,128)(2,1)}, u32[]{:S(2)}) copy-start(bf16[8,32,384]{2,1,0:T(8,128)(2,1)} %cot.1) | copy-start | bytes 589828
  21.4 7.9 %collective-permute-start.7 = (bf16[2,48,384]{2,1,0:T(8,128)(2,1)S(1)}, bf16[2,48,384]{2,1,0:T(8,128)(2,1)S(1)}, u32[]{:S(2)}, u32[]{:S(2)}) collective-permute-start(bf16[2,48,384]{2,1,0:T(8,128)(2,1)S(1)} %pad_maximum_fusion.11), channel_id=1, source_target_pairs={{0,17},{1,16},{16,1},{17,0},{2,19},{3,18},{18,3},{19,2},{4,21},{5,... | collective-permute-start | bytes 221192 | tf_op jit(solution)/shard_map/ppermute | solution.py:21
  23.4 6.0 %collective-permute-start.8 = (bf16[2,48,384]{2,1,0:T(8,128)(2,1)S(1)}, bf16[2,48,384]{2,1,0:T(8,128)(2,1)S(1)}, u32[]{:S(2)}, u32[]{:S(2)}) collective-permute-start(bf16[2,48,384]{2,1,0:T(8,128)(2,1)S(1)} %pad_maximum_fusion.11), channel_id=1, source_target_pairs={{0,16},{1,17},{16,0},{17,1},{2,18},{3,19},{18,2},{19,3},{4,20},{5,... | collective-permute-start | bytes 221192 | tf_op jit(solution)/shard_map/ppermute | solution.py:21
  24.5 4.8 %collective-permute-start.6 = (bf16[138,384]{1,0:T(8,128)(2,1)S(1)}, bf16[138,384]{1,0:T(8,128)(2,1)S(1)}, u32[]{:S(2)}, u32[]{:S(2)}) collective-permute-start(bf16[138,384]{1,0:T(8,128)(2,1)S(1)} %pad_maximum_fusion.10), channel_id=1, source_target_pairs={{0,1},{1,0},{16,17},{17,16},{2,3},{3,2},{18,19},{19,18},{4,5},{5,4... | collective-permute-start | bytes 317960 | tf_op jit(solution)/shard_map/ppermute | solution.py:21
  25.9 8.0 %collective-permute-start.9 = (bf16[14,3,384]{2,1,0:T(4,128)(2,1)S(1)}, bf16[14,3,384]{2,1,0:T(4,128)(2,1)S(1)}, u32[]{:S(2)}, u32[]{:S(2)}) collective-permute-start(bf16[14,3,384]{2,1,0:T(4,128)(2,1)S(1)} %get-tuple-element.141), channel_id=1, source_target_pairs={{1,2},{2,1},{3,4},{4,3},{5,6},{6,5},{9,10},{10,9},{11,12},{12,11},... | collective-permute-start | bytes 96776 | tf_op jit(solution)/shard_map/ppermute | solution.py:34
  29.4 9.9 %collective-permute-start.11 = (bf16[2,192,384]{2,1,0:T(8,128)(2,1)S(1)}, bf16[2,192,384]{2,1,0:T(8,128)(2,1)}, u32[]{:S(2)}, u32[]{:S(2)}) collective-permute-start(bf16[2,192,384]{2,1,0:T(8,128)(2,1)S(1)} %constant_dynamic-update-slice_fusion.7), channel_id=1, source_target_pairs={{0,2},{2,0},{4,6},{6,4},{1,3},{3,1},{5,7},{7,5},{8,10},{10,8},{12,... | collective-permute-start | bytes 884744 | tf_op jit(solution)/shard_map/ppermute | solution.py:21
  30.3 13.9 %collective-permute-start.12 = (bf16[2,192,384]{2,1,0:T(8,128)(2,1)S(1)}, bf16[2,192,384]{2,1,0:T(8,128)(2,1)}, u32[]{:S(2)}, u32[]{:S(2)}) collective-permute-start(bf16[2,192,384]{2,1,0:T(8,128)(2,1)S(1)} %constant_dynamic-update-slice_fusion.7), channel_id=1, source_target_pairs={{0,6},{2,4},{4,2},{6,0},{1,7},{3,5},{5,3},{7,1},{8,14},{10,12},{12... | collective-permute-start | bytes 884744 | tf_op jit(solution)/shard_map/ppermute | solution.py:21
  31.5 13.7 %collective-permute-start.13 = (bf16[2,192,384]{2,1,0:T(8,128)(2,1)S(1)}, bf16[2,192,384]{2,1,0:T(8,128)(2,1)S(1)}, u32[]{:S(2)}, u32[]{:S(2)}) collective-permute-start(bf16[2,192,384]{2,1,0:T(8,128)(2,1)S(1)} %constant_dynamic-update-slice_fusion.7), channel_id=1, source_target_pairs={{0,4},{2,6},{4,0},{6,2},{1,5},{3,7},{5,1},{7,3},{8,12},{10,14},{12... | collective-permute-start | bytes 884744 | tf_op jit(solution)/shard_map/ppermute | solution.py:21
  34.2 3.4 %copy-start.12 = (f32[384]{0:T(512)S(1)}, f32[384]{0:T(512)}, u32[]{:S(2)}) copy-start(f32[384]{0:T(512)} %param.18) | copy-start | bytes 4612
  34.2 3.4 %copy-start.13 = (f32[384]{0:T(512)S(1)}, f32[384]{0:T(512)}, u32[]{:S(2)}) copy-start(f32[384]{0:T(512)} %param.12) | copy-start | bytes 4612
  34.2 3.4 %copy-start.14 = (f32[384]{0:T(512)S(1)}, f32[384]{0:T(512)}, u32[]{:S(2)}) copy-start(f32[384]{0:T(512)} %param.13) | copy-start | bytes 4612
  37.8 0.7 copy-start.15
  37.8 8.2 %copy-start.5 = (bf16[256,384]{1,0:T(8,128)(2,1)}, bf16[256,384]{1,0:T(8,128)(2,1)S(1)}, u32[]{:S(2)}) copy-start(bf16[256,384]{1,0:T(8,128)(2,1)S(1)} %fusion.57) | copy-start | bytes 589828
  37.9 7.4 %collective-permute-start.10 = (bf16[2,256,384]{2,1,0:T(8,128)(2,1)S(1)}, bf16[2,256,384]{2,1,0:T(8,128)(2,1)S(1)}, u32[]{:S(2)}, u32[]{:S(2)}) collective-permute-start(bf16[2,256,384]{2,1,0:T(8,128)(2,1)S(1)} %pad_maximum_fusion.1), channel_id=1, source_target_pairs={{0,8},{8,0},{1,9},{9,1},{2,10},{10,2},{3,11},{11,3},{4,12},{12,4},... | collective-permute-start | bytes 1179656 | tf_op jit(solution)/shard_map/ppermute | solution.py:21
  45.3 0.7 copy-start.7
  45.3 1.6 %copy-start.9 = (bf16[256,384]{1,0:T(8,128)(2,1)}, bf16[256,384]{1,0:T(8,128)(2,1)S(1)}, u32[]{:S(2)}) copy-start(bf16[256,384]{1,0:T(8,128)(2,1)S(1)} %get-tuple-element.138) | copy-start | bytes 589828
  46.0 1.5 %copy-start.2 = (bf16[512,768]{1,0:T(8,128)(2,1)}, bf16[512,768]{1,0:T(8,128)(2,1)S(1)}, u32[]{:S(2)}) copy-start(bf16[512,768]{1,0:T(8,128)(2,1)S(1)} %get-tuple-element.159) | copy-start | bytes 2359300
  46.9 1.2 %copy-start.4 = (bf16[512,768]{1,0:T(8,128)(2,1)}, bf16[512,768]{1,0:T(8,128)(2,1)S(1)}, u32[]{:S(2)}) copy-start(bf16[512,768]{1,0:T(8,128)(2,1)S(1)} %get-tuple-element.162) | copy-start | bytes 2359300
  49.0 2.2 %collective-permute-start.14 = (bf16[2,256,384]{2,1,0:T(8,128)(2,1)}, bf16[2,256,384]{2,1,0:T(8,128)(2,1)S(1)}, u32[]{:S(2)}, u32[]{:S(2)}) collective-permute-start(bf16[2,256,384]{2,1,0:T(8,128)(2,1)} %pad_maximum_fusion.4), channel_id=1, source_target_pairs={{0,8},{8,0},{1,9},{9,1},{2,10},{10,2},{3,11},{11,3},{4,12},{12,4},... | collective-permute-start | bytes 1179656 | tf_op jit(solution)/shard_map/ppermute | solution.py:21
  51.2 4.4 %copy-start.3 = (bf16[512,768]{1,0:T(8,128)(2,1)S(1)}, bf16[512,768]{1,0:T(8,128)(2,1)}, u32[]{:S(2)}) copy-start(bf16[512,768]{1,0:T(8,128)(2,1)} %copy-done.2) | copy-start | bytes 2359300
  51.2 4.4 %copy-start.6 = (bf16[256,384]{1,0:T(8,128)(2,1)S(1)}, bf16[256,384]{1,0:T(8,128)(2,1)}, u32[]{:S(2)}) copy-start(bf16[256,384]{1,0:T(8,128)(2,1)} %copy-done.5) | copy-start | bytes 589828
  51.2 4.3 %copy-start.8 = (bf16[256,384]{1,0:T(8,128)(2,1)S(1)}, bf16[256,384]{1,0:T(8,128)(2,1)}, u32[]{:S(2)}) copy-start(bf16[256,384]{1,0:T(8,128)(2,1)} %copy-done.7) | copy-start | bytes 589828
  55.0 1.6 %collective-permute-start.15 = (bf16[224,384]{1,0:T(8,128)(2,1)S(1)}, bf16[224,384]{1,0:T(8,128)(2,1)S(1)}, u32[]{:S(2)}, u32[]{:S(2)}) collective-permute-start(bf16[224,384]{1,0:T(8,128)(2,1)S(1)} %get-tuple-element.58.mine), channel_id=1, source_target_pairs={{0,8},{8,0},{1,9},{9,1},{2,10},{10,2},{3,11},{11,3},{4,12},{12,4},... | collective-permute-start | bytes 516104 | tf_op jit(solution)/shard_map/ppermute | solution.py:21
  57.3 11.0 %collective-permute-start.19 = (bf16[448,384]{1,0:T(8,128)(2,1)S(1)}, bf16[448,384]{1,0:T(8,128)(2,1)S(1)}, u32[]{:S(2)}, u32[]{:S(2)}) collective-permute-start(bf16[448,384]{1,0:T(8,128)(2,1)S(1)} %get-tuple-element.64), channel_id=1, source_target_pairs={{0,2},{2,0},{4,6},{6,4},{1,3},{3,1},{5,7},{7,5},{8,10},{10,8},{12,... | collective-permute-start | bytes 1032200 | tf_op jit(solution)/shard_map/ppermute | solution.py:21
  57.4 19.0 %collective-permute-start.20 = (bf16[448,384]{1,0:T(8,128)(2,1)S(1)}, bf16[448,384]{1,0:T(8,128)(2,1)S(1)}, u32[]{:S(2)}, u32[]{:S(2)}) collective-permute-start(bf16[448,384]{1,0:T(8,128)(2,1)S(1)} %get-tuple-element.65), channel_id=1, source_target_pairs={{0,6},{2,4},{4,2},{6,0},{1,7},{3,5},{5,3},{7,1},{8,14},{10,12},{12... | collective-permute-start | bytes 1032200 | tf_op jit(solution)/shard_map/ppermute | solution.py:21
  58.6 17.8 %collective-permute-start.21 = (bf16[448,384]{1,0:T(8,128)(2,1)S(1)}, bf16[448,384]{1,0:T(8,128)(2,1)S(1)}, u32[]{:S(2)}, u32[]{:S(2)}) collective-permute-start(bf16[448,384]{1,0:T(8,128)(2,1)S(1)} %get-tuple-element.66), channel_id=1, source_target_pairs={{0,4},{2,6},{4,0},{6,2},{1,5},{3,7},{5,1},{7,3},{8,12},{10,14},{12... | collective-permute-start | bytes 1032200 | tf_op jit(solution)/shard_map/ppermute | solution.py:21
  61.5 19.9 %collective-permute-start.16 = (bf16[3,32,384]{2,1,0:T(8,128)(2,1)S(1)}, bf16[3,32,384]{2,1,0:T(8,128)(2,1)S(1)}, u32[]{:S(2)}, u32[]{:S(2)}) collective-permute-start(bf16[3,32,384]{2,1,0:T(8,128)(2,1)S(1)} %get-tuple-element.61), channel_id=1, source_target_pairs={{8,16},{16,8},{24,32},{32,24},{40,48},{48,40},{56,64},{64,56},{72,... | collective-permute-start | bytes 221192 | tf_op jit(solution)/shard_map/ppermute | solution.py:34
  77.2 13.6 %copy-start.11 = (f32[7,7,384]{2,1,0:T(8,128)S(1)}, f32[7,7,384]{2,1,0:T(8,128)}, u32[]{:S(2)}) copy-start(f32[7,7,384]{2,1,0:T(8,128)} %param.11) | copy-start | bytes 225796
  77.2 5.0 %collective-permute-start.22 = (bf16[160,384]{1,0:T(8,128)(2,1)S(1)}, bf16[160,384]{1,0:T(8,128)(2,1)S(1)}, u32[]{:S(2)}, u32[]{:S(2)}) collective-permute-start(bf16[160,384]{1,0:T(8,128)(2,1)S(1)} %get-tuple-element.69), channel_id=1, source_target_pairs={{0,1},{1,0},{16,17},{17,16},{2,3},{3,2},{18,19},{19,18},{4,5},{5,4... | collective-permute-start | bytes 368648 | tf_op jit(solution)/shard_map/ppermute | solution.py:21
  78.7 8.2 %collective-permute-start.23 = (bf16[160,384]{1,0:T(8,128)(2,1)S(1)}, bf16[160,384]{1,0:T(8,128)(2,1)S(1)}, u32[]{:S(2)}, u32[]{:S(2)}) collective-permute-start(bf16[160,384]{1,0:T(8,128)(2,1)S(1)} %get-tuple-element.70), channel_id=1, source_target_pairs={{0,17},{1,16},{16,1},{17,0},{2,19},{3,18},{18,3},{19,2},{4,21},{5,... | collective-permute-start | bytes 368648 | tf_op jit(solution)/shard_map/ppermute | solution.py:21
  80.1 6.9 %collective-permute-start.24 = (bf16[160,384]{1,0:T(8,128)(2,1)S(1)}, bf16[160,384]{1,0:T(8,128)(2,1)S(1)}, u32[]{:S(2)}, u32[]{:S(2)}) collective-permute-start(bf16[160,384]{1,0:T(8,128)(2,1)S(1)} %get-tuple-element.71), channel_id=1, source_target_pairs={{0,16},{1,17},{16,0},{17,1},{2,18},{3,19},{18,2},{19,3},{4,20},{5,... | collective-permute-start | bytes 368648 | tf_op jit(solution)/shard_map/ppermute | solution.py:21
  87.6 5.2 %collective-permute-start.25 = (bf16[192,384]{1,0:T(8,128)(2,1)S(1)}, bf16[192,384]{1,0:T(8,128)(2,1)S(1)}, u32[]{:S(2)}, u32[]{:S(2)}) collective-permute-start(bf16[192,384]{1,0:T(8,128)(2,1)S(1)} %get-tuple-element.74), channel_id=1, source_target_pairs={{0,32},{32,0},{64,96},{96,64},{128,160},{160,128},{192,224},{224,1... | collective-permute-start | bytes 442376 | tf_op jit(solution)/shard_map/ppermute | solution.py:21
  88.8 11.8 %collective-permute-start.18 = (bf16[14,3,384]{2,1,0:T(4,128)(2,1)S(1)}, bf16[14,3,384]{2,1,0:T(4,128)(2,1)S(1)}, u32[]{:S(2)}, u32[]{:S(2)}) collective-permute-start(bf16[14,3,384]{2,1,0:T(4,128)(2,1)S(1)} %get-tuple-element.139), channel_id=1, source_target_pairs={{1,2},{2,1},{3,4},{4,3},{5,6},{6,5},{9,10},{10,9},{11,12},{12,11},... | collective-permute-start | bytes 96776 | tf_op jit(solution)/shard_map/ppermute | solution.py:34
  90.7 9.9 %collective-permute-start.17 = (bf16[14,3,384]{2,1,0:T(4,128)(2,1)S(1)}, bf16[14,3,384]{2,1,0:T(4,128)(2,1)S(1)}, u32[]{:S(2)}, u32[]{:S(2)}) collective-permute-start(bf16[14,3,384]{2,1,0:T(4,128)(2,1)S(1)} %get-tuple-element.140), channel_id=1, source_target_pairs={{0,1},{1,0},{2,3},{3,2},{4,5},{5,4},{6,7},{7,6},{8,9},{9,8},{10,11... | collective-permute-start | bytes 96776 | tf_op jit(solution)/shard_map/ppermute | solution.py:21
  93.5 11.1 %collective-permute-start.26 = (bf16[96,384]{1,0:T(8,128)(2,1)S(1)}, bf16[96,384]{1,0:T(8,128)(2,1)S(1)}, u32[]{:S(2)}, u32[]{:S(2)}) collective-permute-start(bf16[96,384]{1,0:T(8,128)(2,1)S(1)} %get-tuple-element.77), channel_id=1, source_target_pairs={{0,64},{32,96},{64,0},{96,32},{128,192},{160,224},{192,128},{224,1... | collective-permute-start | bytes 221192 | tf_op jit(solution)/shard_map/ppermute | solution.py:21
  96.9 7.6 %collective-permute-start.27 = (bf16[96,384]{1,0:T(8,128)(2,1)S(1)}, bf16[96,384]{1,0:T(8,128)(2,1)S(1)}, u32[]{:S(2)}, u32[]{:S(2)}) collective-permute-start(bf16[96,384]{1,0:T(8,128)(2,1)S(1)} %get-tuple-element.78), channel_id=1, source_target_pairs={{0,192},{32,224},{64,128},{96,160},{128,64},{160,96},{192,0},{224,... | collective-permute-start | bytes 221192 | tf_op jit(solution)/shard_map/ppermute | solution.py:21
  100.2 9.1 %collective-permute-start.28 = (bf16[96,384]{1,0:T(8,128)(2,1)S(1)}, bf16[96,384]{1,0:T(8,128)(2,1)S(1)}, u32[]{:S(2)}, u32[]{:S(2)}) collective-permute-start(bf16[96,384]{1,0:T(8,128)(2,1)S(1)} %get-tuple-element.79), channel_id=1, source_target_pairs={{0,128},{32,160},{64,192},{96,224},{128,0},{160,32},{192,64},{224,... | collective-permute-start | bytes 221192 | tf_op jit(solution)/shard_map/ppermute | solution.py:21

commit v5 on v4

--- a/solution.py
+++ b/solution.py
@@ -84,7 +84,9 @@
         else:
             others[flip] = swap(x, axis, flip)
     full = jnp.zeros((x.shape[0], 4 * rows, channels), x.dtype)
-    for flip, piece in ((0, x), (1, others[1]), (3, others[3]), (2, others[2])):
+    order = (0, 1, 3, 2) if extra is None else (0, 2, 1, 3)
+    for flip in order:
+        piece = x if flip == 0 else others[flip]
         full = lax.dynamic_update_slice_in_dim(full, piece, (me ^ flip) * rows, axis=1)
     return full if extra is None else (full, extra)
 
@@ -185,7 +187,7 @@
         message[2 * rows :, :] = shared[...]
 
 
-def second_fan(index, win, wout, mine, g1, g3, g2, total, one, three, two, shared):
+def second_fan(index, win, wout, mine, g1, g3, g2, total, two, one, three, shared):
     rows = win.shape[0] // 4
     at = pl.multiple_of(index[1] * rows, rows)
     for k, term in enumerate((win, wout)):
@@ -213,7 +215,7 @@
     message[k * block : k * block + half, :] = value.astype(BF)
 
 
-def third_fan(index, before, mine, g1, g3, g2, total, message, shared):
+def third_fan(index, before, mine, g2, g1, g3, total, message, shared):
     rows = before.shape[1] // 4
     at = pl.multiple_of(index[2] * rows, rows)
     for k in range(2):
@@ -234,7 +236,7 @@
     return jnp.where((which & 2) != 0, low[1], low[0])
 
 
-def fourth_fan(index, before, mine, got, total, one, three, two, shared):
+def fourth_fan(index, before, mine, got, total, two, one, three, shared):
     half = before.shape[1] // 2
     block = up16(half)
     bit = index[3] != 0
@@ -250,7 +252,7 @@
         message[2 * block :, :] = shared[...]
 
 
-def last_sum(index, before, mine, g1, g3, g2, win, wout, small, bias):
+def last_sum(index, before, mine, g2, g1, g3, win, wout, small, bias):
     rows = before.shape[1] // 4
     block = up16(rows)
     for k, out in ((0, win), (1, wout)):
@@ -390,15 +392,15 @@
     def message_of(rows, smalls=1):
         return shape(2 * rows + smalls * SMALL, channels, dtype=BF)
 
-    def fan(messages, axis, unit=1):
-        return [swap(m, axis, flip * unit) for m, flip in zip(messages, (1, 3, 2))]
+    def fan(messages, axis, flips, unit=1):
+        return [swap(m, axis, flip * unit) for m, flip in zip(messages, flips)]
 
     piece = half // 4
     *messages, shared = local_call(
         first_fan, index, [message_of(piece)] * 3 + [small_shape], win_term, wout_term, mine, theirs
     )
     messages[2], outer = lax.optimization_barrier((messages[2], outer))
-    got = fan(messages, "x")
+    got = fan(messages, "x", (1, 3, 2))
     outer_got = outer_swap(outer, ROW)
     rows = edge_order(theirs[2 * SMALL :].reshape(3, col_count, channels), outer_got, ROW)
     low_tall = between(grad_low, rows, 0)
@@ -410,7 +412,7 @@
         win_term, wout_term, shared, *got,
     )
     piece = piece // 4
-    got = fan(messages, Y)
+    got = fan(messages, Y, (2, 1, 3))
     total, message, shared = local_call(
         third_fan,
         index,
@@ -429,7 +431,7 @@
         [shape(2, piece, channels)] + [message_of(up16(units))] * 3 + [small_shape],
         total, shared, got,
     )
-    got = fan(messages, "z", 2)
+    got = fan(messages, "z", (2, 1, 3), 2)
     win_t, grad_w_out, small_grads, grad_b_in = local_call(
         last_sum,
         index,

time: 111 us -> 109 us (0.982)
  waiting for transfers between devices: 33.4 us -> 30.6 us
    ppermute x25, waiting for transfers between devices: 33.4 us -> 30.5 us  [swap(): return lax.ppermute(x, axis, [(i, i ^ flip) for i in range(count)])]
    ppermute x4, starting transfers between devices: 6.08 us -> 7.29 us  [outer_swap(): lax.ppermute(x, axis, [(i, (i + 1 ^ 1) - 1) for i in range(1, peers - 1)])]
    ppermute x25, starting transfers between devices: 40.6 us -> 39.4 us  [swap(): return lax.ppermute(x, axis, [(i, i ^ flip) for i in range(count)])]
  transfers between devices with their start and end apart: 29 -> 29, of which waited for: 11 -> 12; matrix products, arithmetic and copies ran while one was open for 12% -> 12% of each run, Pallas kernels for 5% -> 5%
where the time goes in v5:
time: 109 us; the launch traced here: 108 us
  starting transfers between devices  46.7 us (43%)
  waiting for transfers between devices  30.6 us (28%)
  Pallas kernels  11.5 us (11%)
  other arithmetic  7.4 us (7%)
  local copies, waits for them, and re-layouts  5.07 us (5%)
  matrix products  5.03 us (5%)
  between operations  1.37 us (1%)
    ppermute x25, starting transfers between devices, swap(): return lax.ppermute(x, axis, [(i, i ^ flip) for i in range(count)])  39.4 us
    ppermute x25, waiting for transfers between devices, swap(): return lax.ppermute(x, axis, [(i, i ^ flip) for i in range(count)])  30.5 us
    pallas_call x7, Pallas kernels, local_call(): pl.pallas_call(kernel, out_shape=outs, in_specs=[pl.BlockSpec(memory_spac...  11.5 us
    ppermute x4, starting transfers between devices, outer_swap(): lax.ppermute(x, axis, [(i, (i + 1 ^ 1) - 1) for i in range(1, peers - 1)])  7.29 us
    reduce_sum x1, other arithmetic, on_device(): average = jnp.mean(conv, -1, keepdims=True)  3.15 us
    dynamic_update_slice x8, local copies, waits for them, and re-layouts, quad_gather(): lax.dynamic_update_slice_in_dim(full, piece, (me ^ flip) * rows, axis=1)  2.21 us
  transfers between devices with their start and end apart: 29, of which 12 were waited for; matrix products, arithmetic and copies ran while one was open for 12% of the time, Pallas kernels for 5%

profile of v5, /device:TPU:6, one launch (start us, length us, event | category | flops | bytes accessed | tf_op | source)
XLA Modules:
  0.0 107.7 jit_solution(2224951101509954759)
XLA Ops:
  0.6 0.8 pad_maximum_fusion.13
  1.4 6.4 %collective-permute-start = (bf16[2,6,384]{2,1,0:T(8,128)(2,1)S(1)}, bf16[2,6,384]{2,1,0:T(8,128)(2,1)S(1)}, u32[]{:S(2)}, u32[]{:S(2)}) collective-permute-start(bf16[2,6,384]{2,1,0:T(8,128)(2,1)S(1)} %pad_maximum_fusion.13), channel_id=1, source_target_pairs={{0,192},{32,224},{64,128},{96,160},{128,64},{160,96},{192,0},{224,... | collective-permute-start | bytes 27656 | tf_op jit(solution)/shard_map/ppermute | solution.py:21
  7.8 1.0 collective-permute-start.1
  8.8 1.5 %collective-permute-start.2 = (bf16[2,6,384]{2,1,0:T(8,128)(2,1)S(1)}, bf16[2,6,384]{2,1,0:T(8,128)(2,1)S(1)}, u32[]{:S(2)}, u32[]{:S(2)}) collective-permute-start(bf16[2,6,384]{2,1,0:T(8,128)(2,1)S(1)} %pad_maximum_fusion.13), channel_id=1, source_target_pairs={{0,64},{32,96},{64,0},{96,32},{128,192},{160,224},{192,128},{224,1... | collective-permute-start | bytes 27656 | tf_op jit(solution)/shard_map/ppermute | solution.py:21
  10.2 0.9 broadcast_select_fusion.4
  11.2 0.7 collective-permute-start.5
  11.8 4.6 %collective-permute-start.4 = (bf16[3,32,384]{2,1,0:T(8,128)(2,1)S(1)}, bf16[3,32,384]{2,1,0:T(8,128)(2,1)S(1)}, u32[]{:S(2)}, u32[]{:S(2)}) collective-permute-start(bf16[3,32,384]{2,1,0:T(8,128)(2,1)S(1)} %get-tuple-element.144), channel_id=1, source_target_pairs={{0,8},{8,0},{16,24},{24,16},{32,40},{40,32},{48,56},{56,48},{64,72... | collective-permute-start | bytes 221192 | tf_op jit(solution)/shard_map/ppermute | solution.py:21
  16.5 0.7 broadcast_select_fusion.23
  17.3 1.1 %collective-permute-start.3 = (bf16[2,24,384]{2,1,0:T(8,128)(2,1)S(1)}, bf16[2,24,384]{2,1,0:T(8,128)(2,1)S(1)}, u32[]{:S(2)}, u32[]{:S(2)}) collective-permute-start(bf16[2,24,384]{2,1,0:T(8,128)(2,1)S(1)} %pad_maximum_fusion.12), channel_id=1, source_target_pairs={{0,32},{32,0},{64,96},{96,64},{128,160},{160,128},{192,224},{224,1... | collective-permute-start | bytes 110600 | tf_op jit(solution)/shard_map/ppermute | solution.py:21
  18.4 0.9 reshape.114
  19.4 0.2 reshape.115
  20.0 1.3 %collective-permute-done.3 = bf16[2,24,384]{2,1,0:T(8,128)(2,1)S(1)} collective-permute-done((bf16[2,24,384]{2,1,0:T(8,128)(2,1)S(1)}, bf16[2,24,384]{2,1,0:T(8,128)(2,1)S(1)}, u32[]{:S(2)}, u32[]{:S(2)}) %collective-permute-start.3) | collective-permute-done | bytes 36896 | tf_op jit(solution)/shard_map/ppermute | solution.py:21
  21.4 2.2 %collective-permute-start.6 = (bf16[2,48,384]{2,1,0:T(8,128)(2,1)S(1)}, bf16[2,48,384]{2,1,0:T(8,128)(2,1)S(1)}, u32[]{:S(2)}, u32[]{:S(2)}) collective-permute-start(bf16[2,48,384]{2,1,0:T(8,128)(2,1)S(1)} %pad_maximum_fusion.11), channel_id=1, source_target_pairs={{0,16},{1,17},{16,0},{17,1},{2,18},{3,19},{18,2},{19,3},{4,20},{5,... | collective-permute-start | bytes 221192 | tf_op jit(solution)/shard_map/ppermute | solution.py:21
  23.6 1.3 %collective-permute-start.8 = (bf16[2,48,384]{2,1,0:T(8,128)(2,1)S(1)}, bf16[2,48,384]{2,1,0:T(8,128)(2,1)S(1)}, u32[]{:S(2)}, u32[]{:S(2)}) collective-permute-start(bf16[2,48,384]{2,1,0:T(8,128)(2,1)S(1)} %pad_maximum_fusion.11), channel_id=1, source_target_pairs={{0,17},{1,16},{16,1},{17,0},{2,19},{3,18},{18,3},{19,2},{4,21},{5,... | collective-permute-start | bytes 221192 | tf_op jit(solution)/shard_map/ppermute | solution.py:21
  25.1 0.2 collective-permute-start.7
  25.3 4.0 %collective-permute-start.9 = (bf16[14,3,384]{2,1,0:T(4,128)(2,1)S(1)}, bf16[14,3,384]{2,1,0:T(4,128)(2,1)S(1)}, u32[]{:S(2)}, u32[]{:S(2)}) collective-permute-start(bf16[14,3,384]{2,1,0:T(4,128)(2,1)S(1)} %get-tuple-element.141), channel_id=1, source_target_pairs={{1,2},{2,1},{3,4},{4,3},{5,6},{6,5},{9,10},{10,9},{11,12},{12,11},... | collective-permute-start | bytes 96776 | tf_op jit(solution)/shard_map/ppermute | solution.py:34
  29.4 0.9 collective-permute-done.7
  30.4 0.9 collective-permute-start.11
  31.4 1.1 %collective-permute-start.12 = (bf16[2,192,384]{2,1,0:T(8,128)(2,1)S(1)}, bf16[2,192,384]{2,1,0:T(8,128)(2,1)}, u32[]{:S(2)}, u32[]{:S(2)}) collective-permute-start(bf16[2,192,384]{2,1,0:T(8,128)(2,1)S(1)} %constant_dynamic-update-slice_fusion.7), channel_id=1, source_target_pairs={{0,6},{2,4},{4,2},{6,0},{1,7},{3,5},{5,3},{7,1},{8,14},{10,12},{12... | collective-permute-start | bytes 884744 | tf_op jit(solution)/shard_map/ppermute | solution.py:21
  32.5 2.1 %collective-permute-start.13 = (bf16[2,192,384]{2,1,0:T(8,128)(2,1)S(1)}, bf16[2,192,384]{2,1,0:T(8,128)(2,1)S(1)}, u32[]{:S(2)}, u32[]{:S(2)}) collective-permute-start(bf16[2,192,384]{2,1,0:T(8,128)(2,1)S(1)} %constant_dynamic-update-slice_fusion.7), channel_id=1, source_target_pairs={{0,4},{2,6},{4,0},{6,2},{1,5},{3,7},{5,1},{7,3},{8,12},{10,14},{12... | collective-permute-start | bytes 884744 | tf_op jit(solution)/shard_map/ppermute | solution.py:21
  35.0 0.2 pad_maximum_fusion
  35.2 3.2 %fusion.67 = (f32[8,32]{1,0:T(8,128)S(1)}, f32[8,32,384]{2,1,0:T(8,128)S(1)}) fusion(f32[384]{0:T(512)S(1)} %get-tuple-element.85, f32[14,38,384]{2,1,0:T(8,128)S(1)} %get-tuple-element.136, f32[384]{0:T(512)S(1)} %get-tuple-element.86, f32[384]{0:T(512)S(1)} %get-tuple-element.87, f32[384]{0:T(512)S(1)} %get-tuple-element.88, ...), kind=kLoop, calls=%fused_computation.229 | loop fusion | flops 9633536 | bytes 19737088 | tf_op jit(solution)/shard_map/reduce_sum | solution.py:340
  38.4 0.2 multiply_reduce_fusion
  38.9 0.3 collective-permute-start.10
  39.5 0.7 collective-permute-done.11
  40.2 1.0 constant_dynamic-update-slice_fusion.5
  41.2 3.9 %collective-permute-done.12 = bf16[2,192,384]{2,1,0:T(8,128)(2,1)} collective-permute-done((bf16[2,192,384]{2,1,0:T(8,128)(2,1)S(1)}, bf16[2,192,384]{2,1,0:T(8,128)(2,1)}, u32[]{:S(2)}, u32[]{:S(2)}) %collective-permute-start.12) | collective-permute-done | bytes 294944 | tf_op jit(solution)/shard_map/ppermute | solution.py:21
  45.1 1.0 constant_dynamic-update-slice_fusion.4
  46.3 0.7 multiply_convert_fusion
  47.0 0.9 convert_reduce_fusion
  47.9 0.6 fusion.7.normed_grad
  48.5 0.6 fusion.6.mixed
  49.1 0.8 pad_maximum_fusion.4
  49.9 0.2 broadcast_in_dim.56
  50.2 0.2 broadcast_in_dim.59
  50.4 1.8 %fusion.58.win = f32[768,384]{1,0:T(8,128)S(1)} fusion(bf16[512,768]{1,0:T(8,128)(2,1)} %copy-done.4, bf16[256,384]{1,0:T(8,128)(2,1)} %copy-done.9, bf16[256,384]{1,0:T(8,128)(2,1)S(1)} %bitcast.52), kind=kOutput, calls=%fused_computation.126 | convolution fusion | flops 302776320 | bytes 2359296 | tf_op jit(solution)/shard_map/dot_general | solution.py:359
  52.2 3.7 %shard_map.145 = (bf16[8,32,384]{2,1,0:T(8,128)(2,1)S(1)}, bf16[224,384]{1,0:T(8,128)(2,1)S(1)}, bf16[3,32,384]{2,1,0:T(8,128)(2,1)S(1)}, bf16[8,32,384]{2,1,0:T(8,128)(2,1)}) custom-call(s32[5]{0:T(128)S(1)} %stack.48.index, f32[512,384]{1,0:T(8,128)S(1)} %fusion.7.normed_grad, f32[512,384]{1,0:T(8,128)S(1)} %fusion.6.mixed, ...), custom_call_target="tpu_custom_call" | custom-call | flops 10813440 | bytes 3810816 | tf_op jit(solution)/shard_map/pallas_call | solution.py:96
  55.9 0.6 collective-permute-start.15
  56.5 0.6 fusion.59.wout
  57.1 0.4 collective-permute-done.15.theirs
  57.6 0.7 shard_map.146
  58.3 1.2 %collective-permute-start.20 = (bf16[448,384]{1,0:T(8,128)(2,1)S(1)}, bf16[448,384]{1,0:T(8,128)(2,1)S(1)}, u32[]{:S(2)}, u32[]{:S(2)}) collective-permute-start(bf16[448,384]{1,0:T(8,128)(2,1)S(1)} %get-tuple-element.65), channel_id=1, source_target_pairs={{0,6},{2,4},{4,2},{6,0},{1,7},{3,5},{5,3},{7,1},{8,14},{10,12},{12... | collective-permute-start | bytes 1032200 | tf_op jit(solution)/shard_map/ppermute | solution.py:21
  59.6 2.9 %collective-permute-start.21 = (bf16[448,384]{1,0:T(8,128)(2,1)S(1)}, bf16[448,384]{1,0:T(8,128)(2,1)S(1)}, u32[]{:S(2)}, u32[]{:S(2)}) collective-permute-start(bf16[448,384]{1,0:T(8,128)(2,1)S(1)} %get-tuple-element.66), channel_id=1, source_target_pairs={{0,4},{2,6},{4,0},{6,2},{1,5},{3,7},{5,1},{7,3},{8,12},{10,14},{12... | collective-permute-start | bytes 1032200 | tf_op jit(solution)/shard_map/ppermute | solution.py:21
  62.4 0.7 collective-permute-start.16
  63.1 6.1 %collective-permute-done.19.g1 = bf16[448,384]{1,0:T(8,128)(2,1)S(1)} collective-permute-done((bf16[448,384]{1,0:T(8,128)(2,1)S(1)}, bf16[448,384]{1,0:T(8,128)(2,1)S(1)}, u32[]{:S(2)}, u32[]{:S(2)}) %collective-permute-start.19) | collective-permute-done | bytes 344096 | tf_op jit(solution)/shard_map/ppermute | solution.py:21
  69.2 8.1 %collective-permute-done.20.g3 = bf16[448,384]{1,0:T(8,128)(2,1)S(1)} collective-permute-done((bf16[448,384]{1,0:T(8,128)(2,1)S(1)}, bf16[448,384]{1,0:T(8,128)(2,1)S(1)}, u32[]{:S(2)}, u32[]{:S(2)}) %collective-permute-start.20) | collective-permute-done | bytes 344096 | tf_op jit(solution)/shard_map/ppermute | solution.py:21
  77.3 0.8 shard_map.148
  78.2 1.8 %collective-permute-start.22 = (bf16[160,384]{1,0:T(8,128)(2,1)S(1)}, bf16[160,384]{1,0:T(8,128)(2,1)S(1)}, u32[]{:S(2)}, u32[]{:S(2)}) collective-permute-start(bf16[160,384]{1,0:T(8,128)(2,1)S(1)} %get-tuple-element.69), channel_id=1, source_target_pairs={{0,16},{1,17},{16,0},{17,1},{2,18},{3,19},{18,2},{19,3},{4,20},{5,... | collective-permute-start | bytes 368648 | tf_op jit(solution)/shard_map/ppermute | solution.py:21
  79.9 0.6 collective-permute-start.23
  80.5 1.8 %collective-permute-start.24 = (bf16[160,384]{1,0:T(8,128)(2,1)S(1)}, bf16[160,384]{1,0:T(8,128)(2,1)S(1)}, u32[]{:S(2)}, u32[]{:S(2)}) collective-permute-start(bf16[160,384]{1,0:T(8,128)(2,1)S(1)} %get-tuple-element.71), channel_id=1, source_target_pairs={{0,17},{1,16},{16,1},{17,0},{2,19},{3,18},{18,3},{19,2},{4,21},{5,... | collective-permute-start | bytes 368648 | tf_op jit(solution)/shard_map/ppermute | solution.py:21
  82.4 3.4 %collective-permute-done.22.g2 = bf16[160,384]{1,0:T(8,128)(2,1)S(1)} collective-permute-done((bf16[160,384]{1,0:T(8,128)(2,1)S(1)}, bf16[160,384]{1,0:T(8,128)(2,1)S(1)}, u32[]{:S(2)}, u32[]{:S(2)}) %collective-permute-start.22) | collective-permute-done | bytes 122912 | tf_op jit(solution)/shard_map/ppermute | solution.py:21
  85.9 1.3 %collective-permute-done.24.g3 = bf16[160,384]{1,0:T(8,128)(2,1)S(1)} collective-permute-done((bf16[160,384]{1,0:T(8,128)(2,1)S(1)}, bf16[160,384]{1,0:T(8,128)(2,1)S(1)}, u32[]{:S(2)}, u32[]{:S(2)}) %collective-permute-start.24) | collective-permute-done | bytes 122912 | tf_op jit(solution)/shard_map/ppermute | solution.py:21
  87.2 0.6 shard_map.149
  87.8 1.1 %collective-permute-start.25 = (bf16[192,384]{1,0:T(8,128)(2,1)S(1)}, bf16[192,384]{1,0:T(8,128)(2,1)S(1)}, u32[]{:S(2)}, u32[]{:S(2)}) collective-permute-start(bf16[192,384]{1,0:T(8,128)(2,1)S(1)} %get-tuple-element.74), channel_id=1, source_target_pairs={{0,32},{32,0},{64,96},{96,64},{128,160},{160,128},{192,224},{224,1... | collective-permute-start | bytes 442376 | tf_op jit(solution)/shard_map/ppermute | solution.py:21
  89.0 1.9 %collective-permute-start.18 = (bf16[14,3,384]{2,1,0:T(4,128)(2,1)S(1)}, bf16[14,3,384]{2,1,0:T(4,128)(2,1)S(1)}, u32[]{:S(2)}, u32[]{:S(2)}) collective-permute-start(bf16[14,3,384]{2,1,0:T(4,128)(2,1)S(1)} %get-tuple-element.139), channel_id=1, source_target_pairs={{1,2},{2,1},{3,4},{4,3},{5,6},{6,5},{9,10},{10,9},{11,12},{12,11},... | collective-permute-start | bytes 96776 | tf_op jit(solution)/shard_map/ppermute | solution.py:34
  91.0 2.0 %collective-permute-done.25.got = bf16[192,384]{1,0:T(8,128)(2,1)S(1)} collective-permute-done((bf16[192,384]{1,0:T(8,128)(2,1)S(1)}, bf16[192,384]{1,0:T(8,128)(2,1)S(1)}, u32[]{:S(2)}, u32[]{:S(2)}) %collective-permute-start.25) | collective-permute-done | bytes 147488 | tf_op jit(solution)/shard_map/ppermute | solution.py:21
  93.0 0.6 shard_map.150
  93.6 4.8 %collective-permute-start.26 = (bf16[96,384]{1,0:T(8,128)(2,1)S(1)}, bf16[96,384]{1,0:T(8,128)(2,1)S(1)}, u32[]{:S(2)}, u32[]{:S(2)}) collective-permute-start(bf16[96,384]{1,0:T(8,128)(2,1)S(1)} %get-tuple-element.77), channel_id=1, source_target_pairs={{0,128},{32,160},{64,192},{96,224},{128,0},{160,32},{192,64},{224,... | collective-permute-start | bytes 221192 | tf_op jit(solution)/shard_map/ppermute | solution.py:21
  98.5 1.4 %collective-permute-start.27 = (bf16[96,384]{1,0:T(8,128)(2,1)S(1)}, bf16[96,384]{1,0:T(8,128)(2,1)S(1)}, u32[]{:S(2)}, u32[]{:S(2)}) collective-permute-start(bf16[96,384]{1,0:T(8,128)(2,1)S(1)} %get-tuple-element.78), channel_id=1, source_target_pairs={{0,64},{32,96},{64,0},{96,32},{128,192},{160,224},{192,128},{224,1... | collective-permute-start | bytes 221192 | tf_op jit(solution)/shard_map/ppermute | solution.py:21
  99.9 0.3 collective-permute-start.28
  100.3 3.9 %shard_map.147 = bf16[8,32,384]{2,1,0:T(8,128)(2,1)} custom-call(s32[5]{0:T(128)S(1)} %stack.48.index, bf16[14,32,384]{2,1,0:T(8,128)(2,1)S(1)} %pad_maximum_fusion.5.tall, bf16[14,3,384]{2,1,0:T(4,128)(2,1)S(1)} %get-tuple-element.150.left, bf16[14,3,384]{2,1,0:T(4,128)(2,1)S(1)} %get-tuple-element.149.right, f32[49,384]{1,0:T(8,128)S(1)} %reshape.117.taps, ...), custom_call_target="tpu_custom_call" | custom-call | flops 9633792 | bytes 877056 | tf_op jit(solution)/shard_map/pallas_call | solution.py:96
  104.2 0.8 collective-permute-done.27.g1
  105.0 1.5 %collective-permute-done.28.g3 = bf16[96,384]{1,0:T(8,128)(2,1)S(1)} collective-permute-done((bf16[96,384]{1,0:T(8,128)(2,1)S(1)}, bf16[96,384]{1,0:T(8,128)(2,1)S(1)}, u32[]{:S(2)}, u32[]{:S(2)}) %collective-permute-start.28) | collective-permute-done | bytes 73760 | tf_op jit(solution)/shard_map/ppermute | solution.py:21
  106.5 1.2 %shard_map.151 = (f32[6,384]{1,0:T(8,128)}, f32[6,384]{1,0:T(8,128)}, f32[53,384]{1,0:T(8,128)}, f32[1536]{0:T(1024)}) custom-call(s32[5]{0:T(128)S(1)} %stack.48.index, f32[2,24,384]{2,1,0:T(8,128)S(1)} %get-tuple-element.75.before, bf16[64,384]{1,0:T(8,128)(2,1)S(1)} %get-tuple-element.76.mine, bf16[96,384]{1,0:T(8,128)(2,1)S(1)} %collective-permute-done.26.g2, ...), custom_call_target="tpu_custom_call" | custom-call | flops 1000000 | bytes 450048 | tf_op jit(solution)/shard_map/pallas_call | solution.py:96
  (104 shorter events, 2.5 us)
Async XLA Ops:
  0.6 24.2 %copy-start.1 = (bf16[8,32,384]{2,1,0:T(8,128)(2,1)S(1)}, bf16[8,32,384]{2,1,0:T(8,128)(2,1)}, u32[]{:S(2)}) copy-start(bf16[8,32,384]{2,1,0:T(8,128)(2,1)} %feature) | copy-start | bytes 589828
  1.4 15.1 %collective-permute-start = (bf16[2,6,384]{2,1,0:T(8,128)(2,1)S(1)}, bf16[2,6,384]{2,1,0:T(8,128)(2,1)S(1)}, u32[]{:S(2)}, u32[]{:S(2)}) collective-permute-start(bf16[2,6,384]{2,1,0:T(8,128)(2,1)S(1)} %pad_maximum_fusion.13), channel_id=1, source_target_pairs={{0,192},{32,224},{64,128},{96,160},{128,64},{160,96},{192,0},{224,... | collective-permute-start | bytes 27656 | tf_op jit(solution)/shard_map/ppermute | solution.py:21
  7.8 8.7 %collective-permute-start.1 = (bf16[2,6,384]{2,1,0:T(8,128)(2,1)S(1)}, bf16[2,6,384]{2,1,0:T(8,128)(2,1)S(1)}, u32[]{:S(2)}, u32[]{:S(2)}) collective-permute-start(bf16[2,6,384]{2,1,0:T(8,128)(2,1)S(1)} %pad_maximum_fusion.13), channel_id=1, source_target_pairs={{0,128},{32,160},{64,192},{96,224},{128,0},{160,32},{192,64},{224,... | collective-permute-start | bytes 27656 | tf_op jit(solution)/shard_map/ppermute | solution.py:21
  8.8 7.7 %collective-permute-start.2 = (bf16[2,6,384]{2,1,0:T(8,128)(2,1)S(1)}, bf16[2,6,384]{2,1,0:T(8,128)(2,1)S(1)}, u32[]{:S(2)}, u32[]{:S(2)}) collective-permute-start(bf16[2,6,384]{2,1,0:T(8,128)(2,1)S(1)} %pad_maximum_fusion.13), channel_id=1, source_target_pairs={{0,64},{32,96},{64,0},{96,32},{128,192},{160,224},{192,128},{224,1... | collective-permute-start | bytes 27656 | tf_op jit(solution)/shard_map/ppermute | solution.py:21
  11.2 10.2 %collective-permute-start.5 = (bf16[3,32,384]{2,1,0:T(8,128)(2,1)S(1)}, bf16[3,32,384]{2,1,0:T(8,128)(2,1)S(1)}, u32[]{:S(2)}, u32[]{:S(2)}) collective-permute-start(bf16[3,32,384]{2,1,0:T(8,128)(2,1)S(1)} %get-tuple-element.143), channel_id=1, source_target_pairs={{8,16},{16,8},{24,32},{32,24},{40,48},{48,40},{56,64},{64,56},{72,... | collective-permute-start | bytes 221192 | tf_op jit(solution)/shard_map/ppermute | solution.py:34
  11.8 9.5 %collective-permute-start.4 = (bf16[3,32,384]{2,1,0:T(8,128)(2,1)S(1)}, bf16[3,32,384]{2,1,0:T(8,128)(2,1)S(1)}, u32[]{:S(2)}, u32[]{:S(2)}) collective-permute-start(bf16[3,32,384]{2,1,0:T(8,128)(2,1)S(1)} %get-tuple-element.144), channel_id=1, source_target_pairs={{0,8},{8,0},{16,24},{24,16},{32,40},{40,32},{48,56},{56,48},{64,72... | collective-permute-start | bytes 221192 | tf_op jit(solution)/shard_map/ppermute | solution.py:21
  17.3 4.0 %collective-permute-start.3 = (bf16[2,24,384]{2,1,0:T(8,128)(2,1)S(1)}, bf16[2,24,384]{2,1,0:T(8,128)(2,1)S(1)}, u32[]{:S(2)}, u32[]{:S(2)}) collective-permute-start(bf16[2,24,384]{2,1,0:T(8,128)(2,1)S(1)} %pad_maximum_fusion.12), channel_id=1, source_target_pairs={{0,32},{32,0},{64,96},{96,64},{128,160},{160,128},{192,224},{224,1... | collective-permute-start | bytes 110600 | tf_op jit(solution)/shard_map/ppermute | solution.py:21
  19.4 15.2 %copy-start.10 = (f32[7,7,384]{2,1,0:T(8,128)S(1)}, f32[7,7,384]{2,1,0:T(8,128)}, u32[]{:S(2)}) copy-start(f32[7,7,384]{2,1,0:T(8,128)} %param.11) | copy-start | bytes 225796
  19.4 15.5 %copy-start = (bf16[8,32,384]{2,1,0:T(8,128)(2,1)S(1)}, bf16[8,32,384]{2,1,0:T(8,128)(2,1)}, u32[]{:S(2)}) copy-start(bf16[8,32,384]{2,1,0:T(8,128)(2,1)} %cot.1) | copy-start | bytes 589828
  21.4 8.0 %collective-permute-start.6 = (bf16[2,48,384]{2,1,0:T(8,128)(2,1)S(1)}, bf16[2,48,384]{2,1,0:T(8,128)(2,1)S(1)}, u32[]{:S(2)}, u32[]{:S(2)}) collective-permute-start(bf16[2,48,384]{2,1,0:T(8,128)(2,1)S(1)} %pad_maximum_fusion.11), channel_id=1, source_target_pairs={{0,16},{1,17},{16,0},{17,1},{2,18},{3,19},{18,2},{19,3},{4,20},{5,... | collective-permute-start | bytes 221192 | tf_op jit(solution)/shard_map/ppermute | solution.py:21
  23.6 6.8 %collective-permute-start.8 = (bf16[2,48,384]{2,1,0:T(8,128)(2,1)S(1)}, bf16[2,48,384]{2,1,0:T(8,128)(2,1)S(1)}, u32[]{:S(2)}, u32[]{:S(2)}) collective-permute-start(bf16[2,48,384]{2,1,0:T(8,128)(2,1)S(1)} %pad_maximum_fusion.11), channel_id=1, source_target_pairs={{0,17},{1,16},{16,1},{17,0},{2,19},{3,18},{18,3},{19,2},{4,21},{5,... | collective-permute-start | bytes 221192 | tf_op jit(solution)/shard_map/ppermute | solution.py:21
  25.1 5.3 %collective-permute-start.7 = (bf16[138,384]{1,0:T(8,128)(2,1)S(1)}, bf16[138,384]{1,0:T(8,128)(2,1)S(1)}, u32[]{:S(2)}, u32[]{:S(2)}) collective-permute-start(bf16[138,384]{1,0:T(8,128)(2,1)S(1)} %pad_maximum_fusion.10), channel_id=1, source_target_pairs={{0,1},{1,0},{16,17},{17,16},{2,3},{3,2},{18,19},{19,18},{4,5},{5,4... | collective-permute-start | bytes 317960 | tf_op jit(solution)/shard_map/ppermute | solution.py:21
  25.3 9.7 %collective-permute-start.9 = (bf16[14,3,384]{2,1,0:T(4,128)(2,1)S(1)}, bf16[14,3,384]{2,1,0:T(4,128)(2,1)S(1)}, u32[]{:S(2)}, u32[]{:S(2)}) collective-permute-start(bf16[14,3,384]{2,1,0:T(4,128)(2,1)S(1)} %get-tuple-element.141), channel_id=1, source_target_pairs={{1,2},{2,1},{3,4},{4,3},{5,6},{6,5},{9,10},{10,9},{11,12},{12,11},... | collective-permute-start | bytes 96776 | tf_op jit(solution)/shard_map/ppermute | solution.py:34
  30.4 9.8 %collective-permute-start.11 = (bf16[2,192,384]{2,1,0:T(8,128)(2,1)S(1)}, bf16[2,192,384]{2,1,0:T(8,128)(2,1)}, u32[]{:S(2)}, u32[]{:S(2)}) collective-permute-start(bf16[2,192,384]{2,1,0:T(8,128)(2,1)S(1)} %constant_dynamic-update-slice_fusion.7), channel_id=1, source_target_pairs={{0,2},{2,0},{4,6},{6,4},{1,3},{3,1},{5,7},{7,5},{8,10},{10,8},{12,... | collective-permute-start | bytes 884744 | tf_op jit(solution)/shard_map/ppermute | solution.py:21
  31.4 13.8 %collective-permute-start.12 = (bf16[2,192,384]{2,1,0:T(8,128)(2,1)S(1)}, bf16[2,192,384]{2,1,0:T(8,128)(2,1)}, u32[]{:S(2)}, u32[]{:S(2)}) collective-permute-start(bf16[2,192,384]{2,1,0:T(8,128)(2,1)S(1)} %constant_dynamic-update-slice_fusion.7), channel_id=1, source_target_pairs={{0,6},{2,4},{4,2},{6,0},{1,7},{3,5},{5,3},{7,1},{8,14},{10,12},{12... | collective-permute-start | bytes 884744 | tf_op jit(solution)/shard_map/ppermute | solution.py:21
  32.5 13.7 %collective-permute-start.13 = (bf16[2,192,384]{2,1,0:T(8,128)(2,1)S(1)}, bf16[2,192,384]{2,1,0:T(8,128)(2,1)S(1)}, u32[]{:S(2)}, u32[]{:S(2)}) collective-permute-start(bf16[2,192,384]{2,1,0:T(8,128)(2,1)S(1)} %constant_dynamic-update-slice_fusion.7), channel_id=1, source_target_pairs={{0,4},{2,6},{4,0},{6,2},{1,5},{3,7},{5,1},{7,3},{8,12},{10,14},{12... | collective-permute-start | bytes 884744 | tf_op jit(solution)/shard_map/ppermute | solution.py:21
  35.2 3.4 %copy-start.12 = (f32[384]{0:T(512)S(1)}, f32[384]{0:T(512)}, u32[]{:S(2)}) copy-start(f32[384]{0:T(512)} %param.18) | copy-start | bytes 4612
  35.2 3.4 %copy-start.13 = (f32[384]{0:T(512)S(1)}, f32[384]{0:T(512)}, u32[]{:S(2)}) copy-start(f32[384]{0:T(512)} %param.12) | copy-start | bytes 4612
  35.2 3.4 %copy-start.14 = (f32[384]{0:T(512)S(1)}, f32[384]{0:T(512)}, u32[]{:S(2)}) copy-start(f32[384]{0:T(512)} %param.13) | copy-start | bytes 4612
  38.8 0.7 copy-start.15
  38.9 8.1 %copy-start.5 = (bf16[256,384]{1,0:T(8,128)(2,1)}, bf16[256,384]{1,0:T(8,128)(2,1)S(1)}, u32[]{:S(2)}) copy-start(bf16[256,384]{1,0:T(8,128)(2,1)S(1)} %fusion.57) | copy-start | bytes 589828
  38.9 7.3 %collective-permute-start.10 = (bf16[2,256,384]{2,1,0:T(8,128)(2,1)S(1)}, bf16[2,256,384]{2,1,0:T(8,128)(2,1)S(1)}, u32[]{:S(2)}, u32[]{:S(2)}) collective-permute-start(bf16[2,256,384]{2,1,0:T(8,128)(2,1)S(1)} %pad_maximum_fusion.1), channel_id=1, source_target_pairs={{0,8},{8,0},{1,9},{9,1},{2,10},{10,2},{3,11},{11,3},{4,12},{12,4},... | collective-permute-start | bytes 1179656 | tf_op jit(solution)/shard_map/ppermute | solution.py:21
  46.3 0.7 copy-start.7
  46.3 1.6 %copy-start.9 = (bf16[256,384]{1,0:T(8,128)(2,1)}, bf16[256,384]{1,0:T(8,128)(2,1)S(1)}, u32[]{:S(2)}) copy-start(bf16[256,384]{1,0:T(8,128)(2,1)S(1)} %get-tuple-element.138) | copy-start | bytes 589828
  47.0 1.5 %copy-start.2 = (bf16[512,768]{1,0:T(8,128)(2,1)}, bf16[512,768]{1,0:T(8,128)(2,1)S(1)}, u32[]{:S(2)}) copy-start(bf16[512,768]{1,0:T(8,128)(2,1)S(1)} %get-tuple-element.159) | copy-start | bytes 2359300
  47.9 1.2 %copy-start.4 = (bf16[512,768]{1,0:T(8,128)(2,1)}, bf16[512,768]{1,0:T(8,128)(2,1)S(1)}, u32[]{:S(2)}) copy-start(bf16[512,768]{1,0:T(8,128)(2,1)S(1)} %get-tuple-element.162) | copy-start | bytes 2359300
  49.9 2.2 %collective-permute-start.14 = (bf16[2,256,384]{2,1,0:T(8,128)(2,1)}, bf16[2,256,384]{2,1,0:T(8,128)(2,1)S(1)}, u32[]{:S(2)}, u32[]{:S(2)}) collective-permute-start(bf16[2,256,384]{2,1,0:T(8,128)(2,1)} %pad_maximum_fusion.4), channel_id=1, source_target_pairs={{0,8},{8,0},{1,9},{9,1},{2,10},{10,2},{3,11},{11,3},{4,12},{12,4},... | collective-permute-start | bytes 1179656 | tf_op jit(solution)/shard_map/ppermute | solution.py:21
  52.2 4.4 %copy-start.3 = (bf16[512,768]{1,0:T(8,128)(2,1)S(1)}, bf16[512,768]{1,0:T(8,128)(2,1)}, u32[]{:S(2)}) copy-start(bf16[512,768]{1,0:T(8,128)(2,1)} %copy-done.2) | copy-start | bytes 2359300
  52.2 4.4 %copy-start.6 = (bf16[256,384]{1,0:T(8,128)(2,1)S(1)}, bf16[256,384]{1,0:T(8,128)(2,1)}, u32[]{:S(2)}) copy-start(bf16[256,384]{1,0:T(8,128)(2,1)} %copy-done.5) | copy-start | bytes 589828
  52.2 4.4 %copy-start.8 = (bf16[256,384]{1,0:T(8,128)(2,1)S(1)}, bf16[256,384]{1,0:T(8,128)(2,1)}, u32[]{:S(2)}) copy-start(bf16[256,384]{1,0:T(8,128)(2,1)} %copy-done.7) | copy-start | bytes 589828
  55.9 1.6 %collective-permute-start.15 = (bf16[224,384]{1,0:T(8,128)(2,1)S(1)}, bf16[224,384]{1,0:T(8,128)(2,1)S(1)}, u32[]{:S(2)}, u32[]{:S(2)}) collective-permute-start(bf16[224,384]{1,0:T(8,128)(2,1)S(1)} %get-tuple-element.58.mine), channel_id=1, source_target_pairs={{0,8},{8,0},{1,9},{9,1},{2,10},{10,2},{3,11},{11,3},{4,12},{12,4},... | collective-permute-start | bytes 516104 | tf_op jit(solution)/shard_map/ppermute | solution.py:21
  58.2 11.0 %collective-permute-start.19 = (bf16[448,384]{1,0:T(8,128)(2,1)S(1)}, bf16[448,384]{1,0:T(8,128)(2,1)S(1)}, u32[]{:S(2)}, u32[]{:S(2)}) collective-permute-start(bf16[448,384]{1,0:T(8,128)(2,1)S(1)} %get-tuple-element.64), channel_id=1, source_target_pairs={{0,2},{2,0},{4,6},{6,4},{1,3},{3,1},{5,7},{7,5},{8,10},{10,8},{12,... | collective-permute-start | bytes 1032200 | tf_op jit(solution)/shard_map/ppermute | solution.py:21
  58.3 19.0 %collective-permute-start.20 = (bf16[448,384]{1,0:T(8,128)(2,1)S(1)}, bf16[448,384]{1,0:T(8,128)(2,1)S(1)}, u32[]{:S(2)}, u32[]{:S(2)}) collective-permute-start(bf16[448,384]{1,0:T(8,128)(2,1)S(1)} %get-tuple-element.65), channel_id=1, source_target_pairs={{0,6},{2,4},{4,2},{6,0},{1,7},{3,5},{5,3},{7,1},{8,14},{10,12},{12... | collective-permute-start | bytes 1032200 | tf_op jit(solution)/shard_map/ppermute | solution.py:21
  59.6 17.8 %collective-permute-start.21 = (bf16[448,384]{1,0:T(8,128)(2,1)S(1)}, bf16[448,384]{1,0:T(8,128)(2,1)S(1)}, u32[]{:S(2)}, u32[]{:S(2)}) collective-permute-start(bf16[448,384]{1,0:T(8,128)(2,1)S(1)} %get-tuple-element.66), channel_id=1, source_target_pairs={{0,4},{2,6},{4,0},{6,2},{1,5},{3,7},{5,1},{7,3},{8,12},{10,14},{12... | collective-permute-start | bytes 1032200 | tf_op jit(solution)/shard_map/ppermute | solution.py:21
  62.4 19.9 %collective-permute-start.16 = (bf16[3,32,384]{2,1,0:T(8,128)(2,1)S(1)}, bf16[3,32,384]{2,1,0:T(8,128)(2,1)S(1)}, u32[]{:S(2)}, u32[]{:S(2)}) collective-permute-start(bf16[3,32,384]{2,1,0:T(8,128)(2,1)S(1)} %get-tuple-element.61), channel_id=1, source_target_pairs={{8,16},{16,8},{24,32},{32,24},{40,48},{48,40},{56,64},{64,56},{72,... | collective-permute-start | bytes 221192 | tf_op jit(solution)/shard_map/ppermute | solution.py:34
  78.1 12.8 %copy-start.11 = (f32[7,7,384]{2,1,0:T(8,128)S(1)}, f32[7,7,384]{2,1,0:T(8,128)}, u32[]{:S(2)}) copy-start(f32[7,7,384]{2,1,0:T(8,128)} %param.11) | copy-start | bytes 225796
  78.2 7.7 %collective-permute-start.22 = (bf16[160,384]{1,0:T(8,128)(2,1)S(1)}, bf16[160,384]{1,0:T(8,128)(2,1)S(1)}, u32[]{:S(2)}, u32[]{:S(2)}) collective-permute-start(bf16[160,384]{1,0:T(8,128)(2,1)S(1)} %get-tuple-element.69), channel_id=1, source_target_pairs={{0,16},{1,17},{16,0},{17,1},{2,18},{3,19},{18,2},{19,3},{4,20},{5,... | collective-permute-start | bytes 368648 | tf_op jit(solution)/shard_map/ppermute | solution.py:21
  79.9 5.9 %collective-permute-start.23 = (bf16[160,384]{1,0:T(8,128)(2,1)S(1)}, bf16[160,384]{1,0:T(8,128)(2,1)S(1)}, u32[]{:S(2)}, u32[]{:S(2)}) collective-permute-start(bf16[160,384]{1,0:T(8,128)(2,1)S(1)} %get-tuple-element.70), channel_id=1, source_target_pairs={{0,1},{1,0},{16,17},{17,16},{2,3},{3,2},{18,19},{19,18},{4,5},{5,4... | collective-permute-start | bytes 368648 | tf_op jit(solution)/shard_map/ppermute | solution.py:21
  80.5 6.6 %collective-permute-start.24 = (bf16[160,384]{1,0:T(8,128)(2,1)S(1)}, bf16[160,384]{1,0:T(8,128)(2,1)S(1)}, u32[]{:S(2)}, u32[]{:S(2)}) collective-permute-start(bf16[160,384]{1,0:T(8,128)(2,1)S(1)} %get-tuple-element.71), channel_id=1, source_target_pairs={{0,17},{1,16},{16,1},{17,0},{2,19},{3,18},{18,3},{19,2},{4,21},{5,... | collective-permute-start | bytes 368648 | tf_op jit(solution)/shard_map/ppermute | solution.py:21
  87.8 5.2 %collective-permute-start.25 = (bf16[192,384]{1,0:T(8,128)(2,1)S(1)}, bf16[192,384]{1,0:T(8,128)(2,1)S(1)}, u32[]{:S(2)}, u32[]{:S(2)}) collective-permute-start(bf16[192,384]{1,0:T(8,128)(2,1)S(1)} %get-tuple-element.74), channel_id=1, source_target_pairs={{0,32},{32,0},{64,96},{96,64},{128,160},{160,128},{192,224},{224,1... | collective-permute-start | bytes 442376 | tf_op jit(solution)/shard_map/ppermute | solution.py:21
  89.0 11.3 %collective-permute-start.18 = (bf16[14,3,384]{2,1,0:T(4,128)(2,1)S(1)}, bf16[14,3,384]{2,1,0:T(4,128)(2,1)S(1)}, u32[]{:S(2)}, u32[]{:S(2)}) collective-permute-start(bf16[14,3,384]{2,1,0:T(4,128)(2,1)S(1)} %get-tuple-element.139), channel_id=1, source_target_pairs={{1,2},{2,1},{3,4},{4,3},{5,6},{6,5},{9,10},{10,9},{11,12},{12,11},... | collective-permute-start | bytes 96776 | tf_op jit(solution)/shard_map/ppermute | solution.py:34
  90.9 9.4 %collective-permute-start.17 = (bf16[14,3,384]{2,1,0:T(4,128)(2,1)S(1)}, bf16[14,3,384]{2,1,0:T(4,128)(2,1)S(1)}, u32[]{:S(2)}, u32[]{:S(2)}) collective-permute-start(bf16[14,3,384]{2,1,0:T(4,128)(2,1)S(1)} %get-tuple-element.140), channel_id=1, source_target_pairs={{0,1},{1,0},{2,3},{3,2},{4,5},{5,4},{6,7},{7,6},{8,9},{9,8},{10,11... | collective-permute-start | bytes 96776 | tf_op jit(solution)/shard_map/ppermute | solution.py:21
  93.6 10.5 %collective-permute-start.26 = (bf16[96,384]{1,0:T(8,128)(2,1)S(1)}, bf16[96,384]{1,0:T(8,128)(2,1)S(1)}, u32[]{:S(2)}, u32[]{:S(2)}) collective-permute-start(bf16[96,384]{1,0:T(8,128)(2,1)S(1)} %get-tuple-element.77), channel_id=1, source_target_pairs={{0,128},{32,160},{64,192},{96,224},{128,0},{160,32},{192,64},{224,... | collective-permute-start | bytes 221192 | tf_op jit(solution)/shard_map/ppermute | solution.py:21
  98.5 6.5 %collective-permute-start.27 = (bf16[96,384]{1,0:T(8,128)(2,1)S(1)}, bf16[96,384]{1,0:T(8,128)(2,1)S(1)}, u32[]{:S(2)}, u32[]{:S(2)}) collective-permute-start(bf16[96,384]{1,0:T(8,128)(2,1)S(1)} %get-tuple-element.78), channel_id=1, source_target_pairs={{0,64},{32,96},{64,0},{96,32},{128,192},{160,224},{192,128},{224,1... | collective-permute-start | bytes 221192 | tf_op jit(solution)/shard_map/ppermute | solution.py:21
  99.9 6.6 %collective-permute-start.28 = (bf16[96,384]{1,0:T(8,128)(2,1)S(1)}, bf16[96,384]{1,0:T(8,128)(2,1)S(1)}, u32[]{:S(2)}, u32[]{:S(2)}) collective-permute-start(bf16[96,384]{1,0:T(8,128)(2,1)S(1)} %get-tuple-element.79), channel_id=1, source_target_pairs={{0,192},{32,224},{64,128},{96,160},{128,64},{160,96},{192,0},{224,... | collective-permute-start | bytes 221192 | tf_op jit(solution)/shard_map/ppermute | solution.py:21

commit v6 on v5

--- a/solution.py
+++ b/solution.py
@@ -187,7 +187,7 @@
         message[2 * rows :, :] = shared[...]
 
 
-def second_fan(index, win, wout, mine, g1, g3, g2, total, two, one, three, shared):
+def second_fan(index, win, wout, mine, g1, g3, g2, total, one, three, two, shared):
     rows = win.shape[0] // 4
     at = pl.multiple_of(index[1] * rows, rows)
     for k, term in enumerate((win, wout)):
@@ -215,7 +215,7 @@
     message[k * block : k * block + half, :] = value.astype(BF)
 
 
-def third_fan(index, before, mine, g2, g1, g3, total, message, shared):
+def third_fan(index, before, mine, g1, g3, g2, total, message, shared):
     rows = before.shape[1] // 4
     at = pl.multiple_of(index[2] * rows, rows)
     for k in range(2):
@@ -412,7 +412,7 @@
         win_term, wout_term, shared, *got,
     )
     piece = piece // 4
-    got = fan(messages, Y, (2, 1, 3))
+    got = fan(messages, Y, (1, 3, 2))
     total, message, shared = local_call(
         third_fan,
         index,

time: 109 us -> 109 us (level)
  transfers between devices with their start and end apart: 29 -> 29, of which waited for: 12 -> 11; matrix products, arithmetic and copies ran while one was open for 12% -> 12% of each run, Pallas kernels for 5% -> 5%
where the time goes in v6:
time: 109 us; the launch traced here: 108 us
  starting transfers between devices  46.9 us (43%)
  waiting for transfers between devices  31 us (28%)
  Pallas kernels  11.6 us (11%)
  other arithmetic  7.4 us (7%)
  local copies, waits for them, and re-layouts  5.07 us (5%)
  matrix products  5.03 us (5%)
  between operations  1.37 us (1%)
    ppermute x25, starting transfers between devices, swap(): return lax.ppermute(x, axis, [(i, i ^ flip) for i in range(count)])  39.5 us
    ppermute x25, waiting for transfers between devices, swap(): return lax.ppermute(x, axis, [(i, i ^ flip) for i in range(count)])  31 us
    pallas_call x7, Pallas kernels, local_call(): pl.pallas_call(kernel, out_shape=outs, in_specs=[pl.BlockSpec(memory_spac...  11.6 us
    ppermute x4, starting transfers between devices, outer_swap(): lax.ppermute(x, axis, [(i, (i + 1 ^ 1) - 1) for i in range(1, peers - 1)])  7.34 us
    reduce_sum x1, other arithmetic, on_device(): average = jnp.mean(conv, -1, keepdims=True)  3.15 us
    dynamic_update_slice x8, local copies, waits for them, and re-layouts, quad_gather(): lax.dynamic_update_slice_in_dim(full, piece, (me ^ flip) * rows, axis=1)  2.21 us
  transfers between devices with their start and end apart: 29, of which 11 were waited for; matrix products, arithmetic and copies ran while one was open for 12% of the time, Pallas kernels for 5%

profile of v6, /device:TPU:6, one launch (start us, length us, event | category | flops | bytes accessed | tf_op | source)
XLA Modules:
  0.0 108.3 jit_solution(15944244112959582506)
XLA Ops:
  0.6 0.8 pad_maximum_fusion.13
  1.4 6.4 %collective-permute-start = (bf16[2,6,384]{2,1,0:T(8,128)(2,1)S(1)}, bf16[2,6,384]{2,1,0:T(8,128)(2,1)S(1)}, u32[]{:S(2)}, u32[]{:S(2)}) collective-permute-start(bf16[2,6,384]{2,1,0:T(8,128)(2,1)S(1)} %pad_maximum_fusion.13), channel_id=1, source_target_pairs={{0,192},{32,224},{64,128},{96,160},{128,64},{160,96},{192,0},{224,... | collective-permute-start | bytes 27656 | tf_op jit(solution)/shard_map/ppermute | solution.py:21
  7.8 1.0 collective-permute-start.1
  8.8 1.5 %collective-permute-start.2 = (bf16[2,6,384]{2,1,0:T(8,128)(2,1)S(1)}, bf16[2,6,384]{2,1,0:T(8,128)(2,1)S(1)}, u32[]{:S(2)}, u32[]{:S(2)}) collective-permute-start(bf16[2,6,384]{2,1,0:T(8,128)(2,1)S(1)} %pad_maximum_fusion.13), channel_id=1, source_target_pairs={{0,64},{32,96},{64,0},{96,32},{128,192},{160,224},{192,128},{224,1... | collective-permute-start | bytes 27656 | tf_op jit(solution)/shard_map/ppermute | solution.py:21
  10.2 0.9 broadcast_select_fusion.4
  11.2 0.7 collective-permute-start.5
  11.8 4.6 %collective-permute-start.4 = (bf16[3,32,384]{2,1,0:T(8,128)(2,1)S(1)}, bf16[3,32,384]{2,1,0:T(8,128)(2,1)S(1)}, u32[]{:S(2)}, u32[]{:S(2)}) collective-permute-start(bf16[3,32,384]{2,1,0:T(8,128)(2,1)S(1)} %get-tuple-element.144), channel_id=1, source_target_pairs={{0,8},{8,0},{16,24},{24,16},{32,40},{40,32},{48,56},{56,48},{64,72... | collective-permute-start | bytes 221192 | tf_op jit(solution)/shard_map/ppermute | solution.py:21
  16.5 0.7 broadcast_select_fusion.23
  17.3 1.1 %collective-permute-start.3 = (bf16[2,24,384]{2,1,0:T(8,128)(2,1)S(1)}, bf16[2,24,384]{2,1,0:T(8,128)(2,1)S(1)}, u32[]{:S(2)}, u32[]{:S(2)}) collective-permute-start(bf16[2,24,384]{2,1,0:T(8,128)(2,1)S(1)} %pad_maximum_fusion.12), channel_id=1, source_target_pairs={{0,32},{32,0},{64,96},{96,64},{128,160},{160,128},{192,224},{224,1... | collective-permute-start | bytes 110600 | tf_op jit(solution)/shard_map/ppermute | solution.py:21
  18.4 0.9 reshape.114
  19.4 0.2 reshape.115
  20.0 1.3 %collective-permute-done.3 = bf16[2,24,384]{2,1,0:T(8,128)(2,1)S(1)} collective-permute-done((bf16[2,24,384]{2,1,0:T(8,128)(2,1)S(1)}, bf16[2,24,384]{2,1,0:T(8,128)(2,1)S(1)}, u32[]{:S(2)}, u32[]{:S(2)}) %collective-permute-start.3) | collective-permute-done | bytes 36896 | tf_op jit(solution)/shard_map/ppermute | solution.py:21
  21.4 2.2 %collective-permute-start.6 = (bf16[2,48,384]{2,1,0:T(8,128)(2,1)S(1)}, bf16[2,48,384]{2,1,0:T(8,128)(2,1)S(1)}, u32[]{:S(2)}, u32[]{:S(2)}) collective-permute-start(bf16[2,48,384]{2,1,0:T(8,128)(2,1)S(1)} %pad_maximum_fusion.11), channel_id=1, source_target_pairs={{0,16},{1,17},{16,0},{17,1},{2,18},{3,19},{18,2},{19,3},{4,20},{5,... | collective-permute-start | bytes 221192 | tf_op jit(solution)/shard_map/ppermute | solution.py:21
  23.6 1.3 %collective-permute-start.8 = (bf16[2,48,384]{2,1,0:T(8,128)(2,1)S(1)}, bf16[2,48,384]{2,1,0:T(8,128)(2,1)S(1)}, u32[]{:S(2)}, u32[]{:S(2)}) collective-permute-start(bf16[2,48,384]{2,1,0:T(8,128)(2,1)S(1)} %pad_maximum_fusion.11), channel_id=1, source_target_pairs={{0,17},{1,16},{16,1},{17,0},{2,19},{3,18},{18,3},{19,2},{4,21},{5,... | collective-permute-start | bytes 221192 | tf_op jit(solution)/shard_map/ppermute | solution.py:21
  25.1 0.2 collective-permute-start.7
  25.3 4.0 %collective-permute-start.9 = (bf16[14,3,384]{2,1,0:T(4,128)(2,1)S(1)}, bf16[14,3,384]{2,1,0:T(4,128)(2,1)S(1)}, u32[]{:S(2)}, u32[]{:S(2)}) collective-permute-start(bf16[14,3,384]{2,1,0:T(4,128)(2,1)S(1)} %get-tuple-element.141), channel_id=1, source_target_pairs={{1,2},{2,1},{3,4},{4,3},{5,6},{6,5},{9,10},{10,9},{11,12},{12,11},... | collective-permute-start | bytes 96776 | tf_op jit(solution)/shard_map/ppermute | solution.py:34
  29.4 0.9 collective-permute-done.7
  30.4 0.9 collective-permute-start.11
  31.4 1.1 %collective-permute-start.12 = (bf16[2,192,384]{2,1,0:T(8,128)(2,1)S(1)}, bf16[2,192,384]{2,1,0:T(8,128)(2,1)}, u32[]{:S(2)}, u32[]{:S(2)}) collective-permute-start(bf16[2,192,384]{2,1,0:T(8,128)(2,1)S(1)} %constant_dynamic-update-slice_fusion.7), channel_id=1, source_target_pairs={{0,6},{2,4},{4,2},{6,0},{1,7},{3,5},{5,3},{7,1},{8,14},{10,12},{12... | collective-permute-start | bytes 884744 | tf_op jit(solution)/shard_map/ppermute | solution.py:21
  32.5 2.1 %collective-permute-start.13 = (bf16[2,192,384]{2,1,0:T(8,128)(2,1)S(1)}, bf16[2,192,384]{2,1,0:T(8,128)(2,1)S(1)}, u32[]{:S(2)}, u32[]{:S(2)}) collective-permute-start(bf16[2,192,384]{2,1,0:T(8,128)(2,1)S(1)} %constant_dynamic-update-slice_fusion.7), channel_id=1, source_target_pairs={{0,4},{2,6},{4,0},{6,2},{1,5},{3,7},{5,1},{7,3},{8,12},{10,14},{12... | collective-permute-start | bytes 884744 | tf_op jit(solution)/shard_map/ppermute | solution.py:21
  35.0 0.2 pad_maximum_fusion
  35.2 3.2 %fusion.67 = (f32[8,32]{1,0:T(8,128)S(1)}, f32[8,32,384]{2,1,0:T(8,128)S(1)}) fusion(f32[384]{0:T(512)S(1)} %get-tuple-element.85, f32[14,38,384]{2,1,0:T(8,128)S(1)} %get-tuple-element.136, f32[384]{0:T(512)S(1)} %get-tuple-element.86, f32[384]{0:T(512)S(1)} %get-tuple-element.87, f32[384]{0:T(512)S(1)} %get-tuple-element.88, ...), kind=kLoop, calls=%fused_computation.229 | loop fusion | flops 9633536 | bytes 19737088 | tf_op jit(solution)/shard_map/reduce_sum | solution.py:340
  38.4 0.2 multiply_reduce_fusion
  38.7 0.1 add_convert_fusion
  38.9 0.3 collective-permute-start.10
  39.5 0.7 collective-permute-done.11
  40.2 1.0 constant_dynamic-update-slice_fusion.5
  41.2 3.9 %collective-permute-done.12 = bf16[2,192,384]{2,1,0:T(8,128)(2,1)} collective-permute-done((bf16[2,192,384]{2,1,0:T(8,128)(2,1)S(1)}, bf16[2,192,384]{2,1,0:T(8,128)(2,1)}, u32[]{:S(2)}, u32[]{:S(2)}) %collective-permute-start.12) | collective-permute-done | bytes 294944 | tf_op jit(solution)/shard_map/ppermute | solution.py:21
  45.1 1.0 constant_dynamic-update-slice_fusion.4
  46.3 0.7 multiply_convert_fusion
  47.0 0.9 convert_reduce_fusion
  47.9 0.6 fusion.7.normed_grad
  48.5 0.6 fusion.6.mixed
  49.1 0.8 pad_maximum_fusion.4
  49.9 0.2 broadcast_in_dim.56
  50.2 0.2 broadcast_in_dim.59
  50.4 1.8 %fusion.58.win = f32[768,384]{1,0:T(8,128)S(1)} fusion(bf16[512,768]{1,0:T(8,128)(2,1)} %copy-done.4, bf16[256,384]{1,0:T(8,128)(2,1)} %copy-done.9, bf16[256,384]{1,0:T(8,128)(2,1)S(1)} %bitcast.52), kind=kOutput, calls=%fused_computation.126 | convolution fusion | flops 302776320 | bytes 2359296 | tf_op jit(solution)/shard_map/dot_general | solution.py:359
  52.2 3.7 %shard_map.145 = (bf16[8,32,384]{2,1,0:T(8,128)(2,1)S(1)}, bf16[224,384]{1,0:T(8,128)(2,1)S(1)}, bf16[3,32,384]{2,1,0:T(8,128)(2,1)S(1)}, bf16[8,32,384]{2,1,0:T(8,128)(2,1)}) custom-call(s32[5]{0:T(128)S(1)} %stack.48.index, f32[512,384]{1,0:T(8,128)S(1)} %fusion.7.normed_grad, f32[512,384]{1,0:T(8,128)S(1)} %fusion.6.mixed, ...), custom_call_target="tpu_custom_call" | custom-call | flops 10813440 | bytes 3810816 | tf_op jit(solution)/shard_map/pallas_call | solution.py:96
  55.9 0.6 collective-permute-start.15
  56.5 0.6 fusion.59.wout
  57.1 0.4 collective-permute-done.15.theirs
  57.6 0.7 shard_map.146
  58.3 1.2 %collective-permute-start.20 = (bf16[448,384]{1,0:T(8,128)(2,1)S(1)}, bf16[448,384]{1,0:T(8,128)(2,1)S(1)}, u32[]{:S(2)}, u32[]{:S(2)}) collective-permute-start(bf16[448,384]{1,0:T(8,128)(2,1)S(1)} %get-tuple-element.65), channel_id=1, source_target_pairs={{0,6},{2,4},{4,2},{6,0},{1,7},{3,5},{5,3},{7,1},{8,14},{10,12},{12... | collective-permute-start | bytes 1032200 | tf_op jit(solution)/shard_map/ppermute | solution.py:21
  59.6 2.9 %collective-permute-start.21 = (bf16[448,384]{1,0:T(8,128)(2,1)S(1)}, bf16[448,384]{1,0:T(8,128)(2,1)S(1)}, u32[]{:S(2)}, u32[]{:S(2)}) collective-permute-start(bf16[448,384]{1,0:T(8,128)(2,1)S(1)} %get-tuple-element.66), channel_id=1, source_target_pairs={{0,4},{2,6},{4,0},{6,2},{1,5},{3,7},{5,1},{7,3},{8,12},{10,14},{12... | collective-permute-start | bytes 1032200 | tf_op jit(solution)/shard_map/ppermute | solution.py:21
  62.4 0.7 collective-permute-start.16
  63.1 6.1 %collective-permute-done.19.g1 = bf16[448,384]{1,0:T(8,128)(2,1)S(1)} collective-permute-done((bf16[448,384]{1,0:T(8,128)(2,1)S(1)}, bf16[448,384]{1,0:T(8,128)(2,1)S(1)}, u32[]{:S(2)}, u32[]{:S(2)}) %collective-permute-start.19) | collective-permute-done | bytes 344096 | tf_op jit(solution)/shard_map/ppermute | solution.py:21
  69.2 8.1 %collective-permute-done.20.g3 = bf16[448,384]{1,0:T(8,128)(2,1)S(1)} collective-permute-done((bf16[448,384]{1,0:T(8,128)(2,1)S(1)}, bf16[448,384]{1,0:T(8,128)(2,1)S(1)}, u32[]{:S(2)}, u32[]{:S(2)}) %collective-permute-start.20) | collective-permute-done | bytes 344096 | tf_op jit(solution)/shard_map/ppermute | solution.py:21
  77.3 0.8 shard_map.148
  78.2 0.4 collective-permute-start.22
  78.6 1.9 %collective-permute-start.23 = (bf16[160,384]{1,0:T(8,128)(2,1)S(1)}, bf16[160,384]{1,0:T(8,128)(2,1)S(1)}, u32[]{:S(2)}, u32[]{:S(2)}) collective-permute-start(bf16[160,384]{1,0:T(8,128)(2,1)S(1)} %get-tuple-element.70), channel_id=1, source_target_pairs={{0,17},{1,16},{16,1},{17,0},{2,19},{3,18},{18,3},{19,2},{4,21},{5,... | collective-permute-start | bytes 368648 | tf_op jit(solution)/shard_map/ppermute | solution.py:21
  80.5 1.8 %collective-permute-start.24 = (bf16[160,384]{1,0:T(8,128)(2,1)S(1)}, bf16[160,384]{1,0:T(8,128)(2,1)S(1)}, u32[]{:S(2)}, u32[]{:S(2)}) collective-permute-start(bf16[160,384]{1,0:T(8,128)(2,1)S(1)} %get-tuple-element.71), channel_id=1, source_target_pairs={{0,16},{1,17},{16,0},{17,1},{2,18},{3,19},{18,2},{19,3},{4,20},{5,... | collective-permute-start | bytes 368648 | tf_op jit(solution)/shard_map/ppermute | solution.py:21
  82.4 1.6 %collective-permute-done.22.g1 = bf16[160,384]{1,0:T(8,128)(2,1)S(1)} collective-permute-done((bf16[160,384]{1,0:T(8,128)(2,1)S(1)}, bf16[160,384]{1,0:T(8,128)(2,1)S(1)}, u32[]{:S(2)}, u32[]{:S(2)}) %collective-permute-start.22) | collective-permute-done | bytes 122912 | tf_op jit(solution)/shard_map/ppermute | solution.py:21
  84.0 3.3 %collective-permute-done.23.g3 = bf16[160,384]{1,0:T(8,128)(2,1)S(1)} collective-permute-done((bf16[160,384]{1,0:T(8,128)(2,1)S(1)}, bf16[160,384]{1,0:T(8,128)(2,1)S(1)}, u32[]{:S(2)}, u32[]{:S(2)}) %collective-permute-start.23) | collective-permute-done | bytes 122912 | tf_op jit(solution)/shard_map/ppermute | solution.py:21
  87.3 0.6 shard_map.149
  88.0 1.2 %collective-permute-start.25 = (bf16[192,384]{1,0:T(8,128)(2,1)S(1)}, bf16[192,384]{1,0:T(8,128)(2,1)S(1)}, u32[]{:S(2)}, u32[]{:S(2)}) collective-permute-start(bf16[192,384]{1,0:T(8,128)(2,1)S(1)} %get-tuple-element.74), channel_id=1, source_target_pairs={{0,32},{32,0},{64,96},{96,64},{128,160},{160,128},{192,224},{224,1... | collective-permute-start | bytes 442376 | tf_op jit(solution)/shard_map/ppermute | solution.py:21
  89.2 2.0 %collective-permute-start.18 = (bf16[14,3,384]{2,1,0:T(4,128)(2,1)S(1)}, bf16[14,3,384]{2,1,0:T(4,128)(2,1)S(1)}, u32[]{:S(2)}, u32[]{:S(2)}) collective-permute-start(bf16[14,3,384]{2,1,0:T(4,128)(2,1)S(1)} %get-tuple-element.139), channel_id=1, source_target_pairs={{1,2},{2,1},{3,4},{4,3},{5,6},{6,5},{9,10},{10,9},{11,12},{12,11},... | collective-permute-start | bytes 96776 | tf_op jit(solution)/shard_map/ppermute | solution.py:34
  91.3 1.9 %collective-permute-done.25.got = bf16[192,384]{1,0:T(8,128)(2,1)S(1)} collective-permute-done((bf16[192,384]{1,0:T(8,128)(2,1)S(1)}, bf16[192,384]{1,0:T(8,128)(2,1)S(1)}, u32[]{:S(2)}, u32[]{:S(2)}) %collective-permute-start.25) | collective-permute-done | bytes 147488 | tf_op jit(solution)/shard_map/ppermute | solution.py:21
  93.2 0.6 shard_map.150
  93.8 5.0 %collective-permute-start.26 = (bf16[96,384]{1,0:T(8,128)(2,1)S(1)}, bf16[96,384]{1,0:T(8,128)(2,1)S(1)}, u32[]{:S(2)}, u32[]{:S(2)}) collective-permute-start(bf16[96,384]{1,0:T(8,128)(2,1)S(1)} %get-tuple-element.77), channel_id=1, source_target_pairs={{0,128},{32,160},{64,192},{96,224},{128,0},{160,32},{192,64},{224,... | collective-permute-start | bytes 221192 | tf_op jit(solution)/shard_map/ppermute | solution.py:21
  98.8 1.4 %collective-permute-start.27 = (bf16[96,384]{1,0:T(8,128)(2,1)S(1)}, bf16[96,384]{1,0:T(8,128)(2,1)S(1)}, u32[]{:S(2)}, u32[]{:S(2)}) collective-permute-start(bf16[96,384]{1,0:T(8,128)(2,1)S(1)} %get-tuple-element.78), channel_id=1, source_target_pairs={{0,64},{32,96},{64,0},{96,32},{128,192},{160,224},{192,128},{224,1... | collective-permute-start | bytes 221192 | tf_op jit(solution)/shard_map/ppermute | solution.py:21
  100.2 0.2 collective-permute-start.28
  100.4 3.9 %shard_map.147 = bf16[8,32,384]{2,1,0:T(8,128)(2,1)} custom-call(s32[5]{0:T(128)S(1)} %stack.48.index, bf16[14,32,384]{2,1,0:T(8,128)(2,1)S(1)} %pad_maximum_fusion.5.tall, bf16[14,3,384]{2,1,0:T(4,128)(2,1)S(1)} %get-tuple-element.150.left, bf16[14,3,384]{2,1,0:T(4,128)(2,1)S(1)} %get-tuple-element.149.right, f32[49,384]{1,0:T(8,128)S(1)} %reshape.117.taps, ...), custom_call_target="tpu_custom_call" | custom-call | flops 9633792 | bytes 877056 | tf_op jit(solution)/shard_map/pallas_call | solution.py:96
  104.3 2.8 %collective-permute-done.28.g3 = bf16[96,384]{1,0:T(8,128)(2,1)S(1)} collective-permute-done((bf16[96,384]{1,0:T(8,128)(2,1)S(1)}, bf16[96,384]{1,0:T(8,128)(2,1)S(1)}, u32[]{:S(2)}, u32[]{:S(2)}) %collective-permute-start.28) | collective-permute-done | bytes 73760 | tf_op jit(solution)/shard_map/ppermute | solution.py:21
  107.1 1.2 %shard_map.151 = (f32[6,384]{1,0:T(8,128)}, f32[6,384]{1,0:T(8,128)}, f32[53,384]{1,0:T(8,128)}, f32[1536]{0:T(1024)}) custom-call(s32[5]{0:T(128)S(1)} %stack.48.index, f32[2,24,384]{2,1,0:T(8,128)S(1)} %get-tuple-element.75.before, bf16[64,384]{1,0:T(8,128)(2,1)S(1)} %get-tuple-element.76.mine, bf16[96,384]{1,0:T(8,128)(2,1)S(1)} %collective-permute-done.26.g2, ...), custom_call_target="tpu_custom_call" | custom-call | flops 1000000 | bytes 450048 | tf_op jit(solution)/shard_map/pallas_call | solution.py:96
  (104 shorter events, 2.4 us)
Async XLA Ops:
  0.6 24.2 %copy-start.1 = (bf16[8,32,384]{2,1,0:T(8,128)(2,1)S(1)}, bf16[8,32,384]{2,1,0:T(8,128)(2,1)}, u32[]{:S(2)}) copy-start(bf16[8,32,384]{2,1,0:T(8,128)(2,1)} %feature) | copy-start | bytes 589828
  1.4 15.1 %collective-permute-start = (bf16[2,6,384]{2,1,0:T(8,128)(2,1)S(1)}, bf16[2,6,384]{2,1,0:T(8,128)(2,1)S(1)}, u32[]{:S(2)}, u32[]{:S(2)}) collective-permute-start(bf16[2,6,384]{2,1,0:T(8,128)(2,1)S(1)} %pad_maximum_fusion.13), channel_id=1, source_target_pairs={{0,192},{32,224},{64,128},{96,160},{128,64},{160,96},{192,0},{224,... | collective-permute-start | bytes 27656 | tf_op jit(solution)/shard_map/ppermute | solution.py:21
  7.8 8.7 %collective-permute-start.1 = (bf16[2,6,384]{2,1,0:T(8,128)(2,1)S(1)}, bf16[2,6,384]{2,1,0:T(8,128)(2,1)S(1)}, u32[]{:S(2)}, u32[]{:S(2)}) collective-permute-start(bf16[2,6,384]{2,1,0:T(8,128)(2,1)S(1)} %pad_maximum_fusion.13), channel_id=1, source_target_pairs={{0,128},{32,160},{64,192},{96,224},{128,0},{160,32},{192,64},{224,... | collective-permute-start | bytes 27656 | tf_op jit(solution)/shard_map/ppermute | solution.py:21
  8.8 7.7 %collective-permute-start.2 = (bf16[2,6,384]{2,1,0:T(8,128)(2,1)S(1)}, bf16[2,6,384]{2,1,0:T(8,128)(2,1)S(1)}, u32[]{:S(2)}, u32[]{:S(2)}) collective-permute-start(bf16[2,6,384]{2,1,0:T(8,128)(2,1)S(1)} %pad_maximum_fusion.13), channel_id=1, source_target_pairs={{0,64},{32,96},{64,0},{96,32},{128,192},{160,224},{192,128},{224,1... | collective-permute-start | bytes 27656 | tf_op jit(solution)/shard_map/ppermute | solution.py:21
  11.2 10.2 %collective-permute-start.5 = (bf16[3,32,384]{2,1,0:T(8,128)(2,1)S(1)}, bf16[3,32,384]{2,1,0:T(8,128)(2,1)S(1)}, u32[]{:S(2)}, u32[]{:S(2)}) collective-permute-start(bf16[3,32,384]{2,1,0:T(8,128)(2,1)S(1)} %get-tuple-element.143), channel_id=1, source_target_pairs={{8,16},{16,8},{24,32},{32,24},{40,48},{48,40},{56,64},{64,56},{72,... | collective-permute-start | bytes 221192 | tf_op jit(solution)/shard_map/ppermute | solution.py:34
  11.8 9.5 %collective-permute-start.4 = (bf16[3,32,384]{2,1,0:T(8,128)(2,1)S(1)}, bf16[3,32,384]{2,1,0:T(8,128)(2,1)S(1)}, u32[]{:S(2)}, u32[]{:S(2)}) collective-permute-start(bf16[3,32,384]{2,1,0:T(8,128)(2,1)S(1)} %get-tuple-element.144), channel_id=1, source_target_pairs={{0,8},{8,0},{16,24},{24,16},{32,40},{40,32},{48,56},{56,48},{64,72... | collective-permute-start | bytes 221192 | tf_op jit(solution)/shard_map/ppermute | solution.py:21
  17.3 4.0 %collective-permute-start.3 = (bf16[2,24,384]{2,1,0:T(8,128)(2,1)S(1)}, bf16[2,24,384]{2,1,0:T(8,128)(2,1)S(1)}, u32[]{:S(2)}, u32[]{:S(2)}) collective-permute-start(bf16[2,24,384]{2,1,0:T(8,128)(2,1)S(1)} %pad_maximum_fusion.12), channel_id=1, source_target_pairs={{0,32},{32,0},{64,96},{96,64},{128,160},{160,128},{192,224},{224,1... | collective-permute-start | bytes 110600 | tf_op jit(solution)/shard_map/ppermute | solution.py:21
  19.4 15.2 %copy-start.10 = (f32[7,7,384]{2,1,0:T(8,128)S(1)}, f32[7,7,384]{2,1,0:T(8,128)}, u32[]{:S(2)}) copy-start(f32[7,7,384]{2,1,0:T(8,128)} %param.11) | copy-start | bytes 225796
  19.4 15.5 %copy-start = (bf16[8,32,384]{2,1,0:T(8,128)(2,1)S(1)}, bf16[8,32,384]{2,1,0:T(8,128)(2,1)}, u32[]{:S(2)}) copy-start(bf16[8,32,384]{2,1,0:T(8,128)(2,1)} %cot.1) | copy-start | bytes 589828
  21.4 8.0 %collective-permute-start.6 = (bf16[2,48,384]{2,1,0:T(8,128)(2,1)S(1)}, bf16[2,48,384]{2,1,0:T(8,128)(2,1)S(1)}, u32[]{:S(2)}, u32[]{:S(2)}) collective-permute-start(bf16[2,48,384]{2,1,0:T(8,128)(2,1)S(1)} %pad_maximum_fusion.11), channel_id=1, source_target_pairs={{0,16},{1,17},{16,0},{17,1},{2,18},{3,19},{18,2},{19,3},{4,20},{5,... | collective-permute-start | bytes 221192 | tf_op jit(solution)/shard_map/ppermute | solution.py:21
  23.6 6.8 %collective-permute-start.8 = (bf16[2,48,384]{2,1,0:T(8,128)(2,1)S(1)}, bf16[2,48,384]{2,1,0:T(8,128)(2,1)S(1)}, u32[]{:S(2)}, u32[]{:S(2)}) collective-permute-start(bf16[2,48,384]{2,1,0:T(8,128)(2,1)S(1)} %pad_maximum_fusion.11), channel_id=1, source_target_pairs={{0,17},{1,16},{16,1},{17,0},{2,19},{3,18},{18,3},{19,2},{4,21},{5,... | collective-permute-start | bytes 221192 | tf_op jit(solution)/shard_map/ppermute | solution.py:21
  25.1 5.3 %collective-permute-start.7 = (bf16[138,384]{1,0:T(8,128)(2,1)S(1)}, bf16[138,384]{1,0:T(8,128)(2,1)S(1)}, u32[]{:S(2)}, u32[]{:S(2)}) collective-permute-start(bf16[138,384]{1,0:T(8,128)(2,1)S(1)} %pad_maximum_fusion.10), channel_id=1, source_target_pairs={{0,1},{1,0},{16,17},{17,16},{2,3},{3,2},{18,19},{19,18},{4,5},{5,4... | collective-permute-start | bytes 317960 | tf_op jit(solution)/shard_map/ppermute | solution.py:21
  25.3 9.7 %collective-permute-start.9 = (bf16[14,3,384]{2,1,0:T(4,128)(2,1)S(1)}, bf16[14,3,384]{2,1,0:T(4,128)(2,1)S(1)}, u32[]{:S(2)}, u32[]{:S(2)}) collective-permute-start(bf16[14,3,384]{2,1,0:T(4,128)(2,1)S(1)} %get-tuple-element.141), channel_id=1, source_target_pairs={{1,2},{2,1},{3,4},{4,3},{5,6},{6,5},{9,10},{10,9},{11,12},{12,11},... | collective-permute-start | bytes 96776 | tf_op jit(solution)/shard_map/ppermute | solution.py:34
  30.4 9.8 %collective-permute-start.11 = (bf16[2,192,384]{2,1,0:T(8,128)(2,1)S(1)}, bf16[2,192,384]{2,1,0:T(8,128)(2,1)}, u32[]{:S(2)}, u32[]{:S(2)}) collective-permute-start(bf16[2,192,384]{2,1,0:T(8,128)(2,1)S(1)} %constant_dynamic-update-slice_fusion.7), channel_id=1, source_target_pairs={{0,2},{2,0},{4,6},{6,4},{1,3},{3,1},{5,7},{7,5},{8,10},{10,8},{12,... | collective-permute-start | bytes 884744 | tf_op jit(solution)/shard_map/ppermute | solution.py:21
  31.4 13.8 %collective-permute-start.12 = (bf16[2,192,384]{2,1,0:T(8,128)(2,1)S(1)}, bf16[2,192,384]{2,1,0:T(8,128)(2,1)}, u32[]{:S(2)}, u32[]{:S(2)}) collective-permute-start(bf16[2,192,384]{2,1,0:T(8,128)(2,1)S(1)} %constant_dynamic-update-slice_fusion.7), channel_id=1, source_target_pairs={{0,6},{2,4},{4,2},{6,0},{1,7},{3,5},{5,3},{7,1},{8,14},{10,12},{12... | collective-permute-start | bytes 884744 | tf_op jit(solution)/shard_map/ppermute | solution.py:21
  32.5 13.7 %collective-permute-start.13 = (bf16[2,192,384]{2,1,0:T(8,128)(2,1)S(1)}, bf16[2,192,384]{2,1,0:T(8,128)(2,1)S(1)}, u32[]{:S(2)}, u32[]{:S(2)}) collective-permute-start(bf16[2,192,384]{2,1,0:T(8,128)(2,1)S(1)} %constant_dynamic-update-slice_fusion.7), channel_id=1, source_target_pairs={{0,4},{2,6},{4,0},{6,2},{1,5},{3,7},{5,1},{7,3},{8,12},{10,14},{12... | collective-permute-start | bytes 884744 | tf_op jit(solution)/shard_map/ppermute | solution.py:21
  35.2 3.4 %copy-start.12 = (f32[384]{0:T(512)S(1)}, f32[384]{0:T(512)}, u32[]{:S(2)}) copy-start(f32[384]{0:T(512)} %param.18) | copy-start | bytes 4612
  35.2 3.4 %copy-start.13 = (f32[384]{0:T(512)S(1)}, f32[384]{0:T(512)}, u32[]{:S(2)}) copy-start(f32[384]{0:T(512)} %param.12) | copy-start | bytes 4612
  35.2 3.4 %copy-start.14 = (f32[384]{0:T(512)S(1)}, f32[384]{0:T(512)}, u32[]{:S(2)}) copy-start(f32[384]{0:T(512)} %param.13) | copy-start | bytes 4612
  38.8 0.7 copy-start.15
  38.9 8.1 %copy-start.5 = (bf16[256,384]{1,0:T(8,128)(2,1)}, bf16[256,384]{1,0:T(8,128)(2,1)S(1)}, u32[]{:S(2)}) copy-start(bf16[256,384]{1,0:T(8,128)(2,1)S(1)} %fusion.57) | copy-start | bytes 589828
  38.9 7.3 %collective-permute-start.10 = (bf16[2,256,384]{2,1,0:T(8,128)(2,1)S(1)}, bf16[2,256,384]{2,1,0:T(8,128)(2,1)S(1)}, u32[]{:S(2)}, u32[]{:S(2)}) collective-permute-start(bf16[2,256,384]{2,1,0:T(8,128)(2,1)S(1)} %pad_maximum_fusion.1), channel_id=1, source_target_pairs={{0,8},{8,0},{1,9},{9,1},{2,10},{10,2},{3,11},{11,3},{4,12},{12,4},... | collective-permute-start | bytes 1179656 | tf_op jit(solution)/shard_map/ppermute | solution.py:21
  46.3 0.7 copy-start.7
  46.3 1.6 %copy-start.9 = (bf16[256,384]{1,0:T(8,128)(2,1)}, bf16[256,384]{1,0:T(8,128)(2,1)S(1)}, u32[]{:S(2)}) copy-start(bf16[256,384]{1,0:T(8,128)(2,1)S(1)} %get-tuple-element.138) | copy-start | bytes 589828
  47.0 1.5 %copy-start.2 = (bf16[512,768]{1,0:T(8,128)(2,1)}, bf16[512,768]{1,0:T(8,128)(2,1)S(1)}, u32[]{:S(2)}) copy-start(bf16[512,768]{1,0:T(8,128)(2,1)S(1)} %get-tuple-element.159) | copy-start | bytes 2359300
  47.9 1.2 %copy-start.4 = (bf16[512,768]{1,0:T(8,128)(2,1)}, bf16[512,768]{1,0:T(8,128)(2,1)S(1)}, u32[]{:S(2)}) copy-start(bf16[512,768]{1,0:T(8,128)(2,1)S(1)} %get-tuple-element.162) | copy-start | bytes 2359300
  49.9 2.2 %collective-permute-start.14 = (bf16[2,256,384]{2,1,0:T(8,128)(2,1)}, bf16[2,256,384]{2,1,0:T(8,128)(2,1)S(1)}, u32[]{:S(2)}, u32[]{:S(2)}) collective-permute-start(bf16[2,256,384]{2,1,0:T(8,128)(2,1)} %pad_maximum_fusion.4), channel_id=1, source_target_pairs={{0,8},{8,0},{1,9},{9,1},{2,10},{10,2},{3,11},{11,3},{4,12},{12,4},... | collective-permute-start | bytes 1179656 | tf_op jit(solution)/shard_map/ppermute | solution.py:21
  52.2 4.4 %copy-start.3 = (bf16[512,768]{1,0:T(8,128)(2,1)S(1)}, bf16[512,768]{1,0:T(8,128)(2,1)}, u32[]{:S(2)}) copy-start(bf16[512,768]{1,0:T(8,128)(2,1)} %copy-done.2) | copy-start | bytes 2359300
  52.2 4.4 %copy-start.6 = (bf16[256,384]{1,0:T(8,128)(2,1)S(1)}, bf16[256,384]{1,0:T(8,128)(2,1)}, u32[]{:S(2)}) copy-start(bf16[256,384]{1,0:T(8,128)(2,1)} %copy-done.5) | copy-start | bytes 589828
  52.2 4.4 %copy-start.8 = (bf16[256,384]{1,0:T(8,128)(2,1)S(1)}, bf16[256,384]{1,0:T(8,128)(2,1)}, u32[]{:S(2)}) copy-start(bf16[256,384]{1,0:T(8,128)(2,1)} %copy-done.7) | copy-start | bytes 589828
  55.9 1.6 %collective-permute-start.15 = (bf16[224,384]{1,0:T(8,128)(2,1)S(1)}, bf16[224,384]{1,0:T(8,128)(2,1)S(1)}, u32[]{:S(2)}, u32[]{:S(2)}) collective-permute-start(bf16[224,384]{1,0:T(8,128)(2,1)S(1)} %get-tuple-element.58.mine), channel_id=1, source_target_pairs={{0,8},{8,0},{1,9},{9,1},{2,10},{10,2},{3,11},{11,3},{4,12},{12,4},... | collective-permute-start | bytes 516104 | tf_op jit(solution)/shard_map/ppermute | solution.py:21
  58.2 11.0 %collective-permute-start.19 = (bf16[448,384]{1,0:T(8,128)(2,1)S(1)}, bf16[448,384]{1,0:T(8,128)(2,1)S(1)}, u32[]{:S(2)}, u32[]{:S(2)}) collective-permute-start(bf16[448,384]{1,0:T(8,128)(2,1)S(1)} %get-tuple-element.64), channel_id=1, source_target_pairs={{0,2},{2,0},{4,6},{6,4},{1,3},{3,1},{5,7},{7,5},{8,10},{10,8},{12,... | collective-permute-start | bytes 1032200 | tf_op jit(solution)/shard_map/ppermute | solution.py:21
  58.3 19.0 %collective-permute-start.20 = (bf16[448,384]{1,0:T(8,128)(2,1)S(1)}, bf16[448,384]{1,0:T(8,128)(2,1)S(1)}, u32[]{:S(2)}, u32[]{:S(2)}) collective-permute-start(bf16[448,384]{1,0:T(8,128)(2,1)S(1)} %get-tuple-element.65), channel_id=1, source_target_pairs={{0,6},{2,4},{4,2},{6,0},{1,7},{3,5},{5,3},{7,1},{8,14},{10,12},{12... | collective-permute-start | bytes 1032200 | tf_op jit(solution)/shard_map/ppermute | solution.py:21
  59.6 17.8 %collective-permute-start.21 = (bf16[448,384]{1,0:T(8,128)(2,1)S(1)}, bf16[448,384]{1,0:T(8,128)(2,1)S(1)}, u32[]{:S(2)}, u32[]{:S(2)}) collective-permute-start(bf16[448,384]{1,0:T(8,128)(2,1)S(1)} %get-tuple-element.66), channel_id=1, source_target_pairs={{0,4},{2,6},{4,0},{6,2},{1,5},{3,7},{5,1},{7,3},{8,12},{10,14},{12... | collective-permute-start | bytes 1032200 | tf_op jit(solution)/shard_map/ppermute | solution.py:21
  62.4 19.9 %collective-permute-start.16 = (bf16[3,32,384]{2,1,0:T(8,128)(2,1)S(1)}, bf16[3,32,384]{2,1,0:T(8,128)(2,1)S(1)}, u32[]{:S(2)}, u32[]{:S(2)}) collective-permute-start(bf16[3,32,384]{2,1,0:T(8,128)(2,1)S(1)} %get-tuple-element.61), channel_id=1, source_target_pairs={{8,16},{16,8},{24,32},{32,24},{40,48},{48,40},{56,64},{64,56},{72,... | collective-permute-start | bytes 221192 | tf_op jit(solution)/shard_map/ppermute | solution.py:34
  78.1 13.1 %copy-start.11 = (f32[7,7,384]{2,1,0:T(8,128)S(1)}, f32[7,7,384]{2,1,0:T(8,128)}, u32[]{:S(2)}) copy-start(f32[7,7,384]{2,1,0:T(8,128)} %param.11) | copy-start | bytes 225796
  78.2 5.9 %collective-permute-start.22 = (bf16[160,384]{1,0:T(8,128)(2,1)S(1)}, bf16[160,384]{1,0:T(8,128)(2,1)S(1)}, u32[]{:S(2)}, u32[]{:S(2)}) collective-permute-start(bf16[160,384]{1,0:T(8,128)(2,1)S(1)} %get-tuple-element.69), channel_id=1, source_target_pairs={{0,1},{1,0},{16,17},{17,16},{2,3},{3,2},{18,19},{19,18},{4,5},{5,4... | collective-permute-start | bytes 368648 | tf_op jit(solution)/shard_map/ppermute | solution.py:21
  78.6 8.7 %collective-permute-start.23 = (bf16[160,384]{1,0:T(8,128)(2,1)S(1)}, bf16[160,384]{1,0:T(8,128)(2,1)S(1)}, u32[]{:S(2)}, u32[]{:S(2)}) collective-permute-start(bf16[160,384]{1,0:T(8,128)(2,1)S(1)} %get-tuple-element.70), channel_id=1, source_target_pairs={{0,17},{1,16},{16,1},{17,0},{2,19},{3,18},{18,3},{19,2},{4,21},{5,... | collective-permute-start | bytes 368648 | tf_op jit(solution)/shard_map/ppermute | solution.py:21
  80.5 6.8 %collective-permute-start.24 = (bf16[160,384]{1,0:T(8,128)(2,1)S(1)}, bf16[160,384]{1,0:T(8,128)(2,1)S(1)}, u32[]{:S(2)}, u32[]{:S(2)}) collective-permute-start(bf16[160,384]{1,0:T(8,128)(2,1)S(1)} %get-tuple-element.71), channel_id=1, source_target_pairs={{0,16},{1,17},{16,0},{17,1},{2,18},{3,19},{18,2},{19,3},{4,20},{5,... | collective-permute-start | bytes 368648 | tf_op jit(solution)/shard_map/ppermute | solution.py:21
  88.0 5.2 %collective-permute-start.25 = (bf16[192,384]{1,0:T(8,128)(2,1)S(1)}, bf16[192,384]{1,0:T(8,128)(2,1)S(1)}, u32[]{:S(2)}, u32[]{:S(2)}) collective-permute-start(bf16[192,384]{1,0:T(8,128)(2,1)S(1)} %get-tuple-element.74), channel_id=1, source_target_pairs={{0,32},{32,0},{64,96},{96,64},{128,160},{160,128},{192,224},{224,1... | collective-permute-start | bytes 442376 | tf_op jit(solution)/shard_map/ppermute | solution.py:21
  89.2 11.2 %collective-permute-start.18 = (bf16[14,3,384]{2,1,0:T(4,128)(2,1)S(1)}, bf16[14,3,384]{2,1,0:T(4,128)(2,1)S(1)}, u32[]{:S(2)}, u32[]{:S(2)}) collective-permute-start(bf16[14,3,384]{2,1,0:T(4,128)(2,1)S(1)} %get-tuple-element.139), channel_id=1, source_target_pairs={{1,2},{2,1},{3,4},{4,3},{5,6},{6,5},{9,10},{10,9},{11,12},{12,11},... | collective-permute-start | bytes 96776 | tf_op jit(solution)/shard_map/ppermute | solution.py:34
  91.2 9.2 %collective-permute-start.17 = (bf16[14,3,384]{2,1,0:T(4,128)(2,1)S(1)}, bf16[14,3,384]{2,1,0:T(4,128)(2,1)S(1)}, u32[]{:S(2)}, u32[]{:S(2)}) collective-permute-start(bf16[14,3,384]{2,1,0:T(4,128)(2,1)S(1)} %get-tuple-element.140), channel_id=1, source_target_pairs={{0,1},{1,0},{2,3},{3,2},{4,5},{5,4},{6,7},{7,6},{8,9},{9,8},{10,11... | collective-permute-start | bytes 96776 | tf_op jit(solution)/shard_map/ppermute | solution.py:21
  93.8 10.5 %collective-permute-start.26 = (bf16[96,384]{1,0:T(8,128)(2,1)S(1)}, bf16[96,384]{1,0:T(8,128)(2,1)S(1)}, u32[]{:S(2)}, u32[]{:S(2)}) collective-permute-start(bf16[96,384]{1,0:T(8,128)(2,1)S(1)} %get-tuple-element.77), channel_id=1, source_target_pairs={{0,128},{32,160},{64,192},{96,224},{128,0},{160,32},{192,64},{224,... | collective-permute-start | bytes 221192 | tf_op jit(solution)/shard_map/ppermute | solution.py:21
  98.8 5.5 %collective-permute-start.27 = (bf16[96,384]{1,0:T(8,128)(2,1)S(1)}, bf16[96,384]{1,0:T(8,128)(2,1)S(1)}, u32[]{:S(2)}, u32[]{:S(2)}) collective-permute-start(bf16[96,384]{1,0:T(8,128)(2,1)S(1)} %get-tuple-element.78), channel_id=1, source_target_pairs={{0,64},{32,96},{64,0},{96,32},{128,192},{160,224},{192,128},{224,1... | collective-permute-start | bytes 221192 | tf_op jit(solution)/shard_map/ppermute | solution.py:21
  100.2 6.9 %collective-permute-start.28 = (bf16[96,384]{1,0:T(8,128)(2,1)S(1)}, bf16[96,384]{1,0:T(8,128)(2,1)S(1)}, u32[]{:S(2)}, u32[]{:S(2)}) collective-permute-start(bf16[96,384]{1,0:T(8,128)(2,1)S(1)} %get-tuple-element.79), channel_id=1, source_target_pairs={{0,192},{32,224},{64,128},{96,160},{128,64},{160,96},{192,0},{224,... | collective-permute-start | bytes 221192 | tf_op jit(solution)/shard_map/ppermute | solution.py:21
